TPU v7x, 32 devices: a whole 2x2x4 slice. The times are simulated.
32 devices in a mesh: grp: 8 (over z, y), tm: 4 (over x, core).
Axes of the slice: x: 2, y: 2, z: 4, core: 2. Of those that a mesh axis runs over, the one named last changes fastest.
Arguments:
- voltages: bfloat16 [2, 192, 1048576], P(None, 'grp', 'tm'), may hold values from -6 to 6
- filter_taps: float32 [4, 4096], replicated, may hold values from -3 to 3
- delays: int32 [192, 1536], replicated, may hold values from 0 to 4095
- shifts: int32 [4, 512], replicated, may hold values from 0 to 2
Outputs:
- dedispersed: float32 [1536, 512, 32], P('grp', None, 'tm')
All inputs are finite; a program needn't handle non-finite values.
Results may differ from a plain program's by a relative error of at most 0.0014.
Values may be sent and summed in bfloat16 or wider, within the bound.
No kernel may reach another device: no remote copies, remote signals or barrier semaphores. Data moves between devices by JAX's collectives and lax.ppermute only.
A program may use at most 192 MiB of HBM per device.

v0:
```python
import math

import jax
import jax.numpy as jnp
from jax import lax
from jax.sharding import PartitionSpec as P

STATIONS = 192
TRANSFORM = 4096
CHANNELS = 512
TAPS = 4
INTEG = 8
LEVELS = 4
SHIFT_MOST = 2


two_pi = 2.0 * math.pi


def from_behind(x, axis, by):
    length = lax.axis_size(axis)
    pairs = [(i, i + by) for i in range(length) if 0 <= i + by < length]
    return lax.ppermute(x, axis, pairs)


def for_sending(x):
    return jax.tree.map(lambda a: a.astype(jnp.bfloat16) if a.dtype == jnp.float32 else a, x)


def dft_tables():
    rows_index = jnp.arange(CHANNELS, dtype=jnp.int32)
    cols_index = jnp.arange(TRANSFORM, dtype=jnp.int32)
    product = rows_index[:, None] * cols_index[None, :] % TRANSFORM
    angles = product.astype(jnp.float32) * (two_pi / TRANSFORM)
    scaling = 1.0 / math.sqrt(TRANSFORM)
    return (
        (jnp.cos(angles) * scaling).astype(jnp.bfloat16),
        (jnp.sin(angles) * scaling).astype(jnp.bfloat16),
    )


def beam_weights(channel, delays):
    phases = (channel * delays.T % TRANSFORM).astype(jnp.float32) * (two_pi / TRANSFORM)
    scaling = 1.0 / math.sqrt(STATIONS)
    return (
        (jnp.cos(phases) * scaling).astype(jnp.bfloat16),
        (jnp.sin(phases) * scaling).astype(jnp.bfloat16),
    )


def to_spectra(filtered, cosine, sine):
    real_part = jnp.einsum(
        "kn,stn->kst", cosine, filtered[0], preferred_element_type=jnp.float32
    ) + jnp.einsum("kn,stn->kst", sine, filtered[1], preferred_element_type=jnp.float32)
    imag_part = jnp.einsum(
        "kn,stn->kst", cosine, filtered[1], preferred_element_type=jnp.float32
    ) - jnp.einsum("kn,stn->kst", sine, filtered[0], preferred_element_type=jnp.float32)
    spectra = jnp.stack([real_part, imag_part]).astype(jnp.bfloat16)
    return spectra.reshape(2, CHANNELS, spectra.shape[2], -1, INTEG)


def dedisperse_level(leading, trailing, amounts, out_len):
    shifted = jnp.zeros(leading.shape[:3] + (2, out_len), jnp.float32)
    for offset in range(SHIFT_MOST + 1):
        selector = (amounts == offset).astype(jnp.float32)[None, :, :, :, None]
        shifted = shifted + selector * trailing[:, :, :, None, offset : offset + out_len]
    combined = 0.5 * (leading[:, :, :, None, :] + shifted)
    return combined.reshape(leading.shape[0], -1, out_len)


def local(voltages, filter_taps, delays, shifts):
    station_count = voltages.shape[1]
    frames = voltages.shape[2] // TRANSFORM
    framed = voltages.reshape(2, station_count, frames, TRANSFORM)
    last_frames = framed[:, :, frames - (TAPS - 1) :, :]
    previous = from_behind(last_frames, "tm", 1)
    extended = jnp.concatenate([previous, framed], axis=2).astype(jnp.float32)
    filtered = jnp.zeros((2, station_count, frames, TRANSFORM), jnp.float32)
    for tap in range(TAPS):
        start = TAPS - 1 - tap
        filtered = (
            filtered
            + filter_taps[tap][None, None, None, :] * extended[:, :, start : start + frames, :]
        )
    filtered = filtered.astype(jnp.bfloat16)
    cosine, sine = dft_tables()
    local_channels = CHANNELS // lax.axis_size("grp")
    spectra_all = to_spectra(filtered, cosine, sine)
    received = lax.all_to_all(spectra_all, "grp", split_axis=1, concat_axis=2, tiled=True)
    item_count = received.shape[3]
    all_stations = received.shape[2]
    spectra = received.reshape(2, local_channels, all_stations, item_count * INTEG)
    first_channel = lax.axis_index("grp") * local_channels

    def channel_powers(local_index):
        channel_data = lax.dynamic_index_in_dim(spectra, local_index, 1, keepdims=False)
        weight_cos, weight_sin = beam_weights(first_channel + local_index, delays)
        beam_real = jnp.dot(
            weight_cos, channel_data[0], preferred_element_type=jnp.float32
        ) + jnp.dot(weight_sin, channel_data[1], preferred_element_type=jnp.float32)
        beam_imag = jnp.dot(
            weight_cos, channel_data[1], preferred_element_type=jnp.float32
        ) - jnp.dot(weight_sin, channel_data[0], preferred_element_type=jnp.float32)
        energy = beam_real * beam_real + beam_imag * beam_imag
        power = energy.reshape(energy.shape[0], item_count, INTEG).sum(axis=-1) * (1.0 / INTEG)
        return power.astype(jnp.bfloat16)

    powers = lax.map(channel_powers, jnp.arange(local_channels, dtype=jnp.int32))
    powers = jnp.transpose(powers, (1, 0, 2))
    owned = lax.all_to_all(powers, "grp", split_axis=0, concat_axis=1, tiled=True)
    current = owned.astype(jnp.float32)
    beam_count = current.shape[0]
    power_len = current.shape[2]
    for level_index in range(1, LEVELS + 1):
        half_width = 2 ** (level_index - 1)
        group_count = CHANNELS // (2 * half_width)
        grouped = current.reshape(beam_count, group_count, 2, half_width, power_len)
        leading = grouped[:, :, 0]
        trailing_own = grouped[:, :, 1]
        next_rim = from_behind(for_sending(trailing_own[:, :, :, :SHIFT_MOST]), "tm", -1)
        trailing = jnp.concatenate([trailing_own, next_rim], axis=3)
        amounts = shifts[level_index - 1].reshape(group_count, half_width, 2)
        current = dedisperse_level(leading, trailing, amounts, power_len)
    return current


def solution(mesh):
    placed = (P(None, "grp", "tm"), P(), P(), P())
    return jax.shard_map(
        local, mesh=mesh, in_specs=placed, out_specs=P("grp", None, "tm"), check_vma=False
    )
```

profile of v0, /device:TPU:1, one launch (start us, length us, event | category | flops | bytes accessed | tf_op | source)
XLA Modules:
  0.0 1462.3 jit_solution(16832688132228220939)
XLA Ops:
  0.0 21.3 %copy.154 = bf16[6,8,64,4096]{3,2,1,0:T(8,128)(2,1)S(1)} copy(bf16[6,8,64,4096]{3,1,2,0:T(8,128)(2,1)} %bitcast.195) | data formatting | bytes 50331648
  27.7 13.1 collective-permute-done
  41.8 19.1 %maximum_convert_fusion = f32[2,24,67,4096]{3,2,1,0:T(8,128)} fusion(bf16[2,24,64,4096]{3,2,1,0:T(8,128)(2,1)S(1)} %bitcast.192, bf16[2,24,3,4096]{3,2,1,0:T(4,128)(2,1)S(1)} %copy.126), kind=kLoop, calls=%fused_computation.34 | loop fusion | flops 52690944 | bytes 79036416 | tf_op jit(solution)/shard_map/convert_element_type | solution.py:77
  60.9 76.4 %fusion.17 = bf16[2,24,64,4096]{3,2,1,0:T(8,128)(2,1)} fusion(f32[2,24,67,4096]{3,2,1,0:T(8,128)} %maximum_convert_fusion, f32[4096]{0:T(1024)S(1)} %bitcast.215, f32[4096]{0:T(1024)S(1)} %bitcast.216, f32[4096]{0:T(1024)S(1)} %bitcast.214, f32[4096]{0:T(1024)S(1)} %bitcast.213), kind=kLoop, calls=%fused_computation.28 | loop fusion | flops 100663296 | bytes 226557952 | tf_op jit(solution)/shard_map/convert_element_type | solution.py:85
  137.3 43.1 %fusion.23 = f32[512,24,64]{0,2,1:T(8,128)} fusion(bf16[2,24,64,4096]{3,2,1,0:T(8,128)(2,1)} %fusion.17), kind=kOutput, calls=%fused_computation.43 | convolution fusion | flops 6476005376 | bytes 15728640 | tf_op jit(solution)/shard_map/kn,stn->kst/dot_general | solution.py:54
  180.4 42.4 %fusion.20 = f32[512,24,64]{0,2,1:T(8,128)S(1)} fusion(bf16[2,24,64,4096]{3,2,1,0:T(8,128)(2,1)} %fusion.17), kind=kOutput, calls=%fused_computation.40 | convolution fusion | flops 6476005376 | bytes 15728640 | tf_op jit(solution)/shard_map/kn,stn->kst/dot_general | solution.py:57
  222.8 43.9 %fusion.48 = bf16[1,512,24,8,8]{1,4,3,2,0:T(8,128)(2,1)S(1)} fusion(f32[512,24,64]{0,2,1:T(8,128)} %fusion.23, bf16[2,24,64,4096]{3,2,1,0:T(8,128)(2,1)} %fusion.17), kind=kOutput, calls=%fused_computation.89 | convolution fusion | flops 6477578240 | bytes 17301504 | tf_op jit(solution)/shard_map/kn,stn->kst/dot_general | solution.py:52
  266.7 42.0 %fusion.51 = bf16[1,512,24,8,8]{1,4,3,2,0:T(8,128)(2,1)S(1)} fusion(f32[512,24,64]{0,2,1:T(8,128)S(1)} %fusion.20, bf16[2,24,64,4096]{3,2,1,0:T(8,128)(2,1)} %fusion.17), kind=kOutput, calls=%fused_computation.90 | convolution fusion | flops 6477578240 | bytes 17301504 | tf_op jit(solution)/shard_map/kn,stn->kst/dot_general | solution.py:55
  309.0 26.3 %copy.127 = bf16[2,512,24,8,8]{2,4,3,0,1:T(8,128)(2,1)} copy(bf16[2,512,24,8,8]{1,4,3,2,0:T(8,128)(2,1)S(1)} %pad_maximum_fusion) | data formatting | bytes 6291456 | tf_op jit(solution)/shard_map/stack | solution.py:58
  335.3 24.2 %reshape.336 = bf16[8,2,98304]{2,1,0:T(2,128)(2,1)} reshape(bf16[512,2,8,8,24]{4,3,2,1,0:T(8,128)(2,1)} %bitcast.193) | data formatting | bytes 6291456
  359.5 6.1 all-to-all-start
  365.6 60.2 %all-to-all-done = bf16[8,2,98304]{2,1,0:T(2,128)(2,1)S(1)} async-done(((bf16[8,2,98304]{2,1,0:T(2,128)(2,1)}), bf16[8,2,98304]{2,1,0:T(2,128)(2,1)S(1)}, u32[]{:S(2)}, u32[]{:S(2)}) %all-to-all-start) | async-done | bytes 3145760 | tf_op jit(solution)/shard_map/all_to_all | solution.py:89
  425.8 25.3 %reshape.337 = bf16[512,2,8,8,24]{4,3,2,1,0:T(8,128)(2,1)} reshape(bf16[8,2,98304]{2,1,0:T(2,128)(2,1)S(1)} %all-to-all-done) | data formatting | bytes 6291456
  451.2 25.2 %copy.129 = bf16[2,64,8,24,8,8]{1,5,4,3,2,0:T(8,128)(2,1)} copy(bf16[2,64,8,24,8,8]{3,5,4,0,1,2:T(8,128)(2,1)} %bitcast.194) | data formatting | bytes 6291456 | tf_op jit(solution)/shard_map/all_to_all | solution.py:89
  476.4 9.6 copy.130
  486.0 832.3 %while.12 = (s32[]{:T(128)}, bf16[64,1536,8]{1,2,0:T(8,128)(2,1)}, s32[64]{0:T(128)S(1)}, s32[]{:T(128)}, s32[192,1536]{1,0:T(8,128)S(1)}, /*index=5*/bf16[2,64,...) while((s32[]{:T(128)}, bf16[64,1536,8]{1,2,0:T(8,128)(2,1)}, s32[64]{0:T(128)S(1)}, s32[]{:T(128)}, ...), condition=%wide.region_2.3_spmd, body=%wide.region_0.2_spmd.sunk | while | flops 156905472 | bytes 7398087 | solution.py:108
  489.2 4.8 multiply_convert_fusion.6
  502.2 4.8 multiply_convert_fusion.6
  515.2 4.8 multiply_convert_fusion.6
  528.2 4.8 multiply_convert_fusion.6
  541.2 4.8 multiply_convert_fusion.6
  554.2 4.8 multiply_convert_fusion.6
  567.2 4.8 multiply_convert_fusion.6
  580.2 4.8 multiply_convert_fusion.6
  593.2 4.8 multiply_convert_fusion.6
  606.2 4.8 multiply_convert_fusion.6
  619.2 4.8 multiply_convert_fusion.6
  632.3 4.8 multiply_convert_fusion.6
  645.3 4.8 multiply_convert_fusion.6
  658.3 4.8 multiply_convert_fusion.6
  671.3 4.8 multiply_convert_fusion.6
  684.3 4.8 multiply_convert_fusion.6
  853.3 4.8 multiply_convert_fusion.6
  879.4 4.8 multiply_convert_fusion.6
  905.4 4.8 multiply_convert_fusion.6
  944.4 4.8 multiply_convert_fusion.6
  970.4 4.8 multiply_convert_fusion.6
  983.4 4.8 multiply_convert_fusion.6
  996.4 4.8 multiply_convert_fusion.6
  1152.5 4.8 multiply_convert_fusion.6
  1243.5 4.8 multiply_convert_fusion.6
  1256.5 4.8 multiply_convert_fusion.6
  1324.6 5.8 reshape.338
  1330.4 38.8 %all_to_all.24 = bf16[8,2,49152]{2,1,0:T(2,128)(2,1)} all-to-all(bf16[8,2,49152]{2,1,0:T(2,128)(2,1)S(1)} %reshape.338), channel_id=1, replica_groups=mesh['grp'=8,'tm'=4] {'grp'}, dimensions={0} | all-to-all | bytes 3145728 | tf_op jit(solution)/shard_map/all_to_all | solution.py:110
  1369.2 5.2 reshape.339
  1432.3 5.4 collective-permute-done.3
  1446.8 5.1 collective-permute-done.4
  1456.8 5.2 copy.148
  (508 shorter events, 623.9 us)
Async XLA Ops:
  21.3 6.4 copy-start.6
  23.1 17.6 %collective-permute-start = (bf16[2,24,3,4096]{3,1,2,0:T(8,128)(2,1)S(1)}, bf16[2,24,3,4096]{3,1,2,0:T(8,128)(2,1)S(1)}, u32[]{:S(2)}, u32[]{:S(2)}) collective-permute-start(bf16[2,24,3,4096]{3,1,2,0:T(8,128)(2,1)S(1)} %copy.125), channel_id=1, source_target_pairs={{0,1},{1,2},{2,3},{4,5},{5,6},{6,7},{8,9},{9,10},{10,11},{12,13},{... | collective-permute-start | bytes 3538952 | tf_op jit(solution)/shard_map/ppermute | solution.py:23
  359.5 66.3 %all-to-all-start = ((bf16[8,2,98304]{2,1,0:T(2,128)(2,1)}), bf16[8,2,98304]{2,1,0:T(2,128)(2,1)S(1)}, u32[]{:S(2)}, u32[]{:S(2)}) async-start(bf16[8,2,98304]{2,1,0:T(2,128)(2,1)} %reshape.336), calls=%async_computation | async-start | bytes 6291456 | tf_op jit(solution)/shard_map/all_to_all | solution.py:89
  476.4 9.6 copy-start
  1378.4 8.6 copy-start.7
  1385.0 7.9 collective-permute-start.1
  1390.0 3.0 copy-start.5
  1406.6 7.1 collective-permute-start.2
  1421.9 1.6 copy-start.3
  1422.3 1.9 copy-start.2
  1423.9 1.7 copy-start.1
  1430.0 7.7 collective-permute-start.3
  1439.2 1.6 copy-start.4
  1444.2 7.7 collective-permute-start.4
where the time goes:
time: 1480 us; the launch traced here: 1460 us
  other arithmetic  464 us (31%)
  matrix products  450 us (30%)
  local copies, waits for them, and re-layouts  238 us (16%)
  loops' own time  168 us (11%)
  waiting for transfers between devices  84.6 us (6%)
  blocking collectives  38.8 us (3%)
  starting transfers between devices  18.2 us (1%)
    convert_element_type x64, other arithmetic, beam_weights(): (jnp.sin(phases) * scaling).astype(jnp.bfloat16)  309 us
    another operation x1, loops' own time, local(): lax.map(channel_powers, jnp.arange(local_channels, dtype=jnp.int32))  168 us
    unnamed x23, local copies, waits for them, and re-layouts  89.1 us
    convert_element_type x1, other arithmetic, local(): filtered = filtered.astype(jnp.bfloat16)  76.4 us
    dot_general x64, matrix products, channel_powers(): jnp.dot(weight_sin, channel_data[0], preferred_element_type=jnp.float32)  73 us
    dot_general x64, matrix products, channel_powers(): jnp.dot(weight_sin, channel_data[1], preferred_element_type=jnp.float32)  68.7 us
    dot_general x64, matrix products, channel_powers(): jnp.dot(weight_cos, channel_data[1], preferred_element_type=jnp.float32)  68.3 us
    dot_general x64, matrix products, channel_powers(): jnp.dot(weight_cos, channel_data[0], preferred_element_type=jnp.float32)  68.2 us
  transfers between devices with their start and end apart: 6, of which 5 were waited for; matrix products, arithmetic and copies ran while one was open for 1% of the time, Pallas kernels for 0%

commit v1 on v0

v1 whole, which is shorter than its diff:
```python
import functools
import math

import jax
import jax.numpy as jnp
import numpy as np
from jax import lax
from jax.experimental import pallas as pl
from jax.experimental.pallas import tpu as pltpu
from jax.sharding import PartitionSpec as P

TRANSFORM = 4096
CHANNELS = 512
TAPS = 4
INTEG = 8
LEVELS = 4
SHIFT_MOST = 2

RADIX = 4
SUB = TRANSFORM // RADIX
PER = CHANNELS // RADIX
LANES = 128
ROWS = 8
GROUP = 2**LEVELS
VMEM_LIMIT = 60 * 1024 * 1024


def shift_along(x, axis, by):
    length = lax.axis_size(axis)
    pairs = [(i, i + by) for i in range(length) if 0 <= i + by < length]
    return lax.ppermute(x, axis, pairs)


def table_factors():
    k = (RADIX * np.arange(PER)[None, :] + np.arange(RADIX)[:, None])[:, None, :]
    fine = k * np.arange(ROWS)[None, :, None] % TRANSFORM
    coarse = k * (ROWS * np.arange(SUB // ROWS))[None, :, None] % TRANSFORM
    turn = 2.0 * np.pi / TRANSFORM
    scale = 1.0 / math.sqrt(TRANSFORM)
    fine = np.stack([np.cos(fine * turn), np.sin(fine * turn)], 1)
    coarse = np.stack([np.cos(coarse * turn), np.sin(coarse * turn)], 1) * scale
    return fine.astype(np.float32), coarse.astype(np.float32)


def channel_kernel(frames, x_ref, halo_ref, taps_ref, fine_ref, coarse_ref, out_ref, table, folded, spectra, turned):
    stations = x_ref.shape[1]

    @pl.when(pl.program_id(0) == 0)
    def _():
        def build(u, carry):
            for q in range(RADIX):
                ca, sa = fine_ref[q, 0], fine_ref[q, 1]
                cs, ss = [], []
                for half in range(2):
                    cb = coarse_ref[q, 0, pl.ds(2 * u + half, 1), :]
                    sb = coarse_ref[q, 1, pl.ds(2 * u + half, 1), :]
                    cs.append(cb * ca - sb * sa)
                    ss.append(sb * ca + cb * sa)
                c = jnp.concatenate(cs, 0).astype(jnp.bfloat16)
                s = jnp.concatenate(ss, 0)
                top = pl.ds(pl.multiple_of(u * 2 * ROWS, 2 * ROWS), 2 * ROWS)
                low = pl.ds(pl.multiple_of(SUB + u * 2 * ROWS, 2 * ROWS), 2 * ROWS)
                table[q, top, :PER] = c
                table[q, top, PER:] = (-s).astype(jnp.bfloat16)
                table[q, low, :PER] = s.astype(jnp.bfloat16)
                table[q, low, PER:] = c
            return carry

        lax.fori_loop(0, SUB // (2 * ROWS), build, 0)

    def full(x):
        x = x.astype(jnp.float32)
        if stations < ROWS:
            x = jnp.concatenate([x, jnp.zeros((ROWS - stations, LANES), jnp.float32)], 0)
        return x

    parts = [(c, j) for c in range(2) for j in range(RADIX)]

    def columns(tile, carry):
        taps = [
            [
                jnp.broadcast_to(
                    taps_ref[p : p + 1, pl.ds(pl.multiple_of(j * SUB + tile * LANES, LANES), LANES)],
                    (ROWS, LANES),
                )
                for j in range(RADIX)
            ]
            for p in range(TAPS)
        ]

        def at(ref, f, c, j):
            start = pl.multiple_of(f * TRANSFORM + j * SUB + tile * LANES, LANES)
            return full(ref[c, :, pl.ds(start, LANES)])

        def filtered(f, before):
            z, after = {}, []
            for (c, j), old in zip(parts, before):
                now = at(x_ref, f, c, j)
                total = taps[0][j] * now
                for p in range(1, TAPS):
                    total = total + taps[p][j] * old[p - 1]
                z[c, j] = total
                after.append((now, *old[:-1]))
            even = [z[c, 0] + z[c, 2] for c in range(2)]
            odd = [z[c, 0] - z[c, 2] for c in range(2)]
            even1 = [z[c, 1] + z[c, 3] for c in range(2)]
            odd1 = [z[c, 1] - z[c, 3] for c in range(2)]
            y = {
                (0, 0): even[0] + even1[0], (0, 1): even[1] + even1[1],
                (2, 0): even[0] - even1[0], (2, 1): even[1] - even1[1],
                (1, 0): odd[0] + odd1[1], (1, 1): odd[1] - odd1[0],
                (3, 0): odd[0] - odd1[1], (3, 1): odd[1] + odd1[0],
            }
            return y, after

        def pair(step, before):
            f = step * 2
            first, before = filtered(f, before)
            second, before = filtered(f + 1, before)
            rows = pl.ds(pl.multiple_of(f * ROWS, 2 * ROWS), 2 * ROWS)
            for q in range(RADIX):
                for c in range(2):
                    both = jnp.concatenate([first[q, c], second[q, c]], 0)
                    lanes = pl.ds(pl.multiple_of(c * SUB + tile * LANES, LANES), LANES)
                    folded[q, rows, lanes] = both.astype(jnp.bfloat16)
            return before

        before = [tuple(at(halo_ref, TAPS - 2 - p, c, j) for p in range(TAPS - 1)) for c, j in parts]
        lax.fori_loop(0, frames // 2, pair, before)
        return carry

    lax.fori_loop(0, SUB // LANES, columns, 0)

    def residue(q, carry):
        both = jnp.dot(folded[q], table[q], preferred_element_type=jnp.float32)
        spectra[0] = both[:, :PER]
        spectra[1] = both[:, PER:]
        powers = frames // INTEG
        for s in range(stations):
            rows = [
                spectra[part, pl.ds(i * ROWS + s, powers, stride=INTEG * ROWS), :]
                for part in range(2)
                for i in range(INTEG)
            ]
            turned[pl.ds(s, PER, stride=ROWS), :] = jnp.concatenate(rows, 0).T
        block = turned[...].reshape(out_ref.shape[0], out_ref.shape[1], ROWS, LANES)
        out_ref[:, :, q] = block[:, :, :stations].astype(jnp.bfloat16)
        return carry

    lax.fori_loop(0, RADIX, residue, 0)


def channelize(voltages, halo, filter_taps, owners):
    stations = voltages.shape[1]
    frames = voltages.shape[2] // TRANSFORM
    block = ROWS if stations % ROWS == 0 else stations
    assert block <= ROWS and 2 * frames == LANES
    fine, coarse = table_factors()
    return pl.pallas_call(
        functools.partial(channel_kernel, frames),
        grid=(stations // block,),
        in_specs=[
            pl.BlockSpec((2, block, voltages.shape[2]), lambda i: (0, i, 0)),
            pl.BlockSpec((2, block, halo.shape[2]), lambda i: (0, i, 0)),
            pl.BlockSpec(filter_taps.shape, lambda i: (0, 0)),
            pl.BlockSpec(fine.shape, lambda i: (0, 0, 0, 0)),
            pl.BlockSpec(coarse.shape, lambda i: (0, 0, 0, 0)),
        ],
        out_specs=pl.BlockSpec((owners, PER // owners, RADIX, block, LANES), lambda i: (0, 0, 0, i, 0)),
        out_shape=jax.ShapeDtypeStruct((owners, PER // owners, RADIX, stations, LANES), jnp.bfloat16),
        scratch_shapes=[
            pltpu.VMEM((RADIX, 2 * SUB, 2 * PER), jnp.bfloat16),
            pltpu.VMEM((RADIX, frames * ROWS, 2 * SUB), jnp.bfloat16),
            pltpu.VMEM((2, frames * ROWS, PER), jnp.float32),
            pltpu.VMEM((PER * ROWS, LANES), jnp.float32),
        ],
        compiler_params=pltpu.CompilerParams(vmem_limit_bytes=VMEM_LIMIT),
        name="channelize",
    )(voltages, halo, filter_taps, jnp.asarray(fine), jnp.asarray(coarse))


def turn_of(steps):
    whole = 2 * TRANSFORM
    quarter = whole // 4
    moved = (steps & (whole - 1)) + quarter // 2
    x = ((moved & (quarter - 1)) - quarter // 2).astype(jnp.float32) * (2.0 * math.pi / whole)
    side = (moved >> (quarter.bit_length() - 1)) & 3
    y = x * x
    s = x * (1.0 + y * (-1.0 / 6 + y * (1.0 / 120 + y * (-1.0 / 5040 + y * (1.0 / 362880)))))
    c = 1.0 + y * (-0.5 + y * (1.0 / 24 + y * (-1.0 / 720 + y * (1.0 / 40320))))
    odd = (side & 1) == 1
    cos = jnp.where(odd, s, c)
    sin = jnp.where(odd, c, s)
    cos = jnp.where((side == 1) | (side == 2), -cos, cos)
    sin = jnp.where(side >= 2, -sin, sin)
    return cos, sin


def beam_kernel(first_ref, delays_ref, r_ref, out_ref, step_cos, step_sin, mid_cos, mid_sin, left, power):
    sources, count, share, lanes = r_ref.shape
    stations, beams = delays_ref.shape
    half = lanes // 2
    width = 2 * LANES
    pairs = GROUP // 2

    @pl.when(pl.program_id(0) == 0)
    def _():
        def rows(t, carry):
            at = pl.ds(pl.multiple_of(t * ROWS, ROWS), ROWS)
            ch, sh = turn_of(delays_ref[at, :])
            c1, s1 = ch * ch - sh * sh, 2.0 * sh * ch
            for j in range(pairs):
                step_cos[j, at, :] = ch
                step_sin[j, at, :] = sh
                ch, sh = ch * c1 - sh * s1, sh * c1 + ch * s1
            return carry

        lax.fori_loop(0, stations // ROWS, rows, 0)

    twice = 2 * (first_ref[0] + GROUP * pl.program_id(0)) + GROUP - 1
    scale = 1.0 / math.sqrt(stations)

    def middle(t, carry):
        at = pl.ds(pl.multiple_of(t * ROWS, ROWS), ROWS)
        c, s = turn_of(delays_ref[at, :] * twice)
        mid_cos[at, :] = c * scale
        mid_sin[at, :] = s * scale
        return carry

    lax.fori_loop(0, stations // ROWS, middle, 0)

    def lay(k, carry):
        both = jnp.concatenate([r_ref[g, k].astype(jnp.float32) for g in range(sources)], 0).T
        left[k, 0] = both.astype(jnp.bfloat16)
        left[k, 1] = jnp.concatenate([both[half:], -both[:half]], 0).astype(jnp.bfloat16)
        return carry

    lax.fori_loop(0, count, lay, 0)

    def one(k, cos, sin):
        out = jnp.dot(left[k, 0], cos.astype(jnp.bfloat16), preferred_element_type=jnp.float32)
        out = out + jnp.dot(left[k, 1], sin.astype(jnp.bfloat16), preferred_element_type=jnp.float32)
        energy = (out * out).reshape(2 * INTEG, lanes // (2 * INTEG), width)
        return jnp.sum(energy, 0) * (1.0 / INTEG)

    def tile(step, carry):
        j, b = step // (beams // width), step % (beams // width)
        at = pl.ds(pl.multiple_of(b * width, width), width)
        cm, sm = mid_cos[:, at], mid_sin[:, at]
        cj, sj = step_cos[j, :, at], step_sin[j, :, at]
        cc, ss, sc, cs = cm * cj, sm * sj, sm * cj, cm * sj
        power[pairs + j, :, at] = one(pairs + j, cc - ss, sc + cs)
        power[pairs - 1 - j, :, at] = one(pairs - 1 - j, cc + ss, sc - cs)
        return carry

    lax.fori_loop(0, pairs * (beams // width), tile, 0)
    mine = out_ref.shape[3]
    for g in range(out_ref.shape[0]):
        out_ref[g] = power[:, :, g * mine : (g + 1) * mine].astype(jnp.bfloat16)


def beams_of(first, delays, received, owners):
    sources, count, share, lanes = received.shape
    stations, beams = delays.shape
    powers = lanes // (2 * INTEG)
    mine = beams // owners
    return pl.pallas_call(
        beam_kernel,
        grid=(count // GROUP,),
        in_specs=[
            pl.BlockSpec(memory_space=pltpu.SMEM),
            pl.BlockSpec(delays.shape, lambda i: (0, 0)),
            pl.BlockSpec((sources, GROUP, share, lanes), lambda i: (0, i, 0, 0)),
        ],
        out_specs=pl.BlockSpec((owners, GROUP, powers, mine), lambda i: (0, i, 0, 0)),
        out_shape=jax.ShapeDtypeStruct((owners, count, powers, mine), jnp.bfloat16),
        scratch_shapes=[
            pltpu.VMEM((GROUP // 2, stations, beams), jnp.float32),
            pltpu.VMEM((GROUP // 2, stations, beams), jnp.float32),
            pltpu.VMEM((stations, beams), jnp.float32),
            pltpu.VMEM((stations, beams), jnp.float32),
            pltpu.VMEM((GROUP, 2, lanes, stations), jnp.bfloat16),
            pltpu.VMEM((GROUP, powers, beams), jnp.float32),
        ],
        compiler_params=pltpu.CompilerParams(vmem_limit_bytes=VMEM_LIMIT),
        name="beams",
    )(first, delays, received)


def tree_kernel(shifts_ref, own_ref, next_ref, out_ref, ping, pong):
    slots, length, beams = own_ref.shape
    base = pl.program_id(0) * slots
    span = 2 * length
    ping[:, pl.ds(0, length), :] = own_ref[...].astype(jnp.float32)
    ping[:, pl.ds(length, length), :] = next_ref[...].astype(jnp.float32)
    zeros = jnp.zeros((slots, ROWS, beams), jnp.float32)
    ping[:, pl.ds(span, ROWS), :] = zeros
    pong[:, pl.ds(span, ROWS), :] = zeros
    src, dst = ping, pong
    for level in range(LEVELS):
        h = 2**level
        rows = span if level < LEVELS - 1 else length

        def tree(t, carry, src=src, dst=dst, h=h, rows=rows, level=level):
            start = t * GROUP
            for i in range(GROUP // 2):
                lead = start + i // h * 2 * h + i % h
                first = src[lead, pl.ds(0, rows), :]
                shifted = [src[lead + h, pl.ds(by, rows), :] for by in range(SHIFT_MOST + 1)]
                for c in (2 * i, 2 * i + 1):
                    amount = shifts_ref[level, base + start + c]
                    moved = shifted[SHIFT_MOST]
                    for by in range(SHIFT_MOST):
                        moved = jnp.where(amount == by, shifted[by], moved)
                    dst[start + c, pl.ds(0, rows), :] = first + moved
            return carry

        lax.fori_loop(0, slots // GROUP, tree, 0)
        src, dst = dst, src
    for t in range(length):
        out_ref[:, t, :] = (src[:, t, :] * 0.5**LEVELS).T


def dedisperse(shifts, own, after):
    slots, length, beams = own.shape
    block = LANES
    return pl.pallas_call(
        tree_kernel,
        grid=(slots // block,),
        in_specs=[
            pl.BlockSpec(memory_space=pltpu.SMEM),
            pl.BlockSpec((block, length, beams), lambda i: (i, 0, 0)),
            pl.BlockSpec((block, length, beams), lambda i: (i, 0, 0)),
        ],
        out_specs=pl.BlockSpec((beams, length, block), lambda i: (0, 0, i)),
        out_shape=jax.ShapeDtypeStruct((beams, length, slots), jnp.float32),
        scratch_shapes=[
            pltpu.VMEM((block, 2 * length + ROWS, beams), jnp.float32),
            pltpu.VMEM((block, 2 * length + ROWS, beams), jnp.float32),
        ],
        compiler_params=pltpu.CompilerParams(vmem_limit_bytes=VMEM_LIMIT),
        name="dedisperse",
    )(shifts, own, after)


def local(voltages, filter_taps, delays, shifts):
    owners = lax.axis_size("grp")
    halo = shift_along(voltages[:, :, voltages.shape[2] - (TAPS - 1) * TRANSFORM :], "tm", 1)
    spectra = channelize(voltages, halo, filter_taps, owners)
    share = spectra.shape[3]
    mine = CHANNELS // owners
    spectra = spectra.reshape(owners, mine * share, LANES)
    received = lax.all_to_all(spectra, "grp", split_axis=0, concat_axis=0, tiled=True)
    received = received.reshape(owners, mine, share, LANES)
    if share % ROWS:
        received = jnp.transpose(received, (1, 0, 2, 3)).reshape(1, mine, owners * share, LANES)
    first = (lax.axis_index("grp") * mine).astype(jnp.int32).reshape(1)
    powers = beams_of(first, delays, received, owners)
    owned = lax.all_to_all(powers, "grp", split_axis=0, concat_axis=0, tiled=True)
    owned = owned.reshape(CHANNELS, powers.shape[2], powers.shape[3])
    after = shift_along(owned, "tm", -1)
    return jnp.transpose(dedisperse(shifts, owned, after), (0, 2, 1))


def solution(mesh):
    placed = (P(None, "grp", "tm"), P(), P(), P())
    return jax.shard_map(
        local, mesh=mesh, in_specs=placed, out_specs=P("grp", None, "tm"), check_vma=False
    )
```

time: 1480 us -> 305 us (0.21); the launches traced: 1460 us -> 304 us
  other arithmetic: 464 us -> 0 us
  matrix products: 450 us -> 0 us
  local copies, waits for them, and re-layouts: 238 us -> 11.4 us
  loops' own time: 168 us -> 0 us
  Pallas kernels: 0 us -> 137 us
    dot_general x260 -> x0, matrix products: 450 us -> none  [the longest x64 73 us: channel_powers(): jnp.dot(weight_sin, channel_data[0], preferred_element_type=jnp.float32)]
    convert_element_type x72 -> x0, other arithmetic: 407 us -> none  [the longest x64 309 us: beam_weights(): (jnp.sin(phases) * scaling).astype(jnp.bfloat16)]
    another operation x1 -> x0, loops' own time: 168 us -> none  [local(): lax.map(channel_powers, jnp.arange(local_channels, dtype=jnp.int32))]
    pallas_call x0 -> x3, Pallas kernels: none -> 137 us  [the longest x1 75 us: beams_of(): pl.pallas_call(beam_kernel, grid=(count // GROUP,), in_specs=[pl.BlockSpe...]
    unnamed x23 -> x6, local copies, waits for them, and re-layouts: 89.1 us -> 2.69 us
    dynamic_update_slice x64 -> x0, other arithmetic: 39.3 us -> none  [local(): lax.map(channel_powers, jnp.arange(local_channels, dtype=jnp.int32))]
    dynamic_slice x64 -> x0, local copies, waits for them, and re-layouts: 37.3 us -> none  [local(): lax.map(channel_powers, jnp.arange(local_channels, dtype=jnp.int32))]
    another operation x1 -> x0, local copies, waits for them, and re-layouts: 26.3 us -> none  [to_spectra(): spectra = jnp.stack([real_part, imag_part]).astype(jnp.bfloat16)]
  transfers between devices with their start and end apart: 6 -> 3, of which waited for: 5 -> 3; matrix products, arithmetic and copies ran while one was open for 1% -> 0% of each run, Pallas kernels for 0% -> 0%
where the time goes in v1:
time: 305 us; the launch traced here: 304 us
  Pallas kernels  137 us (45%)
  waiting for transfers between devices  93.5 us (31%)
  blocking collectives  50.1 us (16%)
  starting transfers between devices  12 us (4%)
  local copies, waits for them, and re-layouts  11.4 us (4%)
    pallas_call x1, Pallas kernels, beams_of(): pl.pallas_call(beam_kernel, grid=(count // GROUP,), in_specs=[pl.BlockSpe...  75 us
    all_to_all x1, waiting for transfers between devices, local(): lax.all_to_all(spectra, 'grp', split_axis=0, concat_axis=0, tiled=True)  60.3 us
    all_to_all x1, blocking collectives, local(): lax.all_to_all(powers, 'grp', split_axis=0, concat_axis=0, tiled=True)  50.1 us
    pallas_call x1, Pallas kernels, channelize(): pl.pallas_call(functools.partial(channel_kernel, frames), grid=(stations...  44.7 us
    ppermute x2, waiting for transfers between devices, shift_along(): return lax.ppermute(x, axis, pairs)  33.2 us
    pallas_call x1, Pallas kernels, dedisperse(): pl.pallas_call(tree_kernel, grid=(slots // block,), in_specs=[pl.BlockSpe...  17.5 us
    ppermute x2, starting transfers between devices, shift_along(): return lax.ppermute(x, axis, pairs)  6.41 us
  transfers between devices with their start and end apart: 3, of which 3 were waited for; matrix products, arithmetic and copies ran while one was open for 0% of the time, Pallas kernels for 0%

profile of v1, /device:TPU:1, one launch (start us, length us, event | category | flops | bytes accessed | tf_op | source)
XLA Modules:
  0.0 304.3 jit_solution(17455490190904457192)
XLA Ops:
  0.0 1.3 slice.3
  1.4 4.5 %collective-permute-start = (bf16[2,24,12288]{2,1,0:T(8,128)(2,1)S(1)}, bf16[2,24,12288]{2,1,0:T(8,128)(2,1)S(1)}, u32[]{:S(2)}, u32[]{:S(2)}) collective-permute-start(bf16[2,24,12288]{2,1,0:T(8,128)(2,1)S(1)} %slice.3), channel_id=1, source_target_pairs={{0,1},{1,2},{2,3},{4,5},{5,6},{6,7},{8,9},{9,10},{10,11},{12,13},{... | collective-permute-start | bytes 3538952 | tf_op jit(solution)/shard_map/ppermute | solution.py:31
  5.9 13.1 %collective-permute-done.halo_ref = bf16[2,24,12288]{2,1,0:T(8,128)(2,1)S(1)} collective-permute-done((bf16[2,24,12288]{2,1,0:T(8,128)(2,1)S(1)}, bf16[2,24,12288]{2,1,0:T(8,128)(2,1)S(1)}, u32[]{:S(2)}, u32[]{:S(2)}) %collective-permute-start) | collective-permute-done | bytes 1179680 | tf_op jit(solution)/shard_map/ppermute | solution.py:31
  19.0 0.0 copy-start.2
  19.0 1.0 copy-done.2
  20.0 44.7 %channelize.1 = bf16[8,16,4,24,128]{4,3,2,1,0:T(8,128)(2,1)} custom-call(bf16[2,24,262144]{2,1,0:T(8,128)(2,1)} %x_ref.1, bf16[2,24,12288]{2,1,0:T(8,128)(2,1)} %copy-done.2, f32[4,4096]{1,0:T(4,128)} %taps_ref.1, f32[4,2,8,128]{3,2,1,0:T(8,128)} %constant.12.clone.fine_ref, f32[4,2,128,128]{3,2,1,0:T(8,128)} %constant.13.clone.coarse_ref), custom_call_target="tpu_custom_call" | custom-call | tf_op jit(solution)/shard_map/channelize/pallas_call | solution.py:159
  64.7 5.6 %all-to-all-start = ((bf16[8,1536,128]{2,1,0:T(8,128)(2,1)}), bf16[8,1536,128]{2,1,0:T(8,128)(2,1)S(1)}, u32[]{:S(2)}, u32[]{:S(2)}) async-start(bf16[8,1536,128]{2,1,0:T(8,128)(2,1)} %bitcast.8), calls=%async_computation | async-start | bytes 6291456 | tf_op jit(solution)/shard_map/all_to_all | solution.py:353
  70.3 60.3 %all-to-all-done = bf16[8,1536,128]{2,1,0:T(8,128)(2,1)S(1)} async-done(((bf16[8,1536,128]{2,1,0:T(8,128)(2,1)}), bf16[8,1536,128]{2,1,0:T(8,128)(2,1)S(1)}, u32[]{:S(2)}, u32[]{:S(2)}) %all-to-all-start) | async-done | bytes 3145760 | tf_op jit(solution)/shard_map/all_to_all | solution.py:353
  130.6 0.0 copy-start.1
  130.6 1.7 copy-done.1
  132.3 75.0 %beams.1 = bf16[8,64,8,192]{3,2,1,0:T(8,128)(2,1)} custom-call(s32[1]{0:T(128)} %bitcast.first_ref, s32[192,1536]{1,0:T(8,128)} %delays_ref.1, bf16[8,64,24,128]{3,2,1,0:T(8,128)(2,1)} %bitcast.7), custom_call_target="tpu_custom_call" | custom-call | tf_op jit(solution)/shard_map/beams/pallas_call | solution.py:267
  207.2 50.1 %all_to_all.10 = bf16[8,64,8,192]{3,2,1,0:T(8,128)(2,1)S(1)} all-to-all(bf16[8,64,8,192]{3,2,1,0:T(8,128)(2,1)} %beams.1), channel_id=1, replica_groups=mesh['grp'=8,'tm'=4] {'grp'}, dimensions={0} | all-to-all | bytes 3145728 | tf_op jit(solution)/shard_map/all_to_all | solution.py:359
  257.4 0.0 copy-start
  257.4 3.0 copy.7
  260.4 1.9 collective-permute-start.1
  262.3 20.1 %collective-permute-done.1 = bf16[512,8,192]{0,2,1:T(8,128)(2,1)} collective-permute-done((bf16[512,8,192]{0,2,1:T(8,128)(2,1)}, bf16[512,8,192]{0,2,1:T(8,128)(2,1)}, u32[]{:S(2)}, u32[]{:S(2)}) %collective-permute-start.1) | collective-permute-done | bytes 1572896 | tf_op jit(solution)/shard_map/ppermute | solution.py:31
  282.4 4.4 %copy.8.next_ref = bf16[512,8,192]{2,1,0:T(8,128)(2,1)} copy(bf16[512,8,192]{0,2,1:T(8,128)(2,1)} %collective-permute-done.1) | data formatting | bytes 3145728 | tf_op jit(solution)/shard_map/ppermute | solution.py:31
  286.8 0.0 copy-done
  286.8 17.5 %dedisperse.1 = f32[192,8,512]{2,1,0:T(8,128)} custom-call(s32[4,512]{1,0:T(4,128)} %shifts_ref.1, bf16[512,8,192]{2,1,0:T(8,128)(2,1)} %bitcast.6, bf16[512,8,192]{2,1,0:T(8,128)(2,1)} %copy.8.next_ref), custom_call_target="tpu_custom_call" | custom-call | tf_op jit(solution)/shard_map/dedisperse/pallas_call | solution.py:327
Async XLA Ops:
  1.4 17.6 %collective-permute-start = (bf16[2,24,12288]{2,1,0:T(8,128)(2,1)S(1)}, bf16[2,24,12288]{2,1,0:T(8,128)(2,1)S(1)}, u32[]{:S(2)}, u32[]{:S(2)}) collective-permute-start(bf16[2,24,12288]{2,1,0:T(8,128)(2,1)S(1)} %slice.3), channel_id=1, source_target_pairs={{0,1},{1,2},{2,3},{4,5},{5,6},{6,7},{8,9},{9,10},{10,11},{12,13},{... | collective-permute-start | bytes 3538952 | tf_op jit(solution)/shard_map/ppermute | solution.py:31
  19.0 1.0 copy-start.2
  64.7 65.8 %all-to-all-start = ((bf16[8,1536,128]{2,1,0:T(8,128)(2,1)}), bf16[8,1536,128]{2,1,0:T(8,128)(2,1)S(1)}, u32[]{:S(2)}, u32[]{:S(2)}) async-start(bf16[8,1536,128]{2,1,0:T(8,128)(2,1)} %bitcast.8), calls=%async_computation | async-start | bytes 6291456 | tf_op jit(solution)/shard_map/all_to_all | solution.py:353
  130.6 1.7 copy-start.1
  257.4 29.5 %copy-start = (bf16[8,64,8,192]{3,2,1,0:T(8,128)(2,1)}, bf16[8,64,8,192]{3,2,1,0:T(8,128)(2,1)S(1)}, u32[]{:S(2)}) copy-start(bf16[8,64,8,192]{3,2,1,0:T(8,128)(2,1)S(1)} %all_to_all.10) | copy-start | bytes 4718596
  260.4 22.0 %collective-permute-start.1 = (bf16[512,8,192]{0,2,1:T(8,128)(2,1)}, bf16[512,8,192]{0,2,1:T(8,128)(2,1)}, u32[]{:S(2)}, u32[]{:S(2)}) collective-permute-start(bf16[512,8,192]{0,2,1:T(8,128)(2,1)} %copy.7), channel_id=1, source_target_pairs={{1,0},{2,1},{3,2},{5,4},{6,5},{7,6},{9,8},{10,9},{11,10},{13,12},{... | collective-permute-start | bytes 4718600 | tf_op jit(solution)/shard_map/ppermute | solution.py:31

commit v2 on v1

v2 whole, which is shorter than its diff:
```python
import functools
import math

import jax
import jax.numpy as jnp
import numpy as np
from jax import lax
from jax.experimental import pallas as pl
from jax.experimental.pallas import tpu as pltpu
from jax.sharding import PartitionSpec as P

TRANSFORM = 4096
CHANNELS = 512
TAPS = 4
INTEG = 8
LEVELS = 4
SHIFT_MOST = 2

RADIX = 4
SUB = TRANSFORM // RADIX
PER = CHANNELS // RADIX
LANES = 128
WIDE = 2 * LANES
ROWS = 8
STEPS = 2
GROUP = 2**LEVELS
VMEM_LIMIT = 60 * 1024 * 1024


def shift_along(x, axis, by):
    length = lax.axis_size(axis)
    pairs = [(i, i + by) for i in range(length) if 0 <= i + by < length]
    return lax.ppermute(x, axis, pairs)


def table_factors():
    k = (RADIX * np.arange(PER)[None, :] + np.arange(RADIX)[:, None])[:, None, :]
    fine = k * np.arange(ROWS)[None, :, None] % TRANSFORM
    coarse = k * (ROWS * np.arange(SUB // ROWS))[None, :, None] % TRANSFORM
    turn = 2.0 * np.pi / TRANSFORM
    scale = 1.0 / math.sqrt(TRANSFORM)
    fine = np.stack([np.cos(fine * turn), np.sin(fine * turn)], 1)
    coarse = np.stack([np.cos(coarse * turn), np.sin(coarse * turn)], 1) * scale
    return fine.astype(np.float32), coarse.astype(np.float32)


def channel_kernel(frames, x_ref, halo_ref, taps_ref, fine_ref, coarse_ref, *refs):
    *out_refs, table, folded, spectra, turned, weights, rim = refs
    stations = x_ref.shape[1]
    here = x_ref.shape[2] // TRANSFORM
    step, steps = pl.program_id(1), pl.num_programs(1)

    @pl.when((pl.program_id(0) == 0) & (step == 0))
    def _():
        for p in range(TAPS):
            weights[p] = jnp.broadcast_to(taps_ref[p : p + 1, :], (ROWS, TRANSFORM)).astype(jnp.bfloat16)

        def build(u, carry):
            for q in range(RADIX):
                ca, sa = fine_ref[q, 0], fine_ref[q, 1]
                cs, ss = [], []
                for half in range(2):
                    cb = coarse_ref[q, 0, pl.ds(2 * u + half, 1), :]
                    sb = coarse_ref[q, 1, pl.ds(2 * u + half, 1), :]
                    cs.append(cb * ca - sb * sa)
                    ss.append(sb * ca + cb * sa)
                c = jnp.concatenate(cs, 0).astype(jnp.bfloat16)
                s = jnp.concatenate(ss, 0)
                top = pl.ds(pl.multiple_of(u * 2 * ROWS, 2 * ROWS), 2 * ROWS)
                low = pl.ds(pl.multiple_of(SUB + u * 2 * ROWS, 2 * ROWS), 2 * ROWS)
                table[q, top, :PER] = c
                table[q, top, PER:] = (-s).astype(jnp.bfloat16)
                table[q, low, :PER] = s.astype(jnp.bfloat16)
                table[q, low, PER:] = c
            return carry

        lax.fori_loop(0, SUB // (2 * ROWS), build, 0)

    @pl.when(step == 0)
    def _():
        rim[...] = halo_ref[...]

    def full(x):
        if stations < ROWS:
            x = jnp.concatenate([x, jnp.zeros((ROWS - stations, WIDE), x.dtype)], 0)
        return x

    parts = [(c, j) for c in range(2) for j in range(RADIX)]

    def columns(tile, carry):
        taps = [
            [weights[p, :, pl.ds(pl.multiple_of(j * SUB + tile * WIDE, WIDE), WIDE)] for j in range(RADIX)]
            for p in range(TAPS)
        ]

        def at(ref, f, c, j):
            start = pl.multiple_of(f * TRANSFORM + j * SUB + tile * WIDE, WIDE)
            return full(ref[c, :, pl.ds(start, WIDE)])

        def filtered(f, before):
            z, after = {}, []
            for (c, j), old in zip(parts, before):
                now = at(x_ref, f, c, j)
                total = taps[0][j] * now
                for p in range(1, TAPS):
                    total = total + taps[p][j] * old[p - 1]
                z[c, j] = total
                after.append((now, *old[:-1]))
            even = [z[c, 0] + z[c, 2] for c in range(2)]
            odd = [z[c, 0] - z[c, 2] for c in range(2)]
            even1 = [z[c, 1] + z[c, 3] for c in range(2)]
            odd1 = [z[c, 1] - z[c, 3] for c in range(2)]
            y = {
                (0, 0): even[0] + even1[0], (0, 1): even[1] + even1[1],
                (2, 0): even[0] - even1[0], (2, 1): even[1] - even1[1],
                (1, 0): odd[0] + odd1[1], (1, 1): odd[1] - odd1[0],
                (3, 0): odd[0] - odd1[1], (3, 1): odd[1] + odd1[0],
            }
            return y, after

        def pair(two, before):
            f = two * 2
            first, before = filtered(f, before)
            second, before = filtered(f + 1, before)
            rows = pl.ds(pl.multiple_of((step * here + f) * ROWS, 2 * ROWS), 2 * ROWS)
            for q in range(RADIX):
                for c in range(2):
                    both = jnp.concatenate([first[q, c], second[q, c]], 0)
                    lanes = pl.ds(pl.multiple_of(c * SUB + tile * WIDE, WIDE), WIDE)
                    folded[q, rows, lanes] = both.astype(jnp.bfloat16)
            return before

        before = [tuple(at(rim, TAPS - 2 - p, c, j) for p in range(TAPS - 1)) for c, j in parts]
        lax.fori_loop(0, here // 2, pair, before)
        return carry

    lax.fori_loop(0, SUB // WIDE, columns, 0)

    @pl.when(step < steps - 1)
    def _():
        rim[...] = x_ref[:, :, pl.ds((here - TAPS + 1) * TRANSFORM, (TAPS - 1) * TRANSFORM)]

    def transform(q):
        both = jnp.dot(folded[q], table[q], preferred_element_type=jnp.float32)
        spectra[q % 2, 0] = both[:, :PER]
        spectra[q % 2, 1] = both[:, PER:]

    def lay(q):
        powers = frames // INTEG
        for s in range(stations):
            rows = [
                spectra[q % 2, part, pl.ds(i * ROWS + s, powers, stride=INTEG * ROWS), :]
                for part in range(2)
                for i in range(INTEG)
            ]
            turned[q % 2, pl.ds(s, PER, stride=ROWS), :] = jnp.concatenate(rows, 0).T
        start = 0
        for out_ref in out_refs:
            owners, groups, per = out_ref.shape[:3]
            for n in range(groups):
                many = owners * per * ROWS
                block = turned[q % 2, start : start + many].reshape(owners, per, ROWS, LANES)
                out_ref[:, n, :, q] = block[:, :, :stations].astype(jnp.bfloat16)
                start += many

    @pl.when(step == steps - 1)
    def _():
        for q in range(RADIX + 1):
            if q < RADIX:
                transform(q)
            if q:
                lay(q - 1)


def channelize(voltages, halo, filter_taps, owners, first, last, pieces):
    stations = last - first
    frames = voltages.shape[2] // TRANSFORM
    block = ROWS if stations % ROWS == 0 else stations
    assert block <= ROWS and 2 * frames == LANES and first % block == 0
    offset = first // block
    per = GROUP // RADIX
    fine, coarse = table_factors()
    return pl.pallas_call(
        functools.partial(channel_kernel, frames),
        grid=(stations // block, STEPS),
        in_specs=[
            pl.BlockSpec((2, block, voltages.shape[2] // STEPS), lambda i, h: (0, i + offset, h)),
            pl.BlockSpec((2, block, halo.shape[2]), lambda i, h: (0, i, 0)),
            pl.BlockSpec(filter_taps.shape, lambda i, h: (0, 0)),
            pl.BlockSpec(fine.shape, lambda i, h: (0, 0, 0, 0)),
            pl.BlockSpec(coarse.shape, lambda i, h: (0, 0, 0, 0)),
        ],
        out_specs=[
            pl.BlockSpec((owners, n, per, RADIX, block, LANES), lambda i, h: (0, 0, 0, 0, i, 0)) for n in pieces
        ],
        out_shape=[
            jax.ShapeDtypeStruct((owners, n, per, RADIX, stations, LANES), jnp.bfloat16) for n in pieces
        ],
        scratch_shapes=[
            pltpu.VMEM((RADIX, 2 * SUB, 2 * PER), jnp.bfloat16),
            pltpu.VMEM((RADIX, frames * ROWS, 2 * SUB), jnp.bfloat16),
            pltpu.VMEM((2, 2, frames * ROWS, PER), jnp.float32),
            pltpu.VMEM((2, PER * ROWS, LANES), jnp.float32),
            pltpu.VMEM((TAPS, ROWS, TRANSFORM), jnp.bfloat16),
            pltpu.VMEM((2, block, (TAPS - 1) * TRANSFORM), jnp.bfloat16),
        ],
        compiler_params=pltpu.CompilerParams(vmem_limit_bytes=VMEM_LIMIT),
        cost_estimate=pl.CostEstimate(
            flops=stations * frames * 8 * SUB * CHANNELS, bytes_accessed=stations * 4 * voltages.shape[2], transcendentals=0
        ),
        name="channelize",
    )(voltages, halo, filter_taps, jnp.asarray(fine), jnp.asarray(coarse))


def turn_of(steps):
    whole = 2 * TRANSFORM
    quarter = whole // 4
    moved = (steps & (whole - 1)) + quarter // 2
    x = ((moved & (quarter - 1)) - quarter // 2).astype(jnp.float32) * (2.0 * math.pi / whole)
    side = (moved >> (quarter.bit_length() - 1)) & 3
    y = x * x
    s = x * (1.0 + y * (-1.0 / 6 + y * (1.0 / 120 + y * (-1.0 / 5040 + y * (1.0 / 362880)))))
    c = 1.0 + y * (-0.5 + y * (1.0 / 24 + y * (-1.0 / 720 + y * (1.0 / 40320))))
    odd = (side & 1) == 1
    cos = jnp.where(odd, s, c)
    sin = jnp.where(odd, c, s)
    cos = jnp.where((side == 1) | (side == 2), -cos, cos)
    sin = jnp.where(side >= 2, -sin, sin)
    return cos, sin


def packing(mine):
    whole, rest = divmod(mine, LANES)
    part = 1 << (rest - 1).bit_length() if rest else LANES
    share = part * GROUP // LANES if rest else 0
    return whole, rest, part, share


def turns(first, delays, owners, groups):
    stations, beams = delays.shape
    pairs = GROUP // 2

    def kernel(first_ref, delays_ref, step_ref, mid_ref):
        ch, sh = turn_of(delays_ref[...])
        twice = 2.0 * (ch * ch - sh * sh)
        before, now = (ch, -sh), (ch, sh)
        for j in range(pairs):
            step_ref[j, 0], step_ref[j, 1] = now
            before, now = now, (twice * now[0] - before[0], twice * now[1] - before[1])
        for a in range(groups):
            c, s = turn_of(delays_ref[...] * (2 * (first_ref[0] + owners * GROUP * a) + GROUP - 1))
            mid_ref[a, 0] = c * (1.0 / math.sqrt(stations))
            mid_ref[a, 1] = s * (1.0 / math.sqrt(stations))

    return pl.pallas_call(
        kernel,
        grid=(stations // ROWS,),
        in_specs=[
            pl.BlockSpec(memory_space=pltpu.SMEM),
            pl.BlockSpec((ROWS, beams), lambda i: (i, 0)),
        ],
        out_specs=[
            pl.BlockSpec((pairs, 2, ROWS, beams), lambda i: (0, 0, i, 0)),
            pl.BlockSpec((groups, 2, ROWS, beams), lambda i: (0, 0, i, 0)),
        ],
        out_shape=[
            jax.ShapeDtypeStruct((pairs, 2, stations, beams), jnp.float32),
            jax.ShapeDtypeStruct((groups, 2, stations, beams), jnp.float32),
        ],
        compiler_params=pltpu.CompilerParams(vmem_limit_bytes=VMEM_LIMIT),
        cost_estimate=pl.CostEstimate(
            flops=200 * stations * beams, bytes_accessed=8 * (pairs + groups) * stations * beams, transcendentals=0
        ),
        name="turns",
    )(first, delays)


def beam_kernel(step_ref, mid_ref, *refs):
    left, power = refs[-2:]
    *r_refs, out_ref = refs[:-2]
    lanes = r_refs[0].shape[3]
    _, _, beams = step_ref.shape
    half = lanes // 2
    width = 2 * LANES
    pairs = GROUP // 2
    j = pl.program_id(1)

    def lay(k, carry):
        both = [r[g, k].astype(jnp.float32) for r in r_refs for g in range(r.shape[0])]
        both = jnp.concatenate(both, 0).T
        left[k, 0] = both.astype(jnp.bfloat16)
        left[k, 1] = jnp.concatenate([both[half:], -both[:half]], 0).astype(jnp.bfloat16)
        return carry

    @pl.when(j == 0)
    def _():
        lax.fori_loop(0, GROUP, lay, 0)

    def one(k, cos, sin):
        out = jnp.dot(left[k, 0], cos.astype(jnp.bfloat16), preferred_element_type=jnp.float32)
        out = out + jnp.dot(left[k, 1], sin.astype(jnp.bfloat16), preferred_element_type=jnp.float32)
        energy = (out * out).reshape(2 * INTEG, lanes // (2 * INTEG), width)
        return jnp.sum(energy, 0) * (1.0 / INTEG)

    for b in range(beams // width):
        at = slice(b * width, (b + 1) * width)
        cm, sm = mid_ref[0, :, at], mid_ref[1, :, at]
        cj, sj = step_ref[0, :, at], step_ref[1, :, at]
        cc, ss, sc, cs = cm * cj, sm * sj, sm * cj, cm * sj
        power[pairs + j, :, at] = one(pairs + j, cc - ss, sc + cs)
        power[pairs - 1 - j, :, at] = one(pairs - 1 - j, cc + ss, sc - cs)
    mine = beams // out_ref.shape[0]
    whole, rest, part, share = packing(mine)

    @pl.when(j == pairs - 1)
    def _():
        for g in range(out_ref.shape[0]):
            own = power[:, :, g * mine : (g + 1) * mine]
            for t in range(whole):
                out_ref[g, t * GROUP : (t + 1) * GROUP] = own[:, :, t * LANES : (t + 1) * LANES].astype(jnp.bfloat16)
            if rest:
                tail = own[:, :, whole * LANES :]
                if part > rest:
                    tail = jnp.concatenate([tail, jnp.zeros((*tail.shape[:2], part - rest), tail.dtype)], 2)
                tail = jnp.concatenate([tail[m * share : (m + 1) * share] for m in range(LANES // part)], 2)
                out_ref[g, whole * GROUP :] = tail.astype(jnp.bfloat16)


def beams_of(steps, mids, received, owners, start, count):
    pairs, _, stations, beams = steps.shape
    lanes = received[0][0].shape[3]
    powers = lanes // (2 * INTEG)
    whole, _, _, share = packing(beams // owners)
    rows = whole * GROUP + share
    return pl.pallas_call(
        beam_kernel,
        grid=(count, pairs),
        in_specs=[
            pl.BlockSpec((None, 2, stations, beams), lambda i, j: (j, 0, 0, 0)),
            pl.BlockSpec((None, 2, stations, beams), lambda i, j: (i + start, 0, 0, 0)),
            *[
                pl.BlockSpec((r.shape[0], GROUP, r.shape[2], lanes), lambda i, j, at=at: (0, i + start - at, 0, 0))
                for r, at in received
            ],
        ],
        out_specs=pl.BlockSpec((owners, None, rows, powers, LANES), lambda i, j: (0, i, 0, 0, 0)),
        out_shape=jax.ShapeDtypeStruct((owners, count, rows, powers, LANES), jnp.bfloat16),
        scratch_shapes=[
            pltpu.VMEM((GROUP, 2, lanes, stations), jnp.bfloat16),
            pltpu.VMEM((GROUP, powers, beams), jnp.float32),
        ],
        compiler_params=pltpu.CompilerParams(vmem_limit_bytes=VMEM_LIMIT),
        cost_estimate=pl.CostEstimate(
            flops=8 * count * GROUP * beams * stations * lanes, bytes_accessed=4 * stations * beams, transcendentals=0
        ),
        name="beams",
    )(steps, mids, *[r for r, _ in received])


def tree_kernel(first_slot, beams, shifts_ref, own_ref, next_ref, *refs):
    out_ref, ping, pong = refs[-3:]
    sources, _, _, length, _ = own_ref.shape
    own_ref, next_ref = own_ref.at[:, 0], next_ref.at[:, 0]
    tiles, slots, depth, _ = ping.shape
    base = first_slot + (pl.program_id(0) * pl.num_programs(1) + pl.program_id(1)) * slots
    span = 2 * length
    whole, rest, part, share = packing(beams)
    zeros = jnp.zeros((tiles, slots, depth - span, LANES), jnp.float32)
    ping[:, :, pl.ds(span, depth - span), :] = zeros
    pong[:, :, pl.ds(span, depth - span), :] = zeros
    for ref, at in ((own_ref, 0), (next_ref, length)):
        for s in range(sources):
            for t in range(whole):
                block = ref[s, t * GROUP : (t + 1) * GROUP].astype(jnp.float32)
                ping[t, s * GROUP : (s + 1) * GROUP, pl.ds(at, length), :] = block
            if rest:
                block = ref[s, whole * GROUP :].astype(jnp.float32)
                for m in range(LANES // part):
                    low = s * GROUP + m * share
                    moved = pltpu.roll(block, LANES - m * part, 2) if m else block
                    ping[whole, low : low + share, pl.ds(at, length), :] = moved
    src, dst = ping, pong
    for level in range(LEVELS):
        h = 2**level
        rows = span if level < LEVELS - 1 else length

        def tree(t, carry, src=src, dst=dst, h=h, rows=rows, level=level):
            start = t * GROUP
            for i in range(GROUP // 2):
                lead = start + i // h * 2 * h + i % h
                amounts = [shifts_ref[level, base + start + 2 * i + r] for r in range(2)]
                for tile in range(tiles):
                    first = src[tile, lead, pl.ds(0, rows), :]
                    shifted = [src[tile, lead + h, pl.ds(by, rows), :] for by in range(SHIFT_MOST + 1)]
                    for r in range(2):
                        moved = shifted[SHIFT_MOST]
                        for by in range(SHIFT_MOST):
                            moved = jnp.where(amounts[r] == by, shifted[by], moved)
                        dst[tile, start + 2 * i + r, pl.ds(0, rows), :] = first + moved
            return carry

        lax.fori_loop(0, slots // GROUP, tree, 0)
        src, dst = dst, src
    for tile in range(tiles):
        flat = src.at[tile].reshape(slots * depth, LANES)
        here = min(LANES, beams - tile * LANES)
        for t in range(length):
            turned = (flat[pl.ds(t, slots, stride=depth), :] * 0.5**LEVELS).T
            out_ref[pl.ds(tile * LANES * length + t, here, stride=length), :] = turned[:here]


def dedisperse(shifts, own, after, beams, first_slot, total, so_far):
    sources, groups, rows, length, _ = own.shape
    block = LANES // GROUP
    blocks = sources // block
    tiles = pl.cdiv(beams, LANES)
    depth = 2 * length + ROWS
    earlier = [] if so_far is None else [so_far]
    return pl.pallas_call(
        functools.partial(tree_kernel, first_slot, beams),
        grid=(groups, blocks),
        in_specs=[
            pl.BlockSpec(memory_space=pltpu.SMEM),
            pl.BlockSpec((block, 1, rows, length, LANES), lambda a, i: (i, a, 0, 0, 0)),
            pl.BlockSpec((block, 1, rows, length, LANES), lambda a, i: (i, a, 0, 0, 0)),
            *[pl.BlockSpec(memory_space=pl.ANY) for _ in earlier],
        ],
        out_specs=pl.BlockSpec((beams * length, LANES), lambda a, i: (0, first_slot // LANES + a * blocks + i)),
        out_shape=jax.ShapeDtypeStruct((beams * length, total), jnp.float32),
        scratch_shapes=[pltpu.VMEM((tiles, LANES, depth, LANES), jnp.float32)] * 2,
        input_output_aliases={3: 0} if earlier else {},
        compiler_params=pltpu.CompilerParams(vmem_limit_bytes=VMEM_LIMIT),
        cost_estimate=pl.CostEstimate(
            flops=16 * beams * length * GROUP * sources * groups, bytes_accessed=10 * beams * length * GROUP * sources * groups, transcendentals=0
        ),
        name="dedisperse",
    )(shifts, own, after, *earlier)


def swapped(x, owners):
    return lax.all_to_all(x.reshape(owners, -1, LANES), "grp", split_axis=0, concat_axis=0, tiled=True)


def local(voltages, filter_taps, delays, shifts):
    owners = lax.axis_size("grp")
    share = voltages.shape[1]
    groups = CHANNELS // (owners * GROUP)
    length = voltages.shape[2] // TRANSFORM // INTEG
    beams = delays.shape[1] // owners
    rim = voltages.shape[2] - (TAPS - 1) * TRANSFORM
    cuts = [0, ROWS, share] if share > ROWS else [0, share]
    early = [groups // 2, groups - groups // 2] if groups > 1 else [groups]
    calls = [groups // 2] + [1] * (groups - groups // 2) if groups > 1 else [groups]
    halos = []
    for first, last in zip(cuts, cuts[1:]):
        halos.append(shift_along(voltages[:, first:last, rim:], "tm", 1))
    received = []
    for n, (first, last) in enumerate(zip(cuts, cuts[1:])):
        pieces = early if last == share else [groups]
        arrays = channelize(voltages, halos[n], filter_taps, owners, first, last, pieces)
        start = 0
        for many, array in zip(pieces, arrays):
            here = swapped(array, owners)
            here = here.reshape(owners, many * GROUP, last - first, LANES)
            if (last - first) % ROWS:
                here = jnp.transpose(here, (1, 0, 2, 3)).reshape(1, many * GROUP, -1, LANES)
            received.append((here, start, start + many))
            start += many
    by_owner = delays.reshape(owners, share, delays.shape[1])
    delays = jnp.concatenate([by_owner[:, a:b].reshape(-1, delays.shape[1]) for a, b in zip(cuts, cuts[1:])])
    mine = (lax.axis_index("grp") * GROUP).astype(jnp.int32).reshape(1)
    steps, mids = turns(mine, delays, owners, groups)
    out, start = None, 0
    for many in calls:
        arrays = [(r, low) for r, low, high in received if low <= start and start + many <= high]
        power = beams_of(steps, mids, arrays, owners, start, many)
        owned = swapped(power, owners).reshape(power.shape)
        after = shift_along(owned, "tm", -1)
        out = dedisperse(shifts, owned, after, beams, start * owners * GROUP, CHANNELS, out)
        start += many
    return jnp.transpose(out.reshape(beams, length, CHANNELS), (0, 2, 1))


def solution(mesh):
    placed = (P(None, "grp", "tm"), P(), P(), P())
    return jax.shard_map(local, mesh=mesh, in_specs=placed, out_specs=P("grp", None, "tm"), check_vma=False)
```

time: 305 us -> 226 us (0.74)
  waiting for transfers between devices: 93.5 us -> 24.6 us
  starting transfers between devices: 12 us -> 40.9 us
  blocking collectives: 50.1 us -> 23.2 us
  Pallas kernels: 137 us -> 127 us
  local copies, waits for them, and re-layouts: 11.4 us -> 6.38 us
    all_to_all x1 -> x5, waiting for transfers between devices: 60.3 us -> 10.9 us  [swapped(): lax.all_to_all(x.reshape(owners, -1, LANES), 'grp', split_axis=0, concat_...]
    all_to_all x1, blocking collectives: 50.1 us -> 23.2 us  [swapped(): lax.all_to_all(x.reshape(owners, -1, LANES), 'grp', split_axis=0, concat_...]
    ppermute x2 -> x5, waiting for transfers between devices: 33.2 us -> 13.6 us  [shift_along(): return lax.ppermute(x, axis, pairs)]
    all_to_all x1 -> x5, starting transfers between devices: 5.56 us -> 24.2 us  [swapped(): lax.all_to_all(x.reshape(owners, -1, LANES), 'grp', split_axis=0, concat_...]
    ppermute x2 -> x5, starting transfers between devices: 6.41 us -> 16.7 us  [shift_along(): return lax.ppermute(x, axis, pairs)]
    pallas_call x1 -> x2, Pallas kernels: 44.7 us -> 34.6 us  [channelize(): pl.pallas_call(functools.partial(channel_kernel, frames), grid=(stations...]
    ppermute x1 -> x0, local copies, waits for them, and re-layouts: 4.4 us -> none  [shift_along(): return lax.ppermute(x, axis, pairs)]
    pallas_call x2 -> x7, Pallas kernels: 92.5 us -> 92.5 us  [the longest x3 58.4 us: beams_of(): pl.pallas_call(beam_kernel, grid=(count, pairs), in_specs=[pl.BlockSpec((...]
  transfers between devices with their start and end apart: 3 -> 10, of which waited for: 3 -> 4; matrix products, arithmetic and copies ran while one was open for 0% -> 1% of each run, Pallas kernels for 0% -> 49%
where the time goes in v2:
time: 226 us; the launch traced here: 223 us
  Pallas kernels  127 us (56%)
  starting transfers between devices  40.9 us (18%)
  waiting for transfers between devices  24.6 us (11%)
  blocking collectives  23.2 us (10%)
  local copies, waits for them, and re-layouts  6.38 us (3%)
    pallas_call x3, Pallas kernels, beams_of(): pl.pallas_call(beam_kernel, grid=(count, pairs), in_specs=[pl.BlockSpec((...  58.4 us
    pallas_call x2, Pallas kernels, channelize(): pl.pallas_call(functools.partial(channel_kernel, frames), grid=(stations...  34.6 us
    all_to_all x5, starting transfers between devices, swapped(): lax.all_to_all(x.reshape(owners, -1, LANES), 'grp', split_axis=0, concat_...  24.2 us
    all_to_all x1, blocking collectives, swapped(): lax.all_to_all(x.reshape(owners, -1, LANES), 'grp', split_axis=0, concat_...  23.2 us
    pallas_call x1, Pallas kernels, turns(): pl.pallas_call(kernel, grid=(stations // ROWS,), in_specs=[pl.BlockSpec(m...  17.6 us
    ppermute x5, starting transfers between devices, shift_along(): return lax.ppermute(x, axis, pairs)  16.7 us
    pallas_call x3, Pallas kernels, dedisperse(): pl.pallas_call(functools.partial(tree_kernel, first_slot, beams), grid=(g...  16.5 us
    ppermute x5, waiting for transfers between devices, shift_along(): return lax.ppermute(x, axis, pairs)  13.6 us
  transfers between devices with their start and end apart: 10, of which 4 were waited for; matrix products, arithmetic and copies ran while one was open for 1% of the time, Pallas kernels for 49%

profile of v2, /device:TPU:1, one launch (start us, length us, event | category | flops | bytes accessed | tf_op | source)
XLA Modules:
  0.0 223.4 jit_solution(7669570666100077513)
XLA Ops:
  0.0 1.0 slice.14
  1.0 4.5 %collective-permute-start = (bf16[2,8,12288]{2,1,0:T(8,128)(2,1)S(1)}, bf16[2,8,12288]{2,1,0:T(8,128)(2,1)S(1)}, u32[]{:S(2)}, u32[]{:S(2)}) collective-permute-start(bf16[2,8,12288]{2,1,0:T(8,128)(2,1)S(1)} %slice.14), channel_id=1, source_target_pairs={{0,1},{1,2},{2,3},{4,5},{5,6},{6,7},{8,9},{9,10},{10,11},{12,13},{... | collective-permute-start | bytes 1179656 | tf_op jit(solution)/shard_map/ppermute | solution.py:33
  5.5 4.7 %collective-permute-done.halo_ref = bf16[2,8,12288]{2,1,0:T(8,128)(2,1)S(1)} collective-permute-done((bf16[2,8,12288]{2,1,0:T(8,128)(2,1)S(1)}, bf16[2,8,12288]{2,1,0:T(8,128)(2,1)S(1)}, u32[]{:S(2)}, u32[]{:S(2)}) %collective-permute-start) | collective-permute-done | bytes 393248 | tf_op jit(solution)/shard_map/ppermute | solution.py:33
  10.2 0.0 copy-start.9
  10.2 0.7 copy-done.9
  11.0 12.9 %channelize.2 = bf16[8,4,4,4,8,128]{5,4,3,2,1,0:T(8,128)(2,1)} custom-call(bf16[2,24,262144]{2,1,0:T(8,128)(2,1)} %x_ref.3, bf16[2,8,12288]{2,1,0:T(8,128)(2,1)} %copy-done.9, f32[4,4096]{1,0:T(4,128)} %taps_ref.3, f32[4,2,8,128]{3,2,1,0:T(8,128)} %constant.12.clone.fine_ref, f32[4,2,128,128]{3,2,1,0:T(8,128)} %constant.13.clone.coarse_ref), custom_call_target="tpu_custom_call" | custom-call | flops 2147483648 | bytes 8388608 | tf_op jit(solution)/shard_map/channelize/pallas_call | solution.py:183
  23.9 5.6 %all-to-all-start = ((bf16[8,512,128]{2,1,0:T(8,128)(2,1)}), bf16[8,512,128]{2,1,0:T(8,128)(2,1)S(1)}, u32[]{:S(2)}, u32[]{:S(2)}) async-start(bf16[8,512,128]{2,1,0:T(8,128)(2,1)} %bitcast.25), calls=%async_computation | async-start | bytes 2097152 | tf_op jit(solution)/shard_map/all_to_all | solution.py:441
  29.4 1.2 slice.15
  30.6 4.7 %collective-permute-start.1 = (bf16[2,16,12288]{2,1,0:T(8,128)(2,1)S(1)}, bf16[2,16,12288]{2,1,0:T(8,128)(2,1)S(1)}, u32[]{:S(2)}, u32[]{:S(2)}) collective-permute-start(bf16[2,16,12288]{2,1,0:T(8,128)(2,1)S(1)} %slice.15), channel_id=1, source_target_pairs={{0,1},{1,2},{2,3},{4,5},{5,6},{6,7},{8,9},{9,10},{10,11},{12,13},{... | collective-permute-start | bytes 2359304 | tf_op jit(solution)/shard_map/ppermute | solution.py:33
  35.3 8.9 %collective-permute-done.1.halo_ref = bf16[2,16,12288]{2,1,0:T(8,128)(2,1)S(1)} collective-permute-done((bf16[2,16,12288]{2,1,0:T(8,128)(2,1)S(1)}, bf16[2,16,12288]{2,1,0:T(8,128)(2,1)S(1)}, u32[]{:S(2)}, u32[]{:S(2)}) %collective-permute-start.1) | collective-permute-done | bytes 786464 | tf_op jit(solution)/shard_map/ppermute | solution.py:33
  44.2 0.0 copy-start.5
  44.2 0.9 copy-done.5
  45.1 21.7 %channelize.3 = (bf16[8,2,4,4,16,128]{5,4,3,2,1,0:T(8,128)(2,1)}, bf16[8,2,4,4,16,128]{5,4,3,2,1,0:T(8,128)(2,1)}) custom-call(bf16[2,24,262144]{2,1,0:T(8,128)(2,1)} %x_ref.3, bf16[2,16,12288]{2,1,0:T(8,128)(2,1)} %copy-done.5, f32[4,4096]{1,0:T(4,128)} %taps_ref.3, f32[4,2,8,128]{3,2,1,0:T(8,128)} %constant.12.clone.fine_ref, ...), custom_call_target="tpu_custom_call" | custom-call | flops 4294967296 | bytes 16777216 | tf_op jit(solution)/shard_map/channelize/pallas_call | solution.py:183
  66.8 0.0 all-to-all-done
  66.8 0.0 copy-start
  66.8 23.2 %all_to_all.30 = bf16[8,512,128]{2,1,0:T(8,128)(2,1)} all-to-all(bf16[8,512,128]{2,1,0:T(8,128)(2,1)} %bitcast.38), channel_id=1, replica_groups=mesh['grp'=8,'tm'=4] {'grp'}, dimensions={0} | all-to-all | bytes 2097152 | tf_op jit(solution)/shard_map/all_to_all | solution.py:441
  90.0 4.2 %all-to-all-start.4 = ((bf16[8,512,128]{2,1,0:T(8,128)(2,1)}), bf16[8,512,128]{2,1,0:T(8,128)(2,1)}, u32[]{:S(2)}, u32[]{:S(2)}) async-start(bf16[8,512,128]{2,1,0:T(8,128)(2,1)} %bitcast.37), calls=%async_computation.4 | async-start | bytes 2097152 | tf_op jit(solution)/shard_map/all_to_all | solution.py:441
  94.2 0.0 copy-done.4
  94.2 0.1 slice.17
  94.3 0.0 copy-done
  94.3 1.1 pad_add_fusion.delays_ref
  95.4 17.6 %turns.1 = (f32[8,2,192,1536]{3,2,1,0:T(8,128)}, f32[4,2,192,1536]{3,2,1,0:T(8,128)}) custom-call(s32[1]{0:T(128)} %bitcast.first_ref, s32[192,1536]{1,0:T(8,128)} %pad_add_fusion.delays_ref), custom_call_target="tpu_custom_call" | custom-call | flops 58982400 | bytes 28311552 | tf_op jit(solution)/shard_map/turns/pallas_call | solution.py:255
  113.1 15.1 %beams.4 = bf16[8,1,24,8,128]{4,3,2,1,0:T(8,128)(2,1)} custom-call(f32[8,2,192,1536]{3,2,1,0:T(8,128)} %get-tuple-element.9.step_ref, f32[4,2,192,1536]{3,2,1,0:T(8,128)} %get-tuple-element.10.mid_ref, bf16[8,64,8,128]{3,2,1,0:T(8,128)(2,1)} %bitcast.20, bf16[8,32,16,128]{3,2,1,0:T(8,128)(2,1)} %bitcast.23), custom_call_target="tpu_custom_call" | custom-call | flops 4831838208 | bytes 1179648 | tf_op jit(solution)/shard_map/beams/pallas_call | solution.py:335
  128.1 0.0 all-to-all-done.4
  128.1 5.3 %all-to-all-start.3 = ((bf16[8,192,128]{2,1,0:T(8,128)(2,1)}), bf16[8,192,128]{2,1,0:T(8,128)(2,1)S(1)}, u32[]{:S(2)}, u32[]{:S(2)}) async-start(bf16[8,192,128]{2,1,0:T(8,128)(2,1)} %bitcast.30), calls=%async_computation.3 | async-start | bytes 786432 | tf_op jit(solution)/shard_map/all_to_all | solution.py:441
  133.5 28.3 %beams.5 = bf16[8,2,24,8,128]{4,3,2,1,0:T(8,128)(2,1)} custom-call(f32[8,2,192,1536]{3,2,1,0:T(8,128)} %get-tuple-element.9.step_ref, f32[4,2,192,1536]{3,2,1,0:T(8,128)} %get-tuple-element.10.mid_ref, bf16[8,64,8,128]{3,2,1,0:T(8,128)(2,1)} %bitcast.21, bf16[8,32,16,128]{3,2,1,0:T(8,128)(2,1)} %bitcast.13.refs_1_), custom_call_target="tpu_custom_call" | custom-call | flops 9663676416 | bytes 1179648 | tf_op jit(solution)/shard_map/beams/pallas_call | solution.py:335
  161.7 0.0 all-to-all-done.3
  161.8 5.4 %all-to-all-start.5 = ((bf16[8,384,128]{2,1,0:T(8,128)(2,1)}), bf16[8,384,128]{2,1,0:T(8,128)(2,1)S(1)}, u32[]{:S(2)}, u32[]{:S(2)}) async-start(bf16[8,384,128]{2,1,0:T(8,128)(2,1)} %bitcast.39), calls=%async_computation.5 | async-start | bytes 1572864 | tf_op jit(solution)/shard_map/all_to_all | solution.py:441
  167.2 15.1 %beams.3 = bf16[8,1,24,8,128]{4,3,2,1,0:T(8,128)(2,1)} custom-call(f32[8,2,192,1536]{3,2,1,0:T(8,128)} %get-tuple-element.9.step_ref, f32[4,2,192,1536]{3,2,1,0:T(8,128)} %get-tuple-element.10.mid_ref, bf16[8,64,8,128]{3,2,1,0:T(8,128)(2,1)} %bitcast.22, bf16[8,32,16,128]{3,2,1,0:T(8,128)(2,1)} %bitcast.24), custom_call_target="tpu_custom_call" | custom-call | flops 4831838208 | bytes 1179648 | tf_op jit(solution)/shard_map/beams/pallas_call | solution.py:335
  182.3 4.1 %all-to-all-done.5 = bf16[8,384,128]{2,1,0:T(8,128)(2,1)S(1)} async-done(((bf16[8,384,128]{2,1,0:T(8,128)(2,1)}), bf16[8,384,128]{2,1,0:T(8,128)(2,1)S(1)}, u32[]{:S(2)}, u32[]{:S(2)}) %all-to-all-start.5) | async-done | bytes 786464 | tf_op jit(solution)/shard_map/all_to_all | solution.py:441
  186.3 3.6 %all-to-all-start.2 = ((bf16[8,192,128]{2,1,0:T(8,128)(2,1)}), bf16[8,192,128]{2,1,0:T(8,128)(2,1)S(1)}, u32[]{:S(2)}, u32[]{:S(2)}) async-start(bf16[8,192,128]{2,1,0:T(8,128)(2,1)} %bitcast.29), calls=%async_computation.2 | async-start | bytes 786432 | tf_op jit(solution)/shard_map/all_to_all | solution.py:441
  189.9 2.3 %collective-permute-start.4 = (bf16[8,2,24,8,128]{4,3,2,1,0:T(8,128)(2,1)S(1)}, bf16[8,2,24,8,128]{4,3,2,1,0:T(8,128)(2,1)S(1)}, u32[]{:S(2)}, u32[]{:S(2)}) collective-permute-start(bf16[8,2,24,8,128]{4,3,2,1,0:T(8,128)(2,1)S(1)} %bitcast.26), channel_id=1, source_target_pairs={{1,0},{2,1},{3,2},{5,4},{6,5},{7,6},{9,8},{10,9},{11,10},{13,12},{... | collective-permute-start | bytes 2359304 | tf_op jit(solution)/shard_map/ppermute | solution.py:33
  192.3 0.0 copy-done.2
  192.3 1.9 collective-permute-start.3
  194.2 6.9 %all-to-all-done.2 = bf16[8,192,128]{2,1,0:T(8,128)(2,1)S(1)} async-done(((bf16[8,192,128]{2,1,0:T(8,128)(2,1)}), bf16[8,192,128]{2,1,0:T(8,128)(2,1)S(1)}, u32[]{:S(2)}, u32[]{:S(2)}) %all-to-all-start.2) | async-done | bytes 393248 | tf_op jit(solution)/shard_map/all_to_all | solution.py:441
  201.1 3.3 %collective-permute-start.2 = (bf16[8,1,24,8,128]{4,3,2,1,0:T(8,128)(2,1)S(1)}, bf16[8,1,24,8,128]{4,3,2,1,0:T(8,128)(2,1)S(1)}, u32[]{:S(2)}, u32[]{:S(2)}) collective-permute-start(bf16[8,1,24,8,128]{4,3,2,1,0:T(8,128)(2,1)S(1)} %bitcast.33), channel_id=1, source_target_pairs={{1,0},{2,1},{3,2},{5,4},{6,5},{7,6},{9,8},{10,9},{11,10},{13,12},{... | collective-permute-start | bytes 1179656 | tf_op jit(solution)/shard_map/ppermute | solution.py:33
  204.4 0.0 collective-permute-done.4.next_ref
  204.4 0.0 copy-done.1
  204.4 0.0 copy-start.6
  204.4 0.9 copy-done.6
  205.4 7.3 %dedisperse.3.refs_0_ = f32[1536,512]{1,0:T(8,128)} custom-call(s32[4,512]{1,0:T(4,128)} %shifts_ref.5, bf16[8,2,24,8,128]{4,3,2,1,0:T(8,128)(2,1)} %bitcast.27, bf16[8,2,24,8,128]{4,3,2,1,0:T(8,128)(2,1)} %copy-done.6), custom_call_target="tpu_custom_call" | custom-call | flops 6291456 | bytes 3932160 | tf_op jit(solution)/shard_map/dedisperse/pallas_call | solution.py:419
  212.7 0.0 collective-permute-done.3.next_ref
  212.7 0.7 copy-done.7
  213.4 4.6 %dedisperse.4.refs_0_ = f32[1536,512]{1,0:T(8,128)} custom-call(s32[4,512]{1,0:T(4,128)} %shifts_ref.5, bf16[8,1,24,8,128]{4,3,2,1,0:T(8,128)(2,1)} %bitcast.32, bf16[8,1,24,8,128]{4,3,2,1,0:T(8,128)(2,1)} %copy-done.7, f32[1536,512]{1,0:T(8,128)} %dedisperse.3.refs_0_), custom_call_target="tpu_custom_call", output_to_operand_aliasing={{}: (3, {})} | custom-call | flops 3145728 | bytes 1966080 | tf_op jit(solution)/shard_map/dedisperse/pallas_call | solution.py:419
  218.0 0.0 copy-done.3
  218.0 0.0 collective-permute-done.2.next_ref
  218.0 0.7 copy-done.8
  218.8 4.6 %dedisperse.5 = f32[1536,512]{1,0:T(8,128)} custom-call(s32[4,512]{1,0:T(4,128)} %shifts_ref.5, bf16[8,1,24,8,128]{4,3,2,1,0:T(8,128)(2,1)} %bitcast.34, bf16[8,1,24,8,128]{4,3,2,1,0:T(8,128)(2,1)} %copy-done.8, f32[1536,512]{1,0:T(8,128)} %dedisperse.4.refs_0_), custom_call_target="tpu_custom_call", output_to_operand_aliasing={{}: (3, {})} | custom-call | flops 3145728 | bytes 1966080 | tf_op jit(solution)/shard_map/dedisperse/pallas_call | solution.py:419
  (7 shorter events, 0.0 us)
Async XLA Ops:
  1.0 9.2 %collective-permute-start = (bf16[2,8,12288]{2,1,0:T(8,128)(2,1)S(1)}, bf16[2,8,12288]{2,1,0:T(8,128)(2,1)S(1)}, u32[]{:S(2)}, u32[]{:S(2)}) collective-permute-start(bf16[2,8,12288]{2,1,0:T(8,128)(2,1)S(1)} %slice.14), channel_id=1, source_target_pairs={{0,1},{1,2},{2,3},{4,5},{5,6},{6,7},{8,9},{9,10},{10,11},{12,13},{... | collective-permute-start | bytes 1179656 | tf_op jit(solution)/shard_map/ppermute | solution.py:33
  10.2 0.7 copy-start.9
  23.9 42.9 %all-to-all-start = ((bf16[8,512,128]{2,1,0:T(8,128)(2,1)}), bf16[8,512,128]{2,1,0:T(8,128)(2,1)S(1)}, u32[]{:S(2)}, u32[]{:S(2)}) async-start(bf16[8,512,128]{2,1,0:T(8,128)(2,1)} %bitcast.25), calls=%async_computation | async-start | bytes 2097152 | tf_op jit(solution)/shard_map/all_to_all | solution.py:441
  30.6 13.6 %collective-permute-start.1 = (bf16[2,16,12288]{2,1,0:T(8,128)(2,1)S(1)}, bf16[2,16,12288]{2,1,0:T(8,128)(2,1)S(1)}, u32[]{:S(2)}, u32[]{:S(2)}) collective-permute-start(bf16[2,16,12288]{2,1,0:T(8,128)(2,1)S(1)} %slice.15), channel_id=1, source_target_pairs={{0,1},{1,2},{2,3},{4,5},{5,6},{6,7},{8,9},{9,10},{10,11},{12,13},{... | collective-permute-start | bytes 2359304 | tf_op jit(solution)/shard_map/ppermute | solution.py:33
  44.2 0.9 copy-start.5
  66.8 27.5 %copy-start.4 = (s32[192,1536]{1,0:T(8,128)S(1)}, s32[192,1536]{1,0:T(8,128)}, u32[]{:S(2)}) copy-start(s32[192,1536]{1,0:T(8,128)} %param.10) | copy-start | bytes 3538948
  66.8 27.6 %copy-start = (bf16[8,512,128]{2,1,0:T(8,128)(2,1)}, bf16[8,512,128]{2,1,0:T(8,128)(2,1)S(1)}, u32[]{:S(2)}) copy-start(bf16[8,512,128]{2,1,0:T(8,128)(2,1)S(1)} %all-to-all-done) | copy-start | bytes 3145732
  90.0 38.2 %all-to-all-start.4 = ((bf16[8,512,128]{2,1,0:T(8,128)(2,1)}), bf16[8,512,128]{2,1,0:T(8,128)(2,1)}, u32[]{:S(2)}, u32[]{:S(2)}) async-start(bf16[8,512,128]{2,1,0:T(8,128)(2,1)} %bitcast.37), calls=%async_computation.4 | async-start | bytes 2097152 | tf_op jit(solution)/shard_map/all_to_all | solution.py:441
  128.1 33.6 %all-to-all-start.3 = ((bf16[8,192,128]{2,1,0:T(8,128)(2,1)}), bf16[8,192,128]{2,1,0:T(8,128)(2,1)S(1)}, u32[]{:S(2)}, u32[]{:S(2)}) async-start(bf16[8,192,128]{2,1,0:T(8,128)(2,1)} %bitcast.30), calls=%async_computation.3 | async-start | bytes 786432 | tf_op jit(solution)/shard_map/all_to_all | solution.py:441
  161.8 30.6 %copy-start.2 = (bf16[8,192,128]{2,1,0:T(8,128)(2,1)}, bf16[8,192,128]{2,1,0:T(8,128)(2,1)S(1)}, u32[]{:S(2)}) copy-start(bf16[8,192,128]{2,1,0:T(8,128)(2,1)S(1)} %all-to-all-done.3) | copy-start | bytes 1179652
  161.8 24.6 %all-to-all-start.5 = ((bf16[8,384,128]{2,1,0:T(8,128)(2,1)}), bf16[8,384,128]{2,1,0:T(8,128)(2,1)S(1)}, u32[]{:S(2)}, u32[]{:S(2)}) async-start(bf16[8,384,128]{2,1,0:T(8,128)(2,1)} %bitcast.39), calls=%async_computation.5 | async-start | bytes 1572864 | tf_op jit(solution)/shard_map/all_to_all | solution.py:441
  186.3 18.1 %copy-start.1 = (bf16[8,384,128]{2,1,0:T(8,128)(2,1)}, bf16[8,384,128]{2,1,0:T(8,128)(2,1)S(1)}, u32[]{:S(2)}) copy-start(bf16[8,384,128]{2,1,0:T(8,128)(2,1)S(1)} %all-to-all-done.5) | copy-start | bytes 2359300
  186.3 14.8 %all-to-all-start.2 = ((bf16[8,192,128]{2,1,0:T(8,128)(2,1)}), bf16[8,192,128]{2,1,0:T(8,128)(2,1)S(1)}, u32[]{:S(2)}, u32[]{:S(2)}) async-start(bf16[8,192,128]{2,1,0:T(8,128)(2,1)} %bitcast.29), calls=%async_computation.2 | async-start | bytes 786432 | tf_op jit(solution)/shard_map/all_to_all | solution.py:441
  189.9 14.5 %collective-permute-start.4 = (bf16[8,2,24,8,128]{4,3,2,1,0:T(8,128)(2,1)S(1)}, bf16[8,2,24,8,128]{4,3,2,1,0:T(8,128)(2,1)S(1)}, u32[]{:S(2)}, u32[]{:S(2)}) collective-permute-start(bf16[8,2,24,8,128]{4,3,2,1,0:T(8,128)(2,1)S(1)} %bitcast.26), channel_id=1, source_target_pairs={{1,0},{2,1},{3,2},{5,4},{6,5},{7,6},{9,8},{10,9},{11,10},{13,12},{... | collective-permute-start | bytes 2359304 | tf_op jit(solution)/shard_map/ppermute | solution.py:33
  192.3 20.4 %collective-permute-start.3 = (bf16[8,1,24,8,128]{4,3,2,1,0:T(8,128)(2,1)S(1)}, bf16[8,1,24,8,128]{4,3,2,1,0:T(8,128)(2,1)S(1)}, u32[]{:S(2)}, u32[]{:S(2)}) collective-permute-start(bf16[8,1,24,8,128]{4,3,2,1,0:T(8,128)(2,1)S(1)} %bitcast.31), channel_id=1, source_target_pairs={{1,0},{2,1},{3,2},{5,4},{6,5},{7,6},{9,8},{10,9},{11,10},{13,12},{... | collective-permute-start | bytes 1179656 | tf_op jit(solution)/shard_map/ppermute | solution.py:33
  201.1 16.9 %copy-start.3 = (bf16[8,192,128]{2,1,0:T(8,128)(2,1)}, bf16[8,192,128]{2,1,0:T(8,128)(2,1)S(1)}, u32[]{:S(2)}) copy-start(bf16[8,192,128]{2,1,0:T(8,128)(2,1)S(1)} %all-to-all-done.2) | copy-start | bytes 1179652
  201.1 16.9 %collective-permute-start.2 = (bf16[8,1,24,8,128]{4,3,2,1,0:T(8,128)(2,1)S(1)}, bf16[8,1,24,8,128]{4,3,2,1,0:T(8,128)(2,1)S(1)}, u32[]{:S(2)}, u32[]{:S(2)}) collective-permute-start(bf16[8,1,24,8,128]{4,3,2,1,0:T(8,128)(2,1)S(1)} %bitcast.33), channel_id=1, source_target_pairs={{1,0},{2,1},{3,2},{5,4},{6,5},{7,6},{9,8},{10,9},{11,10},{13,12},{... | collective-permute-start | bytes 1179656 | tf_op jit(solution)/shard_map/ppermute | solution.py:33
  204.4 0.9 copy-start.6
  212.7 0.7 copy-start.7
  218.0 0.8 copy-start.8

commit v3 on v2

--- a/solution.py
+++ b/solution.py
@@ -245,31 +245,32 @@
         twice = 2.0 * (ch * ch - sh * sh)
         before, now = (ch, -sh), (ch, sh)
         for j in range(pairs):
-            step_ref[j, 0], step_ref[j, 1] = now
+            step_ref[j, 0] = now[0].astype(jnp.bfloat16)
+            step_ref[j, 1] = now[1].astype(jnp.bfloat16)
             before, now = now, (twice * now[0] - before[0], twice * now[1] - before[1])
         for a in range(groups):
             c, s = turn_of(delays_ref[...] * (2 * (first_ref[0] + owners * GROUP * a) + GROUP - 1))
-            mid_ref[a, 0] = c * (1.0 / math.sqrt(stations))
-            mid_ref[a, 1] = s * (1.0 / math.sqrt(stations))
+            mid_ref[a, 0] = (c * (1.0 / math.sqrt(stations))).astype(jnp.bfloat16)
+            mid_ref[a, 1] = (s * (1.0 / math.sqrt(stations))).astype(jnp.bfloat16)
 
     return pl.pallas_call(
         kernel,
-        grid=(stations // ROWS,),
+        grid=(stations // (2 * ROWS),),
         in_specs=[
             pl.BlockSpec(memory_space=pltpu.SMEM),
-            pl.BlockSpec((ROWS, beams), lambda i: (i, 0)),
+            pl.BlockSpec((2 * ROWS, beams), lambda i: (i, 0)),
         ],
         out_specs=[
-            pl.BlockSpec((pairs, 2, ROWS, beams), lambda i: (0, 0, i, 0)),
-            pl.BlockSpec((groups, 2, ROWS, beams), lambda i: (0, 0, i, 0)),
+            pl.BlockSpec((pairs, 2, 2 * ROWS, beams), lambda i: (0, 0, i, 0)),
+            pl.BlockSpec((groups, 2, 2 * ROWS, beams), lambda i: (0, 0, i, 0)),
         ],
         out_shape=[
-            jax.ShapeDtypeStruct((pairs, 2, stations, beams), jnp.float32),
-            jax.ShapeDtypeStruct((groups, 2, stations, beams), jnp.float32),
+            jax.ShapeDtypeStruct((pairs, 2, stations, beams), jnp.bfloat16),
+            jax.ShapeDtypeStruct((groups, 2, stations, beams), jnp.bfloat16),
         ],
         compiler_params=pltpu.CompilerParams(vmem_limit_bytes=VMEM_LIMIT),
         cost_estimate=pl.CostEstimate(
-            flops=200 * stations * beams, bytes_accessed=8 * (pairs + groups) * stations * beams, transcendentals=0
+            flops=200 * stations * beams, bytes_accessed=4 * (pairs + groups) * stations * beams, transcendentals=0
         ),
         name="turns",
     )(first, delays)
@@ -294,7 +295,7 @@
 
     @pl.when(j == 0)
     def _():
-        lax.fori_loop(0, GROUP, lay, 0)
+        lax.fori_loop(0, GROUP, lay, 0, unroll=4)
 
     def one(k, cos, sin):
         out = jnp.dot(left[k, 0], cos.astype(jnp.bfloat16), preferred_element_type=jnp.float32)

time: 226 us -> 207 us (0.916)
  Pallas kernels: 127 us -> 105 us
  waiting for transfers between devices: 24.6 us -> 29.1 us
    pallas_call x3, Pallas kernels: 58.4 us -> 40.4 us  [beams_of(): pl.pallas_call(beam_kernel, grid=(count, pairs), in_specs=[pl.BlockSpec((...]
    all_to_all x5, waiting for transfers between devices: 10.9 us -> 15.4 us  [swapped(): lax.all_to_all(x.reshape(owners, -1, LANES), 'grp', split_axis=0, concat_...]
    pallas_call x1, Pallas kernels: 17.6 us -> 13.4 us  [turns(): pl.pallas_call(kernel, grid=(stations // (2 * ROWS),), in_specs=[pl.Block...]
  transfers between devices with their start and end apart: 10 -> 10, of which waited for: 4 -> 4; matrix products, arithmetic and copies ran while one was open for 1% -> 1% of each run, Pallas kernels for 49% -> 42%
where the time goes in v3:
time: 207 us; the launch traced here: 206 us
  Pallas kernels  105 us (51%)
  starting transfers between devices  40.9 us (20%)
  waiting for transfers between devices  29.1 us (14%)
  blocking collectives  23.2 us (11%)
  local copies, waits for them, and re-layouts  6.38 us (3%)
    pallas_call x3, Pallas kernels, beams_of(): pl.pallas_call(beam_kernel, grid=(count, pairs), in_specs=[pl.BlockSpec((...  40.4 us
    pallas_call x2, Pallas kernels, channelize(): pl.pallas_call(functools.partial(channel_kernel, frames), grid=(stations...  34.5 us
    all_to_all x5, starting transfers between devices, swapped(): lax.all_to_all(x.reshape(owners, -1, LANES), 'grp', split_axis=0, concat_...  24.2 us
    all_to_all x1, blocking collectives, swapped(): lax.all_to_all(x.reshape(owners, -1, LANES), 'grp', split_axis=0, concat_...  23.2 us
    ppermute x5, starting transfers between devices, shift_along(): return lax.ppermute(x, axis, pairs)  16.7 us
    pallas_call x3, Pallas kernels, dedisperse(): pl.pallas_call(functools.partial(tree_kernel, first_slot, beams), grid=(g...  16.5 us
    all_to_all x5, waiting for transfers between devices, swapped(): lax.all_to_all(x.reshape(owners, -1, LANES), 'grp', split_axis=0, concat_...  15.4 us
    ppermute x5, waiting for transfers between devices, shift_along(): return lax.ppermute(x, axis, pairs)  13.6 us
  transfers between devices with their start and end apart: 10, of which 4 were waited for; matrix products, arithmetic and copies ran while one was open for 1% of the time, Pallas kernels for 42%

profile of v3, /device:TPU:1, one launch (start us, length us, event | category | flops | bytes accessed | tf_op | source)
XLA Modules:
  0.0 205.6 jit_solution(8058134400037737138)
XLA Ops:
  0.0 1.0 slice.14
  1.0 4.5 %collective-permute-start = (bf16[2,8,12288]{2,1,0:T(8,128)(2,1)S(1)}, bf16[2,8,12288]{2,1,0:T(8,128)(2,1)S(1)}, u32[]{:S(2)}, u32[]{:S(2)}) collective-permute-start(bf16[2,8,12288]{2,1,0:T(8,128)(2,1)S(1)} %slice.14), channel_id=1, source_target_pairs={{0,1},{1,2},{2,3},{4,5},{5,6},{6,7},{8,9},{9,10},{10,11},{12,13},{... | collective-permute-start | bytes 1179656 | tf_op jit(solution)/shard_map/ppermute | solution.py:33
  5.5 4.7 %collective-permute-done.halo_ref = bf16[2,8,12288]{2,1,0:T(8,128)(2,1)S(1)} collective-permute-done((bf16[2,8,12288]{2,1,0:T(8,128)(2,1)S(1)}, bf16[2,8,12288]{2,1,0:T(8,128)(2,1)S(1)}, u32[]{:S(2)}, u32[]{:S(2)}) %collective-permute-start) | collective-permute-done | bytes 393248 | tf_op jit(solution)/shard_map/ppermute | solution.py:33
  10.2 0.0 copy-start.9
  10.2 0.7 copy-done.9
  11.0 12.9 %channelize.2 = bf16[8,4,4,4,8,128]{5,4,3,2,1,0:T(8,128)(2,1)} custom-call(bf16[2,24,262144]{2,1,0:T(8,128)(2,1)} %x_ref.3, bf16[2,8,12288]{2,1,0:T(8,128)(2,1)} %copy-done.9, f32[4,4096]{1,0:T(4,128)} %taps_ref.3, f32[4,2,8,128]{3,2,1,0:T(8,128)} %constant.12.clone.fine_ref, f32[4,2,128,128]{3,2,1,0:T(8,128)} %constant.13.clone.coarse_ref), custom_call_target="tpu_custom_call" | custom-call | flops 2147483648 | bytes 8388608 | tf_op jit(solution)/shard_map/channelize/pallas_call | solution.py:183
  23.9 5.6 %all-to-all-start = ((bf16[8,512,128]{2,1,0:T(8,128)(2,1)}), bf16[8,512,128]{2,1,0:T(8,128)(2,1)S(1)}, u32[]{:S(2)}, u32[]{:S(2)}) async-start(bf16[8,512,128]{2,1,0:T(8,128)(2,1)} %bitcast.20), calls=%async_computation | async-start | bytes 2097152 | tf_op jit(solution)/shard_map/all_to_all | solution.py:442
  29.4 1.2 slice.15
  30.6 4.7 %collective-permute-start.1 = (bf16[2,16,12288]{2,1,0:T(8,128)(2,1)S(1)}, bf16[2,16,12288]{2,1,0:T(8,128)(2,1)S(1)}, u32[]{:S(2)}, u32[]{:S(2)}) collective-permute-start(bf16[2,16,12288]{2,1,0:T(8,128)(2,1)S(1)} %slice.15), channel_id=1, source_target_pairs={{0,1},{1,2},{2,3},{4,5},{5,6},{6,7},{8,9},{9,10},{10,11},{12,13},{... | collective-permute-start | bytes 2359304 | tf_op jit(solution)/shard_map/ppermute | solution.py:33
  35.3 8.9 %collective-permute-done.1.halo_ref = bf16[2,16,12288]{2,1,0:T(8,128)(2,1)S(1)} collective-permute-done((bf16[2,16,12288]{2,1,0:T(8,128)(2,1)S(1)}, bf16[2,16,12288]{2,1,0:T(8,128)(2,1)S(1)}, u32[]{:S(2)}, u32[]{:S(2)}) %collective-permute-start.1) | collective-permute-done | bytes 786464 | tf_op jit(solution)/shard_map/ppermute | solution.py:33
  44.2 0.0 copy-start.5
  44.2 0.9 copy-done.5
  45.1 21.6 %channelize.3 = (bf16[8,2,4,4,16,128]{5,4,3,2,1,0:T(8,128)(2,1)}, bf16[8,2,4,4,16,128]{5,4,3,2,1,0:T(8,128)(2,1)}) custom-call(bf16[2,24,262144]{2,1,0:T(8,128)(2,1)} %x_ref.3, bf16[2,16,12288]{2,1,0:T(8,128)(2,1)} %copy-done.5, f32[4,4096]{1,0:T(4,128)} %taps_ref.3, f32[4,2,8,128]{3,2,1,0:T(8,128)} %constant.12.clone.fine_ref, ...), custom_call_target="tpu_custom_call" | custom-call | flops 4294967296 | bytes 16777216 | tf_op jit(solution)/shard_map/channelize/pallas_call | solution.py:183
  66.7 0.0 all-to-all-done
  66.7 0.0 copy-start.4
  66.7 23.2 %all_to_all.30 = bf16[8,512,128]{2,1,0:T(8,128)(2,1)} all-to-all(bf16[8,512,128]{2,1,0:T(8,128)(2,1)} %bitcast.36), channel_id=1, replica_groups=mesh['grp'=8,'tm'=4] {'grp'}, dimensions={0} | all-to-all | bytes 2097152 | tf_op jit(solution)/shard_map/all_to_all | solution.py:442
  89.9 4.3 %all-to-all-start.4 = ((bf16[8,512,128]{2,1,0:T(8,128)(2,1)}), bf16[8,512,128]{2,1,0:T(8,128)(2,1)}, u32[]{:S(2)}, u32[]{:S(2)}) async-start(bf16[8,512,128]{2,1,0:T(8,128)(2,1)} %bitcast.35), calls=%async_computation.4 | async-start | bytes 2097152 | tf_op jit(solution)/shard_map/all_to_all | solution.py:442
  94.1 0.0 copy-done.3
  94.1 0.1 slice.17
  94.2 0.0 copy-done.4
  94.3 1.1 pad_add_fusion.delays_ref
  95.3 13.4 %turns.1 = (bf16[8,2,192,1536]{3,2,1,0:T(8,128)(2,1)}, bf16[4,2,192,1536]{3,2,1,0:T(8,128)(2,1)}) custom-call(s32[1]{0:T(128)} %bitcast.first_ref, s32[192,1536]{1,0:T(8,128)} %pad_add_fusion.delays_ref), custom_call_target="tpu_custom_call" | custom-call | flops 58982400 | bytes 14155776 | tf_op jit(solution)/shard_map/turns/pallas_call | solution.py:256
  108.7 10.5 %beams.4 = bf16[8,1,24,8,128]{4,3,2,1,0:T(8,128)(2,1)} custom-call(bf16[8,2,192,1536]{3,2,1,0:T(8,128)(2,1)} %get-tuple-element.9.step_ref, bf16[4,2,192,1536]{3,2,1,0:T(8,128)(2,1)} %get-tuple-element.10.mid_ref, bf16[8,64,8,128]{3,2,1,0:T(8,128)(2,1)} %bitcast.30, bf16[8,32,16,128]{3,2,1,0:T(8,128)(2,1)} %bitcast.33), custom_call_target="tpu_custom_call" | custom-call | flops 4831838208 | bytes 1179648 | tf_op jit(solution)/shard_map/beams/pallas_call | solution.py:336
  119.3 0.0 all-to-all-done.4
  119.3 5.3 %all-to-all-start.3 = ((bf16[8,192,128]{2,1,0:T(8,128)(2,1)}), bf16[8,192,128]{2,1,0:T(8,128)(2,1)S(1)}, u32[]{:S(2)}, u32[]{:S(2)}) async-start(bf16[8,192,128]{2,1,0:T(8,128)(2,1)} %bitcast.39), calls=%async_computation.3 | async-start | bytes 786432 | tf_op jit(solution)/shard_map/all_to_all | solution.py:442
  124.6 19.4 %beams.5 = bf16[8,2,24,8,128]{4,3,2,1,0:T(8,128)(2,1)} custom-call(bf16[8,2,192,1536]{3,2,1,0:T(8,128)(2,1)} %get-tuple-element.9.step_ref, bf16[4,2,192,1536]{3,2,1,0:T(8,128)(2,1)} %get-tuple-element.10.mid_ref, bf16[8,64,8,128]{3,2,1,0:T(8,128)(2,1)} %bitcast.31, bf16[8,32,16,128]{3,2,1,0:T(8,128)(2,1)} %bitcast.13.refs_1_), custom_call_target="tpu_custom_call" | custom-call | flops 9663676416 | bytes 1179648 | tf_op jit(solution)/shard_map/beams/pallas_call | solution.py:336
  144.0 0.0 all-to-all-done.3
  144.0 5.4 %all-to-all-start.5 = ((bf16[8,384,128]{2,1,0:T(8,128)(2,1)}), bf16[8,384,128]{2,1,0:T(8,128)(2,1)S(1)}, u32[]{:S(2)}, u32[]{:S(2)}) async-start(bf16[8,384,128]{2,1,0:T(8,128)(2,1)} %bitcast.37), calls=%async_computation.5 | async-start | bytes 1572864 | tf_op jit(solution)/shard_map/all_to_all | solution.py:442
  149.4 10.6 %beams.3 = bf16[8,1,24,8,128]{4,3,2,1,0:T(8,128)(2,1)} custom-call(bf16[8,2,192,1536]{3,2,1,0:T(8,128)(2,1)} %get-tuple-element.9.step_ref, bf16[4,2,192,1536]{3,2,1,0:T(8,128)(2,1)} %get-tuple-element.10.mid_ref, bf16[8,64,8,128]{3,2,1,0:T(8,128)(2,1)} %bitcast.32, bf16[8,32,16,128]{3,2,1,0:T(8,128)(2,1)} %bitcast.34), custom_call_target="tpu_custom_call" | custom-call | flops 4831838208 | bytes 1179648 | tf_op jit(solution)/shard_map/beams/pallas_call | solution.py:336
  159.9 8.6 %all-to-all-done.5 = bf16[8,384,128]{2,1,0:T(8,128)(2,1)S(1)} async-done(((bf16[8,384,128]{2,1,0:T(8,128)(2,1)}), bf16[8,384,128]{2,1,0:T(8,128)(2,1)S(1)}, u32[]{:S(2)}, u32[]{:S(2)}) %all-to-all-start.5) | async-done | bytes 786464 | tf_op jit(solution)/shard_map/all_to_all | solution.py:442
  168.5 3.6 %all-to-all-start.2 = ((bf16[8,192,128]{2,1,0:T(8,128)(2,1)}), bf16[8,192,128]{2,1,0:T(8,128)(2,1)S(1)}, u32[]{:S(2)}, u32[]{:S(2)}) async-start(bf16[8,192,128]{2,1,0:T(8,128)(2,1)} %bitcast.38), calls=%async_computation.2 | async-start | bytes 786432 | tf_op jit(solution)/shard_map/all_to_all | solution.py:442
  172.2 2.3 %collective-permute-start.4 = (bf16[8,2,24,8,128]{4,3,2,1,0:T(8,128)(2,1)S(1)}, bf16[8,2,24,8,128]{4,3,2,1,0:T(8,128)(2,1)S(1)}, u32[]{:S(2)}, u32[]{:S(2)}) collective-permute-start(bf16[8,2,24,8,128]{4,3,2,1,0:T(8,128)(2,1)S(1)} %bitcast.21), channel_id=1, source_target_pairs={{1,0},{2,1},{3,2},{5,4},{6,5},{7,6},{9,8},{10,9},{11,10},{13,12},{... | collective-permute-start | bytes 2359304 | tf_op jit(solution)/shard_map/ppermute | solution.py:33
  174.5 0.0 copy-done.1
  174.5 1.9 collective-permute-start.3
  176.4 6.9 %all-to-all-done.2 = bf16[8,192,128]{2,1,0:T(8,128)(2,1)S(1)} async-done(((bf16[8,192,128]{2,1,0:T(8,128)(2,1)}), bf16[8,192,128]{2,1,0:T(8,128)(2,1)S(1)}, u32[]{:S(2)}, u32[]{:S(2)}) %all-to-all-start.2) | async-done | bytes 393248 | tf_op jit(solution)/shard_map/all_to_all | solution.py:442
  183.3 3.3 %collective-permute-start.2 = (bf16[8,1,24,8,128]{4,3,2,1,0:T(8,128)(2,1)S(1)}, bf16[8,1,24,8,128]{4,3,2,1,0:T(8,128)(2,1)S(1)}, u32[]{:S(2)}, u32[]{:S(2)}) collective-permute-start(bf16[8,1,24,8,128]{4,3,2,1,0:T(8,128)(2,1)S(1)} %bitcast.26), channel_id=1, source_target_pairs={{1,0},{2,1},{3,2},{5,4},{6,5},{7,6},{9,8},{10,9},{11,10},{13,12},{... | collective-permute-start | bytes 1179656 | tf_op jit(solution)/shard_map/ppermute | solution.py:33
  186.6 0.0 collective-permute-done.4.next_ref
  186.6 0.0 copy-done
  186.6 0.0 copy-start.6
  186.6 0.9 copy-done.6
  187.6 7.3 %dedisperse.3.refs_0_ = f32[1536,512]{1,0:T(8,128)} custom-call(s32[4,512]{1,0:T(4,128)} %shifts_ref.5, bf16[8,2,24,8,128]{4,3,2,1,0:T(8,128)(2,1)} %bitcast.22, bf16[8,2,24,8,128]{4,3,2,1,0:T(8,128)(2,1)} %copy-done.6), custom_call_target="tpu_custom_call" | custom-call | flops 6291456 | bytes 3932160 | tf_op jit(solution)/shard_map/dedisperse/pallas_call | solution.py:420
  194.9 0.0 collective-permute-done.3.next_ref
  194.9 0.7 copy-done.7
  195.6 4.6 %dedisperse.4.refs_0_ = f32[1536,512]{1,0:T(8,128)} custom-call(s32[4,512]{1,0:T(4,128)} %shifts_ref.5, bf16[8,1,24,8,128]{4,3,2,1,0:T(8,128)(2,1)} %bitcast.25, bf16[8,1,24,8,128]{4,3,2,1,0:T(8,128)(2,1)} %copy-done.7, f32[1536,512]{1,0:T(8,128)} %dedisperse.3.refs_0_), custom_call_target="tpu_custom_call", output_to_operand_aliasing={{}: (3, {})} | custom-call | flops 3145728 | bytes 1966080 | tf_op jit(solution)/shard_map/dedisperse/pallas_call | solution.py:420
  200.2 0.0 copy-done.2
  200.2 0.0 collective-permute-done.2.next_ref
  200.2 0.7 copy-done.8
  201.0 4.6 %dedisperse.5 = f32[1536,512]{1,0:T(8,128)} custom-call(s32[4,512]{1,0:T(4,128)} %shifts_ref.5, bf16[8,1,24,8,128]{4,3,2,1,0:T(8,128)(2,1)} %bitcast.27, bf16[8,1,24,8,128]{4,3,2,1,0:T(8,128)(2,1)} %copy-done.8, f32[1536,512]{1,0:T(8,128)} %dedisperse.4.refs_0_), custom_call_target="tpu_custom_call", output_to_operand_aliasing={{}: (3, {})} | custom-call | flops 3145728 | bytes 1966080 | tf_op jit(solution)/shard_map/dedisperse/pallas_call | solution.py:420
  (7 shorter events, 0.0 us)
Async XLA Ops:
  1.0 9.2 %collective-permute-start = (bf16[2,8,12288]{2,1,0:T(8,128)(2,1)S(1)}, bf16[2,8,12288]{2,1,0:T(8,128)(2,1)S(1)}, u32[]{:S(2)}, u32[]{:S(2)}) collective-permute-start(bf16[2,8,12288]{2,1,0:T(8,128)(2,1)S(1)} %slice.14), channel_id=1, source_target_pairs={{0,1},{1,2},{2,3},{4,5},{5,6},{6,7},{8,9},{9,10},{10,11},{12,13},{... | collective-permute-start | bytes 1179656 | tf_op jit(solution)/shard_map/ppermute | solution.py:33
  10.2 0.7 copy-start.9
  23.9 42.8 %all-to-all-start = ((bf16[8,512,128]{2,1,0:T(8,128)(2,1)}), bf16[8,512,128]{2,1,0:T(8,128)(2,1)S(1)}, u32[]{:S(2)}, u32[]{:S(2)}) async-start(bf16[8,512,128]{2,1,0:T(8,128)(2,1)} %bitcast.20), calls=%async_computation | async-start | bytes 2097152 | tf_op jit(solution)/shard_map/all_to_all | solution.py:442
  30.6 13.6 %collective-permute-start.1 = (bf16[2,16,12288]{2,1,0:T(8,128)(2,1)S(1)}, bf16[2,16,12288]{2,1,0:T(8,128)(2,1)S(1)}, u32[]{:S(2)}, u32[]{:S(2)}) collective-permute-start(bf16[2,16,12288]{2,1,0:T(8,128)(2,1)S(1)} %slice.15), channel_id=1, source_target_pairs={{0,1},{1,2},{2,3},{4,5},{5,6},{6,7},{8,9},{9,10},{10,11},{12,13},{... | collective-permute-start | bytes 2359304 | tf_op jit(solution)/shard_map/ppermute | solution.py:33
  44.2 0.9 copy-start.5
  66.7 27.5 %copy-start.3 = (s32[192,1536]{1,0:T(8,128)S(1)}, s32[192,1536]{1,0:T(8,128)}, u32[]{:S(2)}) copy-start(s32[192,1536]{1,0:T(8,128)} %param.10) | copy-start | bytes 3538948
  66.7 27.6 %copy-start.4 = (bf16[8,512,128]{2,1,0:T(8,128)(2,1)}, bf16[8,512,128]{2,1,0:T(8,128)(2,1)S(1)}, u32[]{:S(2)}) copy-start(bf16[8,512,128]{2,1,0:T(8,128)(2,1)S(1)} %all-to-all-done) | copy-start | bytes 3145732
  89.9 29.4 %all-to-all-start.4 = ((bf16[8,512,128]{2,1,0:T(8,128)(2,1)}), bf16[8,512,128]{2,1,0:T(8,128)(2,1)}, u32[]{:S(2)}, u32[]{:S(2)}) async-start(bf16[8,512,128]{2,1,0:T(8,128)(2,1)} %bitcast.35), calls=%async_computation.4 | async-start | bytes 2097152 | tf_op jit(solution)/shard_map/all_to_all | solution.py:442
  119.3 24.7 %all-to-all-start.3 = ((bf16[8,192,128]{2,1,0:T(8,128)(2,1)}), bf16[8,192,128]{2,1,0:T(8,128)(2,1)S(1)}, u32[]{:S(2)}, u32[]{:S(2)}) async-start(bf16[8,192,128]{2,1,0:T(8,128)(2,1)} %bitcast.39), calls=%async_computation.3 | async-start | bytes 786432 | tf_op jit(solution)/shard_map/all_to_all | solution.py:442
  144.0 30.6 %copy-start.1 = (bf16[8,192,128]{2,1,0:T(8,128)(2,1)}, bf16[8,192,128]{2,1,0:T(8,128)(2,1)S(1)}, u32[]{:S(2)}) copy-start(bf16[8,192,128]{2,1,0:T(8,128)(2,1)S(1)} %all-to-all-done.3) | copy-start | bytes 1179652
  144.0 24.6 %all-to-all-start.5 = ((bf16[8,384,128]{2,1,0:T(8,128)(2,1)}), bf16[8,384,128]{2,1,0:T(8,128)(2,1)S(1)}, u32[]{:S(2)}, u32[]{:S(2)}) async-start(bf16[8,384,128]{2,1,0:T(8,128)(2,1)} %bitcast.37), calls=%async_computation.5 | async-start | bytes 1572864 | tf_op jit(solution)/shard_map/all_to_all | solution.py:442
  168.5 18.1 %copy-start = (bf16[8,384,128]{2,1,0:T(8,128)(2,1)}, bf16[8,384,128]{2,1,0:T(8,128)(2,1)S(1)}, u32[]{:S(2)}) copy-start(bf16[8,384,128]{2,1,0:T(8,128)(2,1)S(1)} %all-to-all-done.5) | copy-start | bytes 2359300
  168.5 14.8 %all-to-all-start.2 = ((bf16[8,192,128]{2,1,0:T(8,128)(2,1)}), bf16[8,192,128]{2,1,0:T(8,128)(2,1)S(1)}, u32[]{:S(2)}, u32[]{:S(2)}) async-start(bf16[8,192,128]{2,1,0:T(8,128)(2,1)} %bitcast.38), calls=%async_computation.2 | async-start | bytes 786432 | tf_op jit(solution)/shard_map/all_to_all | solution.py:442
  172.2 14.5 %collective-permute-start.4 = (bf16[8,2,24,8,128]{4,3,2,1,0:T(8,128)(2,1)S(1)}, bf16[8,2,24,8,128]{4,3,2,1,0:T(8,128)(2,1)S(1)}, u32[]{:S(2)}, u32[]{:S(2)}) collective-permute-start(bf16[8,2,24,8,128]{4,3,2,1,0:T(8,128)(2,1)S(1)} %bitcast.21), channel_id=1, source_target_pairs={{1,0},{2,1},{3,2},{5,4},{6,5},{7,6},{9,8},{10,9},{11,10},{13,12},{... | collective-permute-start | bytes 2359304 | tf_op jit(solution)/shard_map/ppermute | solution.py:33
  174.5 20.4 %collective-permute-start.3 = (bf16[8,1,24,8,128]{4,3,2,1,0:T(8,128)(2,1)S(1)}, bf16[8,1,24,8,128]{4,3,2,1,0:T(8,128)(2,1)S(1)}, u32[]{:S(2)}, u32[]{:S(2)}) collective-permute-start(bf16[8,1,24,8,128]{4,3,2,1,0:T(8,128)(2,1)S(1)} %bitcast.24), channel_id=1, source_target_pairs={{1,0},{2,1},{3,2},{5,4},{6,5},{7,6},{9,8},{10,9},{11,10},{13,12},{... | collective-permute-start | bytes 1179656 | tf_op jit(solution)/shard_map/ppermute | solution.py:33
  183.3 16.9 %copy-start.2 = (bf16[8,192,128]{2,1,0:T(8,128)(2,1)}, bf16[8,192,128]{2,1,0:T(8,128)(2,1)S(1)}, u32[]{:S(2)}) copy-start(bf16[8,192,128]{2,1,0:T(8,128)(2,1)S(1)} %all-to-all-done.2) | copy-start | bytes 1179652
  183.3 16.9 %collective-permute-start.2 = (bf16[8,1,24,8,128]{4,3,2,1,0:T(8,128)(2,1)S(1)}, bf16[8,1,24,8,128]{4,3,2,1,0:T(8,128)(2,1)S(1)}, u32[]{:S(2)}, u32[]{:S(2)}) collective-permute-start(bf16[8,1,24,8,128]{4,3,2,1,0:T(8,128)(2,1)S(1)} %bitcast.26), channel_id=1, source_target_pairs={{1,0},{2,1},{3,2},{5,4},{6,5},{7,6},{9,8},{10,9},{11,10},{13,12},{... | collective-permute-start | bytes 1179656 | tf_op jit(solution)/shard_map/ppermute | solution.py:33
  186.6 0.9 copy-start.6
  194.9 0.7 copy-start.7
  200.2 0.8 copy-start.8

commit v4 on v3

--- a/solution.py
+++ b/solution.py
@@ -24,7 +24,7 @@
 ROWS = 8
 STEPS = 2
 GROUP = 2**LEVELS
-VMEM_LIMIT = 60 * 1024 * 1024
+MIB = 1024 * 1024
 
 
 def shift_along(x, axis, by):
@@ -204,7 +204,7 @@
             pltpu.VMEM((TAPS, ROWS, TRANSFORM), jnp.bfloat16),
             pltpu.VMEM((2, block, (TAPS - 1) * TRANSFORM), jnp.bfloat16),
         ],
-        compiler_params=pltpu.CompilerParams(vmem_limit_bytes=VMEM_LIMIT),
+        compiler_params=pltpu.CompilerParams(vmem_limit_bytes=40 * MIB),
         cost_estimate=pl.CostEstimate(
             flops=stations * frames * 8 * SUB * CHANNELS, bytes_accessed=stations * 4 * voltages.shape[2], transcendentals=0
         ),
@@ -268,7 +268,7 @@
             jax.ShapeDtypeStruct((pairs, 2, stations, beams), jnp.bfloat16),
             jax.ShapeDtypeStruct((groups, 2, stations, beams), jnp.bfloat16),
         ],
-        compiler_params=pltpu.CompilerParams(vmem_limit_bytes=VMEM_LIMIT),
+        compiler_params=pltpu.CompilerParams(vmem_limit_bytes=16 * MIB),
         cost_estimate=pl.CostEstimate(
             flops=200 * stations * beams, bytes_accessed=4 * (pairs + groups) * stations * beams, transcendentals=0
         ),
@@ -350,7 +350,7 @@
             pltpu.VMEM((GROUP, 2, lanes, stations), jnp.bfloat16),
             pltpu.VMEM((GROUP, powers, beams), jnp.float32),
         ],
-        compiler_params=pltpu.CompilerParams(vmem_limit_bytes=VMEM_LIMIT),
+        compiler_params=pltpu.CompilerParams(vmem_limit_bytes=24 * MIB),
         cost_estimate=pl.CostEstimate(
             flops=8 * count * GROUP * beams * stations * lanes, bytes_accessed=4 * stations * beams, transcendentals=0
         ),
@@ -358,17 +358,14 @@
     )(steps, mids, *[r for r, _ in received])
 
 
-def tree_kernel(first_slot, beams, shifts_ref, own_ref, next_ref, *refs):
+def tree_kernel(beams, moves_ref, own_ref, next_ref, *refs):
+
     out_ref, ping, pong = refs[-3:]
     sources, _, _, length, _ = own_ref.shape
     own_ref, next_ref = own_ref.at[:, 0], next_ref.at[:, 0]
     tiles, slots, depth, _ = ping.shape
-    base = first_slot + (pl.program_id(0) * pl.num_programs(1) + pl.program_id(1)) * slots
     span = 2 * length
     whole, rest, part, share = packing(beams)
-    zeros = jnp.zeros((tiles, slots, depth - span, LANES), jnp.float32)
-    ping[:, :, pl.ds(span, depth - span), :] = zeros
-    pong[:, :, pl.ds(span, depth - span), :] = zeros
     for ref, at in ((own_ref, 0), (next_ref, length)):
         for s in range(sources):
             for t in range(whole):
@@ -389,14 +386,17 @@
             start = t * GROUP
             for i in range(GROUP // 2):
                 lead = start + i // h * 2 * h + i % h
-                amounts = [shifts_ref[level, base + start + 2 * i + r] for r in range(2)]
+                masks = []
+                for r in range(2):
+                    amount = jnp.broadcast_to(moves_ref[level, pl.ds(start + 2 * i + r, 1), :], (rows, LANES))
+                    masks.append([amount == by for by in range(SHIFT_MOST)])
                 for tile in range(tiles):
                     first = src[tile, lead, pl.ds(0, rows), :]
                     shifted = [src[tile, lead + h, pl.ds(by, rows), :] for by in range(SHIFT_MOST + 1)]
                     for r in range(2):
                         moved = shifted[SHIFT_MOST]
                         for by in range(SHIFT_MOST):
-                            moved = jnp.where(amounts[r] == by, shifted[by], moved)
+                            moved = jnp.where(masks[r][by], shifted[by], moved)
                         dst[tile, start + 2 * i + r, pl.ds(0, rows), :] = first + moved
             return carry
 
@@ -410,7 +410,7 @@
             out_ref[pl.ds(tile * LANES * length + t, here, stride=length), :] = turned[:here]
 
 
-def dedisperse(shifts, own, after, beams, first_slot, total, so_far):
+def dedisperse(moves, own, after, beams, first_slot, total, so_far):
     sources, groups, rows, length, _ = own.shape
     block = LANES // GROUP
     blocks = sources // block
@@ -418,10 +418,10 @@
     depth = 2 * length + ROWS
     earlier = [] if so_far is None else [so_far]
     return pl.pallas_call(
-        functools.partial(tree_kernel, first_slot, beams),
+        functools.partial(tree_kernel, beams),
         grid=(groups, blocks),
         in_specs=[
-            pl.BlockSpec(memory_space=pltpu.SMEM),
+            pl.BlockSpec((LEVELS, LANES, LANES), lambda a, i: (0, first_slot // LANES + a * blocks + i, 0)),
             pl.BlockSpec((block, 1, rows, length, LANES), lambda a, i: (i, a, 0, 0, 0)),
             pl.BlockSpec((block, 1, rows, length, LANES), lambda a, i: (i, a, 0, 0, 0)),
             *[pl.BlockSpec(memory_space=pl.ANY) for _ in earlier],
@@ -430,12 +430,12 @@
         out_shape=jax.ShapeDtypeStruct((beams * length, total), jnp.float32),
         scratch_shapes=[pltpu.VMEM((tiles, LANES, depth, LANES), jnp.float32)] * 2,
         input_output_aliases={3: 0} if earlier else {},
-        compiler_params=pltpu.CompilerParams(vmem_limit_bytes=VMEM_LIMIT),
+        compiler_params=pltpu.CompilerParams(vmem_limit_bytes=16 * MIB),
         cost_estimate=pl.CostEstimate(
             flops=16 * beams * length * GROUP * sources * groups, bytes_accessed=10 * beams * length * GROUP * sources * groups, transcendentals=0
         ),
         name="dedisperse",
-    )(shifts, own, after, *earlier)
+    )(moves, own, after, *earlier)
 
 
 def swapped(x, owners):
@@ -452,6 +452,7 @@
     cuts = [0, ROWS, share] if share > ROWS else [0, share]
     early = [groups // 2, groups - groups // 2] if groups > 1 else [groups]
     calls = [groups // 2] + [1] * (groups - groups // 2) if groups > 1 else [groups]
+    moves = jnp.broadcast_to(shifts[:, :, None], (*shifts.shape, LANES))
     halos = []
     for first, last in zip(cuts, cuts[1:]):
         halos.append(shift_along(voltages[:, first:last, rim:], "tm", 1))
@@ -477,7 +478,7 @@
         power = beams_of(steps, mids, arrays, owners, start, many)
         owned = swapped(power, owners).reshape(power.shape)
         after = shift_along(owned, "tm", -1)
-        out = dedisperse(shifts, owned, after, beams, start * owners * GROUP, CHANNELS, out)
+        out = dedisperse(moves, owned, after, beams, start * owners * GROUP, CHANNELS, out)
         start += many
     return jnp.transpose(out.reshape(beams, length, CHANNELS), (0, 2, 1))
 

time: 207 us -> 201 us (0.971)
  Pallas kernels: 105 us -> 77.2 us
  local copies, waits for them, and re-layouts: 6.38 us -> 30.5 us
    unnamed x20 -> x36, local copies, waits for them, and re-layouts: 4.09 us -> 24.9 us
    pallas_call x3, Pallas kernels: 40.4 us -> 23.1 us  [beams_of(): pl.pallas_call(beam_kernel, grid=(count, pairs), in_specs=[pl.BlockSpec((...]
    pallas_call x3, Pallas kernels: 16.5 us -> 9.13 us  [dedisperse(): pl.pallas_call(functools.partial(tree_kernel, beams), grid=(groups, block...]
    pallas_call x1, Pallas kernels: 13.4 us -> 11.1 us  [turns(): pl.pallas_call(kernel, grid=(stations // (2 * ROWS),), in_specs=[pl.Block...]
  transfers between devices with their start and end apart: 10 -> 10, of which waited for: 4 -> 4; matrix products, arithmetic and copies ran while one was open for 1% -> 3% of each run, Pallas kernels for 42% -> 31%
where the time goes in v4:
time: 201 us; the launch traced here: 200 us
  Pallas kernels  77.2 us (38%)
  starting transfers between devices  40.7 us (20%)
  local copies, waits for them, and re-layouts  30.5 us (15%)
  waiting for transfers between devices  27.3 us (14%)
  blocking collectives  22.7 us (11%)
    pallas_call x2, Pallas kernels, channelize(): pl.pallas_call(functools.partial(channel_kernel, frames), grid=(stations...  33.8 us
    unnamed x36, local copies, waits for them, and re-layouts  24.9 us
    all_to_all x5, starting transfers between devices, swapped(): lax.all_to_all(x.reshape(owners, -1, LANES), 'grp', split_axis=0, concat_...  23.6 us
    pallas_call x3, Pallas kernels, beams_of(): pl.pallas_call(beam_kernel, grid=(count, pairs), in_specs=[pl.BlockSpec((...  23.1 us
    all_to_all x1, blocking collectives, swapped(): lax.all_to_all(x.reshape(owners, -1, LANES), 'grp', split_axis=0, concat_...  22.7 us
    ppermute x5, starting transfers between devices, shift_along(): return lax.ppermute(x, axis, pairs)  17.1 us
    all_to_all x5, waiting for transfers between devices, swapped(): lax.all_to_all(x.reshape(owners, -1, LANES), 'grp', split_axis=0, concat_...  13.7 us
    ppermute x5, waiting for transfers between devices, shift_along(): return lax.ppermute(x, axis, pairs)  13.6 us
  transfers between devices with their start and end apart: 10, of which 4 were waited for; matrix products, arithmetic and copies ran while one was open for 3% of the time, Pallas kernels for 31%

profile of v4, /device:TPU:1, one launch (start us, length us, event | category | flops | bytes accessed | tf_op | source)
XLA Modules:
  0.0 199.9 jit_solution(9280593731500627499)
XLA Ops:
  0.0 1.0 slice.14
  1.0 4.5 %collective-permute-start = (bf16[2,8,12288]{2,1,0:T(8,128)(2,1)S(1)}, bf16[2,8,12288]{2,1,0:T(8,128)(2,1)S(1)}, u32[]{:S(2)}, u32[]{:S(2)}) collective-permute-start(bf16[2,8,12288]{2,1,0:T(8,128)(2,1)S(1)} %slice.14), channel_id=1, source_target_pairs={{0,1},{1,2},{2,3},{4,5},{5,6},{6,7},{8,9},{9,10},{10,11},{12,13},{... | collective-permute-start | bytes 1179656 | tf_op jit(solution)/shard_map/ppermute | solution.py:33
  5.5 4.7 %collective-permute-done.halo_ref = bf16[2,8,12288]{2,1,0:T(8,128)(2,1)S(1)} collective-permute-done((bf16[2,8,12288]{2,1,0:T(8,128)(2,1)S(1)}, bf16[2,8,12288]{2,1,0:T(8,128)(2,1)S(1)}, u32[]{:S(2)}, u32[]{:S(2)}) %collective-permute-start) | collective-permute-done | bytes 393248 | tf_op jit(solution)/shard_map/ppermute | solution.py:33
  10.2 1.0 copy-done
  11.3 0.8 copy-done.7
  12.1 0.8 copy-done.9
  12.9 12.6 %channelize.2 = bf16[8,4,4,4,8,128]{5,4,3,2,1,0:T(8,128)(2,1)} custom-call(bf16[2,24,262144]{2,1,0:T(8,128)(2,1)} %x_ref.3, bf16[2,8,12288]{2,1,0:T(8,128)(2,1)S(1)} %collective-permute-done.halo_ref, f32[4,4096]{1,0:T(4,128)S(1)} %copy-done.7, f32[4,2,8,128]{3,2,1,0:T(8,128)S(1)} %copy-done.9, f32[4,2,128,128]{3,2,1,0:T(8,128)S(1)} %copy-done), custom_call_target="tpu_custom_call" | custom-call | flops 2147483648 | bytes 8388608 | tf_op jit(solution)/shard_map/channelize/pallas_call | solution.py:183
  25.5 5.7 %all-to-all-start = ((bf16[8,512,128]{2,1,0:T(8,128)(2,1)}), bf16[8,512,128]{2,1,0:T(8,128)(2,1)S(1)}, u32[]{:S(2)}, u32[]{:S(2)}) async-start(bf16[8,512,128]{2,1,0:T(8,128)(2,1)} %bitcast.4), calls=%async_computation | async-start | bytes 2097152 | tf_op jit(solution)/shard_map/all_to_all | solution.py:442
  31.2 1.2 slice.15
  32.4 4.7 %collective-permute-start.1 = (bf16[2,16,12288]{2,1,0:T(8,128)(2,1)S(1)}, bf16[2,16,12288]{2,1,0:T(8,128)(2,1)S(1)}, u32[]{:S(2)}, u32[]{:S(2)}) collective-permute-start(bf16[2,16,12288]{2,1,0:T(8,128)(2,1)S(1)} %slice.15), channel_id=1, source_target_pairs={{0,1},{1,2},{2,3},{4,5},{5,6},{6,7},{8,9},{9,10},{10,11},{12,13},{... | collective-permute-start | bytes 2359304 | tf_op jit(solution)/shard_map/ppermute | solution.py:33
  37.0 8.9 %collective-permute-done.1.halo_ref = bf16[2,16,12288]{2,1,0:T(8,128)(2,1)S(1)} collective-permute-done((bf16[2,16,12288]{2,1,0:T(8,128)(2,1)S(1)}, bf16[2,16,12288]{2,1,0:T(8,128)(2,1)S(1)}, u32[]{:S(2)}, u32[]{:S(2)}) %collective-permute-start.1) | collective-permute-done | bytes 786464 | tf_op jit(solution)/shard_map/ppermute | solution.py:33
  46.0 21.2 %channelize.3 = (bf16[8,2,4,4,16,128]{5,4,3,2,1,0:T(8,128)(2,1)}, bf16[8,2,4,4,16,128]{5,4,3,2,1,0:T(8,128)(2,1)S(1)}) custom-call(bf16[2,24,262144]{2,1,0:T(8,128)(2,1)} %x_ref.3, bf16[2,16,12288]{2,1,0:T(8,128)(2,1)S(1)} %collective-permute-done.1.halo_ref, f32[4,4096]{1,0:T(4,128)S(1)} %copy-done.8, f32[4,2,8,128]{3,2,1,0:T(8,128)S(1)} %copy-done.10, ...), custom_call_target="tpu_custom_call" | custom-call | flops 4294967296 | bytes 16777216 | tf_op jit(solution)/shard_map/channelize/pallas_call | solution.py:183
  67.2 0.0 all-to-all-done
  67.2 22.7 %all_to_all.30 = bf16[8,512,128]{2,1,0:T(8,128)(2,1)S(1)} all-to-all(bf16[8,512,128]{2,1,0:T(8,128)(2,1)S(1)} %bitcast.32), channel_id=1, replica_groups=mesh['grp'=8,'tm'=4] {'grp'}, dimensions={0} | all-to-all | bytes 2097152 | tf_op jit(solution)/shard_map/all_to_all | solution.py:442
  89.9 3.6 %all-to-all-start.4 = ((bf16[8,512,128]{2,1,0:T(8,128)(2,1)}), bf16[8,512,128]{2,1,0:T(8,128)(2,1)S(1)}, u32[]{:S(2)}, u32[]{:S(2)}) async-start(bf16[8,512,128]{2,1,0:T(8,128)(2,1)} %bitcast.12), calls=%async_computation.4 | async-start | bytes 2097152 | tf_op jit(solution)/shard_map/all_to_all | solution.py:442
  93.5 2.1 %slice.17 = s32[8,16,1536]{2,1,0:T(8,128)} slice(s32[8,24,1536]{2,1,0:T(8,128)} %bitcast.37), slice={[0:8], [8:24], [0:1536]} | slice | bytes 1572864 | tf_op jit(solution)/shard_map/slice | solution.py:472
  95.6 1.0 slice_bitcast_fusion
  96.6 1.2 pad_add_fusion.delays_ref
  97.8 11.1 %turns.1 = (bf16[8,2,192,1536]{3,2,1,0:T(8,128)(2,1)S(1)}, bf16[4,2,192,1536]{3,2,1,0:T(8,128)(2,1)S(1)}) custom-call(s32[1]{0:T(128)} %bitcast.first_ref, s32[192,1536]{1,0:T(8,128)S(1)} %pad_add_fusion.delays_ref), custom_call_target="tpu_custom_call" | custom-call | flops 58982400 | bytes 14155776 | tf_op jit(solution)/shard_map/turns/pallas_call | solution.py:256
  108.9 5.7 %beams.4 = bf16[8,1,24,8,128]{4,3,2,1,0:T(8,128)(2,1)S(1)} custom-call(bf16[8,2,192,1536]{3,2,1,0:T(8,128)(2,1)S(1)} %get-tuple-element.9.step_ref, bf16[4,2,192,1536]{3,2,1,0:T(8,128)(2,1)S(1)} %get-tuple-element.10.mid_ref, bf16[8,64,8,128]{3,2,1,0:T(8,128)(2,1)S(1)} %bitcast.26, bf16[8,32,16,128]{3,2,1,0:T(8,128)(2,1)S(1)} %bitcast.29), custom_call_target="tpu_custom_call" | custom-call | flops 4831838208 | bytes 1179648 | tf_op jit(solution)/shard_map/beams/pallas_call | solution.py:336
  114.7 0.7 copy-done.6
  115.4 3.7 %copy-done.11 = bf16[8,2,192,1536]{3,2,1,0:T(8,128)(2,1)} copy-done((bf16[8,2,192,1536]{3,2,1,0:T(8,128)(2,1)}, bf16[8,2,192,1536]{3,2,1,0:T(8,128)(2,1)S(1)}, u32[]{:S(2)}) %copy-start.11) | copy-done | bytes 9437208
  119.1 2.2 %copy-done.14 = bf16[4,2,192,1536]{3,2,1,0:T(8,128)(2,1)} copy-done((bf16[4,2,192,1536]{3,2,1,0:T(8,128)(2,1)}, bf16[4,2,192,1536]{3,2,1,0:T(8,128)(2,1)S(1)}, u32[]{:S(2)}) %copy-start.14) | copy-done | bytes 4718616
  121.3 5.4 %all-to-all-start.3 = ((bf16[8,192,128]{2,1,0:T(8,128)(2,1)}), bf16[8,192,128]{2,1,0:T(8,128)(2,1)S(1)}, u32[]{:S(2)}, u32[]{:S(2)}) async-start(bf16[8,192,128]{2,1,0:T(8,128)(2,1)} %bitcast.35), calls=%async_computation.3 | async-start | bytes 786432 | tf_op jit(solution)/shard_map/all_to_all | solution.py:442
  126.7 3.7 %copy-done.12 = bf16[8,2,192,1536]{3,2,1,0:T(8,128)(2,1)S(1)} copy-done((bf16[8,2,192,1536]{3,2,1,0:T(8,128)(2,1)S(1)}, bf16[8,2,192,1536]{3,2,1,0:T(8,128)(2,1)}, u32[]{:S(2)}) %copy-start.12) | copy-done | bytes 9437208
  130.4 2.3 %copy-done.15 = bf16[4,2,192,1536]{3,2,1,0:T(8,128)(2,1)S(1)} copy-done((bf16[4,2,192,1536]{3,2,1,0:T(8,128)(2,1)S(1)}, bf16[4,2,192,1536]{3,2,1,0:T(8,128)(2,1)}, u32[]{:S(2)}) %copy-start.15) | copy-done | bytes 4718616
  132.7 11.7 %beams.5 = bf16[8,2,24,8,128]{4,3,2,1,0:T(8,128)(2,1)S(1)} custom-call(bf16[8,2,192,1536]{3,2,1,0:T(8,128)(2,1)S(1)} %copy-done.12, bf16[4,2,192,1536]{3,2,1,0:T(8,128)(2,1)S(1)} %copy-done.15, bf16[8,64,8,128]{3,2,1,0:T(8,128)(2,1)S(1)} %bitcast.27, bf16[8,32,16,128]{3,2,1,0:T(8,128)(2,1)S(1)} %bitcast.31), custom_call_target="tpu_custom_call" | custom-call | flops 9663676416 | bytes 1179648 | tf_op jit(solution)/shard_map/beams/pallas_call | solution.py:336
  144.4 0.0 copy-start.2
  144.4 0.9 copy-done.2
  145.2 5.4 %all-to-all-start.5 = ((bf16[8,384,128]{2,1,0:T(8,128)(2,1)}), bf16[8,384,128]{2,1,0:T(8,128)(2,1)S(1)}, u32[]{:S(2)}, u32[]{:S(2)}) async-start(bf16[8,384,128]{2,1,0:T(8,128)(2,1)} %bitcast.33), calls=%async_computation.5 | async-start | bytes 1572864 | tf_op jit(solution)/shard_map/all_to_all | solution.py:442
  150.7 3.7 %copy-done.13 = bf16[8,2,192,1536]{3,2,1,0:T(8,128)(2,1)S(1)} copy-done((bf16[8,2,192,1536]{3,2,1,0:T(8,128)(2,1)S(1)}, bf16[8,2,192,1536]{3,2,1,0:T(8,128)(2,1)}, u32[]{:S(2)}) %copy-start.13) | copy-done | bytes 9437208
  154.4 2.3 %copy-done.16 = bf16[4,2,192,1536]{3,2,1,0:T(8,128)(2,1)S(1)} copy-done((bf16[4,2,192,1536]{3,2,1,0:T(8,128)(2,1)S(1)}, bf16[4,2,192,1536]{3,2,1,0:T(8,128)(2,1)}, u32[]{:S(2)}) %copy-start.16) | copy-done | bytes 4718616
  156.7 5.7 %beams.3 = bf16[8,1,24,8,128]{4,3,2,1,0:T(8,128)(2,1)S(1)} custom-call(bf16[8,2,192,1536]{3,2,1,0:T(8,128)(2,1)S(1)} %copy-done.13, bf16[4,2,192,1536]{3,2,1,0:T(8,128)(2,1)S(1)} %copy-done.16, bf16[8,64,8,128]{3,2,1,0:T(8,128)(2,1)S(1)} %bitcast.28, bf16[8,32,16,128]{3,2,1,0:T(8,128)(2,1)S(1)} %bitcast.30), custom_call_target="tpu_custom_call" | custom-call | flops 4831838208 | bytes 1179648 | tf_op jit(solution)/shard_map/beams/pallas_call | solution.py:336
  162.4 0.7 copy-done.5
  163.2 7.1 %all-to-all-done.5 = bf16[8,384,128]{2,1,0:T(8,128)(2,1)S(1)} async-done(((bf16[8,384,128]{2,1,0:T(8,128)(2,1)}), bf16[8,384,128]{2,1,0:T(8,128)(2,1)S(1)}, u32[]{:S(2)}, u32[]{:S(2)}) %all-to-all-start.5) | async-done | bytes 786464 | tf_op jit(solution)/shard_map/all_to_all | solution.py:442
  170.3 3.5 %all-to-all-start.2 = ((bf16[8,192,128]{2,1,0:T(8,128)(2,1)}), bf16[8,192,128]{2,1,0:T(8,128)(2,1)S(1)}, u32[]{:S(2)}, u32[]{:S(2)}) async-start(bf16[8,192,128]{2,1,0:T(8,128)(2,1)} %bitcast.34), calls=%async_computation.2 | async-start | bytes 786432 | tf_op jit(solution)/shard_map/all_to_all | solution.py:442
  173.8 2.6 %collective-permute-start.4 = (bf16[8,2,24,8,128]{4,3,2,1,0:T(8,128)(2,1)S(1)}, bf16[8,2,24,8,128]{4,3,2,1,0:T(8,128)(2,1)S(1)}, u32[]{:S(2)}, u32[]{:S(2)}) collective-permute-start(bf16[8,2,24,8,128]{4,3,2,1,0:T(8,128)(2,1)S(1)} %bitcast.20), channel_id=1, source_target_pairs={{1,0},{2,1},{3,2},{5,4},{6,5},{7,6},{9,8},{10,9},{11,10},{13,12},{... | collective-permute-start | bytes 2359304 | tf_op jit(solution)/shard_map/ppermute | solution.py:33
  176.4 1.9 collective-permute-start.3
  178.3 6.6 %all-to-all-done.2 = bf16[8,192,128]{2,1,0:T(8,128)(2,1)S(1)} async-done(((bf16[8,192,128]{2,1,0:T(8,128)(2,1)}), bf16[8,192,128]{2,1,0:T(8,128)(2,1)S(1)}, u32[]{:S(2)}, u32[]{:S(2)}) %all-to-all-start.2) | async-done | bytes 393248 | tf_op jit(solution)/shard_map/all_to_all | solution.py:442
  184.9 3.4 %collective-permute-start.2 = (bf16[8,1,24,8,128]{4,3,2,1,0:T(8,128)(2,1)S(1)}, bf16[8,1,24,8,128]{4,3,2,1,0:T(8,128)(2,1)S(1)}, u32[]{:S(2)}, u32[]{:S(2)}) collective-permute-start(bf16[8,1,24,8,128]{4,3,2,1,0:T(8,128)(2,1)S(1)} %bitcast.24), channel_id=1, source_target_pairs={{1,0},{2,1},{3,2},{5,4},{6,5},{7,6},{9,8},{10,9},{11,10},{13,12},{... | collective-permute-start | bytes 1179656 | tf_op jit(solution)/shard_map/ppermute | solution.py:33
  188.4 0.0 copy-start.3
  188.4 0.9 copy-done.3
  189.2 0.3 broadcast_in_dim.2.moves_ref
  189.6 0.0 copy-start.4
  189.6 1.1 copy-done.4
  190.7 4.2 %dedisperse.3.refs_0_ = f32[1536,512]{1,0:T(8,128)} custom-call(s32[4,512,128]{2,1,0:T(8,128)S(1)} %broadcast_in_dim.2.moves_ref, bf16[8,2,24,8,128]{4,3,2,1,0:T(8,128)(2,1)S(1)} %bitcast.21, bf16[8,2,24,8,128]{4,3,2,1,0:T(8,128)(2,1)S(1)} %copy-done.4), custom_call_target="tpu_custom_call" | custom-call | flops 6291456 | bytes 3932160 | tf_op jit(solution)/shard_map/dedisperse/pallas_call | solution.py:420
  194.9 2.5 %dedisperse.4.refs_0_ = f32[1536,512]{1,0:T(8,128)} custom-call(s32[4,512,128]{2,1,0:T(8,128)S(1)} %broadcast_in_dim.2.moves_ref, bf16[8,1,24,8,128]{4,3,2,1,0:T(8,128)(2,1)S(1)} %bitcast.23, bf16[8,1,24,8,128]{4,3,2,1,0:T(8,128)(2,1)S(1)} %collective-permute-done.3.next_ref, f32[1536,512]{1,0:T(8,128)} %dedisperse.3.refs_0_), custom_call_target="tpu_custom_call", output_to_operand_aliasing={{}: (3, {})} | custom-call | flops 3145728 | bytes 1966080 | tf_op jit(solution)/shard_map/dedisperse/pallas_call | solution.py:420
  197.4 2.5 %dedisperse.5 = f32[1536,512]{1,0:T(8,128)} custom-call(s32[4,512,128]{2,1,0:T(8,128)S(1)} %broadcast_in_dim.2.moves_ref, bf16[8,1,24,8,128]{4,3,2,1,0:T(8,128)(2,1)S(1)} %bitcast.25, bf16[8,1,24,8,128]{4,3,2,1,0:T(8,128)(2,1)S(1)} %collective-permute-done.2.next_ref, f32[1536,512]{1,0:T(8,128)} %dedisperse.4.refs_0_), custom_call_target="tpu_custom_call", output_to_operand_aliasing={{}: (3, {})} | custom-call | flops 3145728 | bytes 1966080 | tf_op jit(solution)/shard_map/dedisperse/pallas_call | solution.py:420
  (24 shorter events, 0.0 us)
Async XLA Ops:
  1.0 9.2 %collective-permute-start = (bf16[2,8,12288]{2,1,0:T(8,128)(2,1)S(1)}, bf16[2,8,12288]{2,1,0:T(8,128)(2,1)S(1)}, u32[]{:S(2)}, u32[]{:S(2)}) collective-permute-start(bf16[2,8,12288]{2,1,0:T(8,128)(2,1)S(1)} %slice.14), channel_id=1, source_target_pairs={{0,1},{1,2},{2,3},{4,5},{5,6},{6,7},{8,9},{9,10},{10,11},{12,13},{... | collective-permute-start | bytes 1179656 | tf_op jit(solution)/shard_map/ppermute | solution.py:33
  10.2 1.0 copy-start
  11.3 0.8 copy-start.7
  12.1 0.8 copy-start.9
  25.5 20.5 %copy-start.1 = (f32[4,2,128,128]{3,2,1,0:T(8,128)S(1)}, f32[4,2,128,128]{3,2,1,0:T(8,128)}, u32[]{:S(2)}) copy-start(f32[4,2,128,128]{3,2,1,0:T(8,128)} %constant.13.clone.coarse_ref) | copy-start | bytes 1572868
  25.5 20.5 %copy-start.8 = (f32[4,4096]{1,0:T(4,128)S(1)}, f32[4,4096]{1,0:T(4,128)}, u32[]{:S(2)}) copy-start(f32[4,4096]{1,0:T(4,128)} %taps_ref.3) | copy-start | bytes 196612
  25.5 20.5 %copy-start.10 = (f32[4,2,8,128]{3,2,1,0:T(8,128)S(1)}, f32[4,2,8,128]{3,2,1,0:T(8,128)}, u32[]{:S(2)}) copy-start(f32[4,2,8,128]{3,2,1,0:T(8,128)} %constant.12.clone.fine_ref) | copy-start | bytes 98308
  25.5 41.7 %all-to-all-start = ((bf16[8,512,128]{2,1,0:T(8,128)(2,1)}), bf16[8,512,128]{2,1,0:T(8,128)(2,1)S(1)}, u32[]{:S(2)}, u32[]{:S(2)}) async-start(bf16[8,512,128]{2,1,0:T(8,128)(2,1)} %bitcast.4), calls=%async_computation | async-start | bytes 2097152 | tf_op jit(solution)/shard_map/all_to_all | solution.py:442
  32.4 13.6 %collective-permute-start.1 = (bf16[2,16,12288]{2,1,0:T(8,128)(2,1)S(1)}, bf16[2,16,12288]{2,1,0:T(8,128)(2,1)S(1)}, u32[]{:S(2)}, u32[]{:S(2)}) collective-permute-start(bf16[2,16,12288]{2,1,0:T(8,128)(2,1)S(1)} %slice.15), channel_id=1, source_target_pairs={{0,1},{1,2},{2,3},{4,5},{5,6},{6,7},{8,9},{9,10},{10,11},{12,13},{... | collective-permute-start | bytes 2359304 | tf_op jit(solution)/shard_map/ppermute | solution.py:33
  89.9 31.4 %all-to-all-start.4 = ((bf16[8,512,128]{2,1,0:T(8,128)(2,1)}), bf16[8,512,128]{2,1,0:T(8,128)(2,1)S(1)}, u32[]{:S(2)}, u32[]{:S(2)}) async-start(bf16[8,512,128]{2,1,0:T(8,128)(2,1)} %bitcast.12), calls=%async_computation.4 | async-start | bytes 2097152 | tf_op jit(solution)/shard_map/all_to_all | solution.py:442
  114.7 0.8 copy-start.6
  115.4 3.7 %copy-start.11 = (bf16[8,2,192,1536]{3,2,1,0:T(8,128)(2,1)}, bf16[8,2,192,1536]{3,2,1,0:T(8,128)(2,1)S(1)}, u32[]{:S(2)}) copy-start(bf16[8,2,192,1536]{3,2,1,0:T(8,128)(2,1)S(1)} %get-tuple-element.9.step_ref) | copy-start | bytes 28311556
  119.1 2.2 %copy-start.14 = (bf16[4,2,192,1536]{3,2,1,0:T(8,128)(2,1)}, bf16[4,2,192,1536]{3,2,1,0:T(8,128)(2,1)S(1)}, u32[]{:S(2)}) copy-start(bf16[4,2,192,1536]{3,2,1,0:T(8,128)(2,1)S(1)} %get-tuple-element.10.mid_ref) | copy-start | bytes 14155780
  121.3 23.9 %all-to-all-start.3 = ((bf16[8,192,128]{2,1,0:T(8,128)(2,1)}), bf16[8,192,128]{2,1,0:T(8,128)(2,1)S(1)}, u32[]{:S(2)}, u32[]{:S(2)}) async-start(bf16[8,192,128]{2,1,0:T(8,128)(2,1)} %bitcast.35), calls=%async_computation.3 | async-start | bytes 786432 | tf_op jit(solution)/shard_map/all_to_all | solution.py:442
  126.7 3.7 %copy-start.12 = (bf16[8,2,192,1536]{3,2,1,0:T(8,128)(2,1)S(1)}, bf16[8,2,192,1536]{3,2,1,0:T(8,128)(2,1)}, u32[]{:S(2)}) copy-start(bf16[8,2,192,1536]{3,2,1,0:T(8,128)(2,1)} %copy-done.11) | copy-start | bytes 28311556
  130.4 2.3 %copy-start.15 = (bf16[4,2,192,1536]{3,2,1,0:T(8,128)(2,1)S(1)}, bf16[4,2,192,1536]{3,2,1,0:T(8,128)(2,1)}, u32[]{:S(2)}) copy-start(bf16[4,2,192,1536]{3,2,1,0:T(8,128)(2,1)} %copy-done.14) | copy-start | bytes 14155780
  144.4 0.9 copy-start.2
  145.2 25.1 %all-to-all-start.5 = ((bf16[8,384,128]{2,1,0:T(8,128)(2,1)}), bf16[8,384,128]{2,1,0:T(8,128)(2,1)S(1)}, u32[]{:S(2)}, u32[]{:S(2)}) async-start(bf16[8,384,128]{2,1,0:T(8,128)(2,1)} %bitcast.33), calls=%async_computation.5 | async-start | bytes 1572864 | tf_op jit(solution)/shard_map/all_to_all | solution.py:442
  150.7 3.7 %copy-start.13 = (bf16[8,2,192,1536]{3,2,1,0:T(8,128)(2,1)S(1)}, bf16[8,2,192,1536]{3,2,1,0:T(8,128)(2,1)}, u32[]{:S(2)}) copy-start(bf16[8,2,192,1536]{3,2,1,0:T(8,128)(2,1)} %copy-done.11) | copy-start | bytes 28311556
  154.4 2.3 %copy-start.16 = (bf16[4,2,192,1536]{3,2,1,0:T(8,128)(2,1)S(1)}, bf16[4,2,192,1536]{3,2,1,0:T(8,128)(2,1)}, u32[]{:S(2)}) copy-start(bf16[4,2,192,1536]{3,2,1,0:T(8,128)(2,1)} %copy-done.14) | copy-start | bytes 14155780
  156.7 32.6 %copy-start.17 = (s32[4,512]{1,0:T(4,128)S(1)}, s32[4,512]{1,0:T(4,128)}, u32[]{:S(2)}) copy-start(s32[4,512]{1,0:T(4,128)} %param.11) | copy-start | bytes 24580
  162.4 0.7 copy-start.5
  170.3 14.6 %all-to-all-start.2 = ((bf16[8,192,128]{2,1,0:T(8,128)(2,1)}), bf16[8,192,128]{2,1,0:T(8,128)(2,1)S(1)}, u32[]{:S(2)}, u32[]{:S(2)}) async-start(bf16[8,192,128]{2,1,0:T(8,128)(2,1)} %bitcast.34), calls=%async_computation.2 | async-start | bytes 786432 | tf_op jit(solution)/shard_map/all_to_all | solution.py:442
  173.8 14.5 %collective-permute-start.4 = (bf16[8,2,24,8,128]{4,3,2,1,0:T(8,128)(2,1)S(1)}, bf16[8,2,24,8,128]{4,3,2,1,0:T(8,128)(2,1)S(1)}, u32[]{:S(2)}, u32[]{:S(2)}) collective-permute-start(bf16[8,2,24,8,128]{4,3,2,1,0:T(8,128)(2,1)S(1)} %bitcast.20), channel_id=1, source_target_pairs={{1,0},{2,1},{3,2},{5,4},{6,5},{7,6},{9,8},{10,9},{11,10},{13,12},{... | collective-permute-start | bytes 2359304 | tf_op jit(solution)/shard_map/ppermute | solution.py:33
  176.4 18.5 %collective-permute-start.3 = (bf16[8,1,24,8,128]{4,3,2,1,0:T(8,128)(2,1)S(1)}, bf16[8,1,24,8,128]{4,3,2,1,0:T(8,128)(2,1)S(1)}, u32[]{:S(2)}, u32[]{:S(2)}) collective-permute-start(bf16[8,1,24,8,128]{4,3,2,1,0:T(8,128)(2,1)S(1)} %bitcast.22), channel_id=1, source_target_pairs={{1,0},{2,1},{3,2},{5,4},{6,5},{7,6},{9,8},{10,9},{11,10},{13,12},{... | collective-permute-start | bytes 1179656 | tf_op jit(solution)/shard_map/ppermute | solution.py:33
  184.9 12.5 %collective-permute-start.2 = (bf16[8,1,24,8,128]{4,3,2,1,0:T(8,128)(2,1)S(1)}, bf16[8,1,24,8,128]{4,3,2,1,0:T(8,128)(2,1)S(1)}, u32[]{:S(2)}, u32[]{:S(2)}) collective-permute-start(bf16[8,1,24,8,128]{4,3,2,1,0:T(8,128)(2,1)S(1)} %bitcast.24), channel_id=1, source_target_pairs={{1,0},{2,1},{3,2},{5,4},{6,5},{7,6},{9,8},{10,9},{11,10},{13,12},{... | collective-permute-start | bytes 1179656 | tf_op jit(solution)/shard_map/ppermute | solution.py:33
  188.4 0.9 copy-start.3
  189.6 1.1 copy-start.4

commit v5 on v4

--- a/solution.py
+++ b/solution.py
@@ -276,9 +276,9 @@
     )(first, delays)
 
 
-def beam_kernel(step_ref, mid_ref, *refs):
+def beam_kernel(apart, step_ref, mid_ref, *refs):
     left, power = refs[-2:]
-    *r_refs, out_ref = refs[:-2]
+    r_refs, out_refs = refs[: -2 - apart], refs[-2 - apart : -2]
     lanes = r_refs[0].shape[3]
     _, _, beams = step_ref.shape
     half = lanes // 2
@@ -310,11 +310,10 @@
         cc, ss, sc, cs = cm * cj, sm * sj, sm * cj, cm * sj
         power[pairs + j, :, at] = one(pairs + j, cc - ss, sc + cs)
         power[pairs - 1 - j, :, at] = one(pairs - 1 - j, cc + ss, sc - cs)
-    mine = beams // out_ref.shape[0]
+    mine = beams // out_refs[0].shape[0]
     whole, rest, part, share = packing(mine)
 
-    @pl.when(j == pairs - 1)
-    def _():
+    def give(out_ref):
         for g in range(out_ref.shape[0]):
             own = power[:, :, g * mine : (g + 1) * mine]
             for t in range(whole):
@@ -326,15 +325,20 @@
                 tail = jnp.concatenate([tail[m * share : (m + 1) * share] for m in range(LANES // part)], 2)
                 out_ref[g, whole * GROUP :] = tail.astype(jnp.bfloat16)
 
-
-def beams_of(steps, mids, received, owners, start, count):
+    for n, out_ref in enumerate(out_refs):
+        mine_now = (pl.program_id(0) == n) | (apart == 1)
+        pl.when(mine_now & (j == pairs - 1))(functools.partial(give, out_ref))
+
+
+def beams_of(steps, mids, received, owners, start, count, apart):
     pairs, _, stations, beams = steps.shape
     lanes = received[0][0].shape[3]
     powers = lanes // (2 * INTEG)
     whole, _, _, share = packing(beams // owners)
     rows = whole * GROUP + share
+    held = count // apart
     return pl.pallas_call(
-        beam_kernel,
+        functools.partial(beam_kernel, apart),
         grid=(count, pairs),
         in_specs=[
             pl.BlockSpec((None, 2, stations, beams), lambda i, j: (j, 0, 0, 0)),
@@ -344,8 +348,10 @@
                 for r, at in received
             ],
         ],
-        out_specs=pl.BlockSpec((owners, None, rows, powers, LANES), lambda i, j: (0, i, 0, 0, 0)),
-        out_shape=jax.ShapeDtypeStruct((owners, count, rows, powers, LANES), jnp.bfloat16),
+        out_specs=[
+            pl.BlockSpec((owners, None, rows, powers, LANES), lambda i, j: (0, i if apart == 1 else 0, 0, 0, 0))
+        ] * apart,
+        out_shape=[jax.ShapeDtypeStruct((owners, held, rows, powers, LANES), jnp.bfloat16)] * apart,
         scratch_shapes=[
             pltpu.VMEM((GROUP, 2, lanes, stations), jnp.bfloat16),
             pltpu.VMEM((GROUP, powers, beams), jnp.float32),
@@ -451,10 +457,9 @@
     rim = voltages.shape[2] - (TAPS - 1) * TRANSFORM
     cuts = [0, ROWS, share] if share > ROWS else [0, share]
     early = [groups // 2, groups - groups // 2] if groups > 1 else [groups]
-    calls = [groups // 2] + [1] * (groups - groups // 2) if groups > 1 else [groups]
     moves = jnp.broadcast_to(shifts[:, :, None], (*shifts.shape, LANES))
     halos = []
-    for first, last in zip(cuts, cuts[1:]):
+    for n, (first, last) in enumerate(zip(cuts, cuts[1:])):
         halos.append(shift_along(voltages[:, first:last, rim:], "tm", 1))
     received = []
     for n, (first, last) in enumerate(zip(cuts, cuts[1:])):
@@ -472,14 +477,17 @@
     delays = jnp.concatenate([by_owner[:, a:b].reshape(-1, delays.shape[1]) for a, b in zip(cuts, cuts[1:])])
     mine = (lax.axis_index("grp") * GROUP).astype(jnp.int32).reshape(1)
     steps, mids = turns(mine, delays, owners, groups)
-    out, start = None, 0
-    for many in calls:
+    out, start, n = None, 0, 0
+    for call, many in enumerate(early):
         arrays = [(r, low) for r, low, high in received if low <= start and start + many <= high]
-        power = beams_of(steps, mids, arrays, owners, start, many)
-        owned = swapped(power, owners).reshape(power.shape)
-        after = shift_along(owned, "tm", -1)
-        out = dedisperse(moves, owned, after, beams, start * owners * GROUP, CHANNELS, out)
-        start += many
+        apart = many if call else 1
+        given = beams_of(steps, mids, arrays, owners, start, many, apart)
+        for power in given:
+            owned = swapped(power, owners).reshape(power.shape)
+            after = shift_along(owned, "tm", -1)
+            out = dedisperse(moves, owned, after, beams, start * owners * GROUP, CHANNELS, out)
+            start += many // apart
+            n += 1
     return jnp.transpose(out.reshape(beams, length, CHANNELS), (0, 2, 1))
 
 

time: 201 us -> 206 us (1.025)
  blocking collectives: 22.7 us -> 47.7 us
  local copies, waits for them, and re-layouts: 30.5 us -> 22.6 us
  waiting for transfers between devices: 27.3 us -> 20.4 us
  starting transfers between devices: 40.7 us -> 35.2 us
    all_to_all x1 -> x2, blocking collectives: 22.7 us -> 47.7 us  [swapped(): lax.all_to_all(x.reshape(owners, -1, LANES), 'grp', split_axis=0, concat_...]
    unnamed x36 -> x28, local copies, waits for them, and re-layouts: 24.9 us -> 16.9 us
    all_to_all x5 -> x4, waiting for transfers between devices: 13.7 us -> 6.6 us  [swapped(): lax.all_to_all(x.reshape(owners, -1, LANES), 'grp', split_axis=0, concat_...]
    all_to_all x5 -> x4, starting transfers between devices: 23.6 us -> 18.1 us  [swapped(): lax.all_to_all(x.reshape(owners, -1, LANES), 'grp', split_axis=0, concat_...]
    pallas_call x3 -> x2, Pallas kernels: 23.1 us -> 23.4 us  [beams_of(): pl.pallas_call(functools.partial(beam_kernel, apart), grid=(count, pairs)...]
  transfers between devices with their start and end apart: 10 -> 9, of which waited for: 4 -> 4; matrix products, arithmetic and copies ran while one was open for 3% -> 3% of each run, Pallas kernels for 31% -> 30%
where the time goes in v5:
time: 206 us; the launch traced here: 205 us
  Pallas kernels  77.5 us (38%)
  blocking collectives  47.7 us (23%)
  starting transfers between devices  35.2 us (17%)
  local copies, waits for them, and re-layouts  22.6 us (11%)
  waiting for transfers between devices  20.4 us (10%)
    all_to_all x2, blocking collectives, swapped(): lax.all_to_all(x.reshape(owners, -1, LANES), 'grp', split_axis=0, concat_...  47.7 us
    pallas_call x2, Pallas kernels, channelize(): pl.pallas_call(functools.partial(channel_kernel, frames), grid=(stations...  33.8 us
    pallas_call x2, Pallas kernels, beams_of(): pl.pallas_call(functools.partial(beam_kernel, apart), grid=(count, pairs)...  23.4 us
    all_to_all x4, starting transfers between devices, swapped(): lax.all_to_all(x.reshape(owners, -1, LANES), 'grp', split_axis=0, concat_...  18.1 us
    ppermute x5, starting transfers between devices, shift_along(): return lax.ppermute(x, axis, pairs)  17.1 us
    unnamed x28, local copies, waits for them, and re-layouts  16.9 us
    ppermute x5, waiting for transfers between devices, shift_along(): return lax.ppermute(x, axis, pairs)  13.8 us
    pallas_call x1, Pallas kernels, turns(): pl.pallas_call(kernel, grid=(stations // (2 * ROWS),), in_specs=[pl.Block...  11.1 us
  transfers between devices with their start and end apart: 9, of which 4 were waited for; matrix products, arithmetic and copies ran while one was open for 3% of the time, Pallas kernels for 30%

profile of v5, /device:TPU:1, one launch (start us, length us, event | category | flops | bytes accessed | tf_op | source)
XLA Modules:
  0.0 204.7 jit_solution(2369827237053970024)
XLA Ops:
  0.0 1.0 slice.14
  1.0 4.5 %collective-permute-start = (bf16[2,8,12288]{2,1,0:T(8,128)(2,1)S(1)}, bf16[2,8,12288]{2,1,0:T(8,128)(2,1)S(1)}, u32[]{:S(2)}, u32[]{:S(2)}) collective-permute-start(bf16[2,8,12288]{2,1,0:T(8,128)(2,1)S(1)} %slice.14), channel_id=1, source_target_pairs={{0,1},{1,2},{2,3},{4,5},{5,6},{6,7},{8,9},{9,10},{10,11},{12,13},{... | collective-permute-start | bytes 1179656 | tf_op jit(solution)/shard_map/ppermute | solution.py:33
  5.5 4.7 %collective-permute-done.halo_ref = bf16[2,8,12288]{2,1,0:T(8,128)(2,1)S(1)} collective-permute-done((bf16[2,8,12288]{2,1,0:T(8,128)(2,1)S(1)}, bf16[2,8,12288]{2,1,0:T(8,128)(2,1)S(1)}, u32[]{:S(2)}, u32[]{:S(2)}) %collective-permute-start) | collective-permute-done | bytes 393248 | tf_op jit(solution)/shard_map/ppermute | solution.py:33
  10.2 1.0 copy-done
  11.3 0.8 copy-done.5
  12.1 0.8 copy-done.7
  12.9 12.6 %channelize.2 = bf16[8,4,4,4,8,128]{5,4,3,2,1,0:T(8,128)(2,1)} custom-call(bf16[2,24,262144]{2,1,0:T(8,128)(2,1)} %x_ref.3, bf16[2,8,12288]{2,1,0:T(8,128)(2,1)S(1)} %collective-permute-done.halo_ref, f32[4,4096]{1,0:T(4,128)S(1)} %copy-done.5, f32[4,2,8,128]{3,2,1,0:T(8,128)S(1)} %copy-done.7, f32[4,2,128,128]{3,2,1,0:T(8,128)S(1)} %copy-done), custom_call_target="tpu_custom_call" | custom-call | flops 2147483648 | bytes 8388608 | tf_op jit(solution)/shard_map/channelize/pallas_call | solution.py:183
  25.5 5.7 %all-to-all-start = ((bf16[8,512,128]{2,1,0:T(8,128)(2,1)}), bf16[8,512,128]{2,1,0:T(8,128)(2,1)S(1)}, u32[]{:S(2)}, u32[]{:S(2)}) async-start(bf16[8,512,128]{2,1,0:T(8,128)(2,1)} %bitcast.4), calls=%async_computation | async-start | bytes 2097152 | tf_op jit(solution)/shard_map/all_to_all | solution.py:448
  31.2 1.2 slice.15
  32.4 4.7 %collective-permute-start.1 = (bf16[2,16,12288]{2,1,0:T(8,128)(2,1)S(1)}, bf16[2,16,12288]{2,1,0:T(8,128)(2,1)S(1)}, u32[]{:S(2)}, u32[]{:S(2)}) collective-permute-start(bf16[2,16,12288]{2,1,0:T(8,128)(2,1)S(1)} %slice.15), channel_id=1, source_target_pairs={{0,1},{1,2},{2,3},{4,5},{5,6},{6,7},{8,9},{9,10},{10,11},{12,13},{... | collective-permute-start | bytes 2359304 | tf_op jit(solution)/shard_map/ppermute | solution.py:33
  37.0 8.9 %collective-permute-done.1.halo_ref = bf16[2,16,12288]{2,1,0:T(8,128)(2,1)S(1)} collective-permute-done((bf16[2,16,12288]{2,1,0:T(8,128)(2,1)S(1)}, bf16[2,16,12288]{2,1,0:T(8,128)(2,1)S(1)}, u32[]{:S(2)}, u32[]{:S(2)}) %collective-permute-start.1) | collective-permute-done | bytes 786464 | tf_op jit(solution)/shard_map/ppermute | solution.py:33
  45.9 0.0 copy-done.1
  46.0 0.0 copy-done.6
  46.0 21.2 %channelize.3 = (bf16[8,2,4,4,16,128]{5,4,3,2,1,0:T(8,128)(2,1)}, bf16[8,2,4,4,16,128]{5,4,3,2,1,0:T(8,128)(2,1)S(1)}) custom-call(bf16[2,24,262144]{2,1,0:T(8,128)(2,1)} %x_ref.3, bf16[2,16,12288]{2,1,0:T(8,128)(2,1)S(1)} %collective-permute-done.1.halo_ref, f32[4,4096]{1,0:T(4,128)S(1)} %copy-done.6, f32[4,2,8,128]{3,2,1,0:T(8,128)S(1)} %copy-done.8, ...), custom_call_target="tpu_custom_call" | custom-call | flops 4294967296 | bytes 16777216 | tf_op jit(solution)/shard_map/channelize/pallas_call | solution.py:183
  67.2 0.0 all-to-all-done
  67.2 22.7 %all_to_all.30 = bf16[8,512,128]{2,1,0:T(8,128)(2,1)S(1)} all-to-all(bf16[8,512,128]{2,1,0:T(8,128)(2,1)S(1)} %bitcast.30), channel_id=1, replica_groups=mesh['grp'=8,'tm'=4] {'grp'}, dimensions={0} | all-to-all | bytes 2097152 | tf_op jit(solution)/shard_map/all_to_all | solution.py:448
  89.9 3.6 %all-to-all-start.4 = ((bf16[8,512,128]{2,1,0:T(8,128)(2,1)}), bf16[8,512,128]{2,1,0:T(8,128)(2,1)S(1)}, u32[]{:S(2)}, u32[]{:S(2)}) async-start(bf16[8,512,128]{2,1,0:T(8,128)(2,1)} %bitcast.12), calls=%async_computation.4 | async-start | bytes 2097152 | tf_op jit(solution)/shard_map/all_to_all | solution.py:448
  93.5 2.1 %slice.17 = s32[8,16,1536]{2,1,0:T(8,128)} slice(s32[8,24,1536]{2,1,0:T(8,128)} %bitcast.35), slice={[0:8], [8:24], [0:1536]} | slice | bytes 1572864 | tf_op jit(solution)/shard_map/slice | solution.py:477
  95.6 1.0 slice_bitcast_fusion
  96.6 1.2 pad_add_fusion.delays_ref
  97.8 11.1 %turns.1 = (bf16[8,2,192,1536]{3,2,1,0:T(8,128)(2,1)S(1)}, bf16[4,2,192,1536]{3,2,1,0:T(8,128)(2,1)S(1)}) custom-call(s32[1]{0:T(128)} %bitcast.first_ref, s32[192,1536]{1,0:T(8,128)S(1)} %pad_add_fusion.delays_ref), custom_call_target="tpu_custom_call" | custom-call | flops 58982400 | bytes 14155776 | tf_op jit(solution)/shard_map/turns/pallas_call | solution.py:256
  108.9 11.7 %beams.2 = (bf16[8,1,24,8,128]{4,3,2,1,0:T(8,128)(2,1)S(1)}, bf16[8,1,24,8,128]{4,3,2,1,0:T(8,128)(2,1)S(1)}) custom-call(bf16[8,2,192,1536]{3,2,1,0:T(8,128)(2,1)S(1)} %get-tuple-element.11.step_ref, bf16[4,2,192,1536]{3,2,1,0:T(8,128)(2,1)S(1)} %get-tuple-element.12.mid_ref, bf16[8,64,8,128]{3,2,1,0:T(8,128)(2,1)S(1)} %bitcast.26, ...), custom_call_target="tpu_custom_call" | custom-call | flops 9663676416 | bytes 1179648 | tf_op jit(solution)/shard_map/beams/pallas_call | solution.py:340
  120.7 0.7 copy-done.3
  121.4 0.8 copy-done.4
  122.2 3.7 %copy-done.9 = bf16[8,2,192,1536]{3,2,1,0:T(8,128)(2,1)} copy-done((bf16[8,2,192,1536]{3,2,1,0:T(8,128)(2,1)}, bf16[8,2,192,1536]{3,2,1,0:T(8,128)(2,1)S(1)}, u32[]{:S(2)}) %copy-start.9) | copy-done | bytes 9437208
  125.8 2.2 %copy-done.11 = bf16[4,2,192,1536]{3,2,1,0:T(8,128)(2,1)} copy-done((bf16[4,2,192,1536]{3,2,1,0:T(8,128)(2,1)}, bf16[4,2,192,1536]{3,2,1,0:T(8,128)(2,1)S(1)}, u32[]{:S(2)}) %copy-start.11) | copy-done | bytes 4718616
  128.1 0.0 all-to-all-done.4
  128.1 5.4 %all-to-all-start.3 = ((bf16[8,192,128]{2,1,0:T(8,128)(2,1)}), bf16[8,192,128]{2,1,0:T(8,128)(2,1)S(1)}, u32[]{:S(2)}, u32[]{:S(2)}) async-start(bf16[8,192,128]{2,1,0:T(8,128)(2,1)} %bitcast.33), calls=%async_computation.3 | async-start | bytes 786432 | tf_op jit(solution)/shard_map/all_to_all | solution.py:448
  133.4 3.7 %copy-done.10 = bf16[8,2,192,1536]{3,2,1,0:T(8,128)(2,1)S(1)} copy-done((bf16[8,2,192,1536]{3,2,1,0:T(8,128)(2,1)S(1)}, bf16[8,2,192,1536]{3,2,1,0:T(8,128)(2,1)}, u32[]{:S(2)}) %copy-start.10) | copy-done | bytes 9437208
  137.1 2.3 %copy-done.12 = bf16[4,2,192,1536]{3,2,1,0:T(8,128)(2,1)S(1)} copy-done((bf16[4,2,192,1536]{3,2,1,0:T(8,128)(2,1)S(1)}, bf16[4,2,192,1536]{3,2,1,0:T(8,128)(2,1)}, u32[]{:S(2)}) %copy-start.12) | copy-done | bytes 4718616
  139.4 11.7 %beams.3 = bf16[8,2,24,8,128]{4,3,2,1,0:T(8,128)(2,1)S(1)} custom-call(bf16[8,2,192,1536]{3,2,1,0:T(8,128)(2,1)S(1)} %copy-done.10, bf16[4,2,192,1536]{3,2,1,0:T(8,128)(2,1)S(1)} %copy-done.12, bf16[8,64,8,128]{3,2,1,0:T(8,128)(2,1)S(1)} %bitcast.27, bf16[8,32,16,128]{3,2,1,0:T(8,128)(2,1)S(1)} %bitcast.28), custom_call_target="tpu_custom_call" | custom-call | flops 9663676416 | bytes 1179648 | tf_op jit(solution)/shard_map/beams/pallas_call | solution.py:340
  151.1 0.0 copy-start.2
  151.1 0.9 copy-done.2
  152.0 0.0 all-to-all-done.3
  152.0 25.0 %all_to_all.31 = bf16[8,384,128]{2,1,0:T(8,128)(2,1)S(1)} all-to-all(bf16[8,384,128]{2,1,0:T(8,128)(2,1)} %bitcast.31), channel_id=1, replica_groups=mesh['grp'=8,'tm'=4] {'grp'}, dimensions={0} | all-to-all | bytes 1572864 | tf_op jit(solution)/shard_map/all_to_all | solution.py:448
  177.0 3.5 %all-to-all-start.2 = ((bf16[8,192,128]{2,1,0:T(8,128)(2,1)}), bf16[8,192,128]{2,1,0:T(8,128)(2,1)S(1)}, u32[]{:S(2)}, u32[]{:S(2)}) async-start(bf16[8,192,128]{2,1,0:T(8,128)(2,1)} %bitcast.32), calls=%async_computation.2 | async-start | bytes 786432 | tf_op jit(solution)/shard_map/all_to_all | solution.py:448
  180.5 2.6 %collective-permute-start.4 = (bf16[8,2,24,8,128]{4,3,2,1,0:T(8,128)(2,1)S(1)}, bf16[8,2,24,8,128]{4,3,2,1,0:T(8,128)(2,1)S(1)}, u32[]{:S(2)}, u32[]{:S(2)}) collective-permute-start(bf16[8,2,24,8,128]{4,3,2,1,0:T(8,128)(2,1)S(1)} %bitcast.20), channel_id=1, source_target_pairs={{1,0},{2,1},{3,2},{5,4},{6,5},{7,6},{9,8},{10,9},{11,10},{13,12},{... | collective-permute-start | bytes 2359304 | tf_op jit(solution)/shard_map/ppermute | solution.py:33
  183.0 1.9 collective-permute-start.3
  185.0 6.6 %all-to-all-done.2 = bf16[8,192,128]{2,1,0:T(8,128)(2,1)S(1)} async-done(((bf16[8,192,128]{2,1,0:T(8,128)(2,1)}), bf16[8,192,128]{2,1,0:T(8,128)(2,1)S(1)}, u32[]{:S(2)}, u32[]{:S(2)}) %all-to-all-start.2) | async-done | bytes 393248 | tf_op jit(solution)/shard_map/all_to_all | solution.py:448
  191.6 3.4 %collective-permute-start.2 = (bf16[8,1,24,8,128]{4,3,2,1,0:T(8,128)(2,1)S(1)}, bf16[8,1,24,8,128]{4,3,2,1,0:T(8,128)(2,1)S(1)}, u32[]{:S(2)}, u32[]{:S(2)}) collective-permute-start(bf16[8,1,24,8,128]{4,3,2,1,0:T(8,128)(2,1)S(1)} %bitcast.24), channel_id=1, source_target_pairs={{1,0},{2,1},{3,2},{5,4},{6,5},{7,6},{9,8},{10,9},{11,10},{13,12},{... | collective-permute-start | bytes 1179656 | tf_op jit(solution)/shard_map/ppermute | solution.py:33
  195.0 0.0 collective-permute-done.4.next_ref
  195.0 0.0 copy-done.13
  195.0 0.3 broadcast_in_dim.2.moves_ref
  195.4 4.2 %dedisperse.3.refs_0_ = f32[1536,512]{1,0:T(8,128)} custom-call(s32[4,512,128]{2,1,0:T(8,128)S(1)} %broadcast_in_dim.2.moves_ref, bf16[8,2,24,8,128]{4,3,2,1,0:T(8,128)(2,1)S(1)} %bitcast.21, bf16[8,2,24,8,128]{4,3,2,1,0:T(8,128)(2,1)S(1)} %collective-permute-done.4.next_ref), custom_call_target="tpu_custom_call" | custom-call | flops 6291456 | bytes 3932160 | tf_op jit(solution)/shard_map/dedisperse/pallas_call | solution.py:426
  199.6 0.0 collective-permute-done.3.next_ref
  199.6 2.5 %dedisperse.4.refs_0_ = f32[1536,512]{1,0:T(8,128)} custom-call(s32[4,512,128]{2,1,0:T(8,128)S(1)} %broadcast_in_dim.2.moves_ref, bf16[8,1,24,8,128]{4,3,2,1,0:T(8,128)(2,1)S(1)} %bitcast.23, bf16[8,1,24,8,128]{4,3,2,1,0:T(8,128)(2,1)S(1)} %collective-permute-done.3.next_ref, f32[1536,512]{1,0:T(8,128)} %dedisperse.3.refs_0_), custom_call_target="tpu_custom_call", output_to_operand_aliasing={{}: (3, {})} | custom-call | flops 3145728 | bytes 1966080 | tf_op jit(solution)/shard_map/dedisperse/pallas_call | solution.py:426
  202.0 0.1 collective-permute-done.2.next_ref
  202.2 2.5 %dedisperse.5 = f32[1536,512]{1,0:T(8,128)} custom-call(s32[4,512,128]{2,1,0:T(8,128)S(1)} %broadcast_in_dim.2.moves_ref, bf16[8,1,24,8,128]{4,3,2,1,0:T(8,128)(2,1)S(1)} %bitcast.25, bf16[8,1,24,8,128]{4,3,2,1,0:T(8,128)(2,1)S(1)} %collective-permute-done.2.next_ref, f32[1536,512]{1,0:T(8,128)} %dedisperse.4.refs_0_), custom_call_target="tpu_custom_call", output_to_operand_aliasing={{}: (3, {})} | custom-call | flops 3145728 | bytes 1966080 | tf_op jit(solution)/shard_map/dedisperse/pallas_call | solution.py:426
  (14 shorter events, 0.0 us)
Async XLA Ops:
  1.0 9.2 %collective-permute-start = (bf16[2,8,12288]{2,1,0:T(8,128)(2,1)S(1)}, bf16[2,8,12288]{2,1,0:T(8,128)(2,1)S(1)}, u32[]{:S(2)}, u32[]{:S(2)}) collective-permute-start(bf16[2,8,12288]{2,1,0:T(8,128)(2,1)S(1)} %slice.14), channel_id=1, source_target_pairs={{0,1},{1,2},{2,3},{4,5},{5,6},{6,7},{8,9},{9,10},{10,11},{12,13},{... | collective-permute-start | bytes 1179656 | tf_op jit(solution)/shard_map/ppermute | solution.py:33
  10.2 1.0 copy-start
  11.3 0.8 copy-start.5
  12.1 0.8 copy-start.7
  25.5 20.5 %copy-start.1 = (f32[4,2,128,128]{3,2,1,0:T(8,128)S(1)}, f32[4,2,128,128]{3,2,1,0:T(8,128)}, u32[]{:S(2)}) copy-start(f32[4,2,128,128]{3,2,1,0:T(8,128)} %constant.13.clone.coarse_ref) | copy-start | bytes 1572868
  25.5 20.5 %copy-start.6 = (f32[4,4096]{1,0:T(4,128)S(1)}, f32[4,4096]{1,0:T(4,128)}, u32[]{:S(2)}) copy-start(f32[4,4096]{1,0:T(4,128)} %taps_ref.3) | copy-start | bytes 196612
  25.5 20.5 %copy-start.8 = (f32[4,2,8,128]{3,2,1,0:T(8,128)S(1)}, f32[4,2,8,128]{3,2,1,0:T(8,128)}, u32[]{:S(2)}) copy-start(f32[4,2,8,128]{3,2,1,0:T(8,128)} %constant.12.clone.fine_ref) | copy-start | bytes 98308
  25.5 41.7 %all-to-all-start = ((bf16[8,512,128]{2,1,0:T(8,128)(2,1)}), bf16[8,512,128]{2,1,0:T(8,128)(2,1)S(1)}, u32[]{:S(2)}, u32[]{:S(2)}) async-start(bf16[8,512,128]{2,1,0:T(8,128)(2,1)} %bitcast.4), calls=%async_computation | async-start | bytes 2097152 | tf_op jit(solution)/shard_map/all_to_all | solution.py:448
  32.4 13.6 %collective-permute-start.1 = (bf16[2,16,12288]{2,1,0:T(8,128)(2,1)S(1)}, bf16[2,16,12288]{2,1,0:T(8,128)(2,1)S(1)}, u32[]{:S(2)}, u32[]{:S(2)}) collective-permute-start(bf16[2,16,12288]{2,1,0:T(8,128)(2,1)S(1)} %slice.15), channel_id=1, source_target_pairs={{0,1},{1,2},{2,3},{4,5},{5,6},{6,7},{8,9},{9,10},{10,11},{12,13},{... | collective-permute-start | bytes 2359304 | tf_op jit(solution)/shard_map/ppermute | solution.py:33
  89.9 38.1 %all-to-all-start.4 = ((bf16[8,512,128]{2,1,0:T(8,128)(2,1)}), bf16[8,512,128]{2,1,0:T(8,128)(2,1)S(1)}, u32[]{:S(2)}, u32[]{:S(2)}) async-start(bf16[8,512,128]{2,1,0:T(8,128)(2,1)} %bitcast.12), calls=%async_computation.4 | async-start | bytes 2097152 | tf_op jit(solution)/shard_map/all_to_all | solution.py:448
  120.6 0.8 copy-start.3
  121.4 0.8 copy-start.4
  122.2 3.7 %copy-start.9 = (bf16[8,2,192,1536]{3,2,1,0:T(8,128)(2,1)}, bf16[8,2,192,1536]{3,2,1,0:T(8,128)(2,1)S(1)}, u32[]{:S(2)}) copy-start(bf16[8,2,192,1536]{3,2,1,0:T(8,128)(2,1)S(1)} %get-tuple-element.11.step_ref) | copy-start | bytes 28311556
  125.8 2.2 %copy-start.11 = (bf16[4,2,192,1536]{3,2,1,0:T(8,128)(2,1)}, bf16[4,2,192,1536]{3,2,1,0:T(8,128)(2,1)S(1)}, u32[]{:S(2)}) copy-start(bf16[4,2,192,1536]{3,2,1,0:T(8,128)(2,1)S(1)} %get-tuple-element.12.mid_ref) | copy-start | bytes 14155780
  128.1 23.9 %all-to-all-start.3 = ((bf16[8,192,128]{2,1,0:T(8,128)(2,1)}), bf16[8,192,128]{2,1,0:T(8,128)(2,1)S(1)}, u32[]{:S(2)}, u32[]{:S(2)}) async-start(bf16[8,192,128]{2,1,0:T(8,128)(2,1)} %bitcast.33), calls=%async_computation.3 | async-start | bytes 786432 | tf_op jit(solution)/shard_map/all_to_all | solution.py:448
  133.4 3.7 %copy-start.10 = (bf16[8,2,192,1536]{3,2,1,0:T(8,128)(2,1)S(1)}, bf16[8,2,192,1536]{3,2,1,0:T(8,128)(2,1)}, u32[]{:S(2)}) copy-start(bf16[8,2,192,1536]{3,2,1,0:T(8,128)(2,1)} %copy-done.9) | copy-start | bytes 28311556
  137.1 2.3 %copy-start.12 = (bf16[4,2,192,1536]{3,2,1,0:T(8,128)(2,1)S(1)}, bf16[4,2,192,1536]{3,2,1,0:T(8,128)(2,1)}, u32[]{:S(2)}) copy-start(bf16[4,2,192,1536]{3,2,1,0:T(8,128)(2,1)} %copy-done.11) | copy-start | bytes 14155780
  139.4 55.6 %copy-start.13 = (s32[4,512]{1,0:T(4,128)S(1)}, s32[4,512]{1,0:T(4,128)}, u32[]{:S(2)}) copy-start(s32[4,512]{1,0:T(4,128)} %param.11) | copy-start | bytes 24580
  151.1 0.9 copy-start.2
  177.0 14.6 %all-to-all-start.2 = ((bf16[8,192,128]{2,1,0:T(8,128)(2,1)}), bf16[8,192,128]{2,1,0:T(8,128)(2,1)S(1)}, u32[]{:S(2)}, u32[]{:S(2)}) async-start(bf16[8,192,128]{2,1,0:T(8,128)(2,1)} %bitcast.32), calls=%async_computation.2 | async-start | bytes 786432 | tf_op jit(solution)/shard_map/all_to_all | solution.py:448
  180.5 14.5 %collective-permute-start.4 = (bf16[8,2,24,8,128]{4,3,2,1,0:T(8,128)(2,1)S(1)}, bf16[8,2,24,8,128]{4,3,2,1,0:T(8,128)(2,1)S(1)}, u32[]{:S(2)}, u32[]{:S(2)}) collective-permute-start(bf16[8,2,24,8,128]{4,3,2,1,0:T(8,128)(2,1)S(1)} %bitcast.20), channel_id=1, source_target_pairs={{1,0},{2,1},{3,2},{5,4},{6,5},{7,6},{9,8},{10,9},{11,10},{13,12},{... | collective-permute-start | bytes 2359304 | tf_op jit(solution)/shard_map/ppermute | solution.py:33
  183.0 16.5 %collective-permute-start.3 = (bf16[8,1,24,8,128]{4,3,2,1,0:T(8,128)(2,1)S(1)}, bf16[8,1,24,8,128]{4,3,2,1,0:T(8,128)(2,1)S(1)}, u32[]{:S(2)}, u32[]{:S(2)}) collective-permute-start(bf16[8,1,24,8,128]{4,3,2,1,0:T(8,128)(2,1)S(1)} %bitcast.22), channel_id=1, source_target_pairs={{1,0},{2,1},{3,2},{5,4},{6,5},{7,6},{9,8},{10,9},{11,10},{13,12},{... | collective-permute-start | bytes 1179656 | tf_op jit(solution)/shard_map/ppermute | solution.py:33
  191.6 10.6 %collective-permute-start.2 = (bf16[8,1,24,8,128]{4,3,2,1,0:T(8,128)(2,1)S(1)}, bf16[8,1,24,8,128]{4,3,2,1,0:T(8,128)(2,1)S(1)}, u32[]{:S(2)}, u32[]{:S(2)}) collective-permute-start(bf16[8,1,24,8,128]{4,3,2,1,0:T(8,128)(2,1)S(1)} %bitcast.24), channel_id=1, source_target_pairs={{1,0},{2,1},{3,2},{5,4},{6,5},{7,6},{9,8},{10,9},{11,10},{13,12},{... | collective-permute-start | bytes 1179656 | tf_op jit(solution)/shard_map/ppermute | solution.py:33

commit v6 on v5

--- a/solution.py
+++ b/solution.py
@@ -236,11 +236,11 @@
     return whole, rest, part, share
 
 
-def turns(first, delays, owners, groups):
+def turns(first, delays, owners, counts):
     stations, beams = delays.shape
     pairs = GROUP // 2
 
-    def kernel(first_ref, delays_ref, step_ref, mid_ref):
+    def kernel(first_ref, delays_ref, step_ref, *mid_refs):
         ch, sh = turn_of(delays_ref[...])
         twice = 2.0 * (ch * ch - sh * sh)
         before, now = (ch, -sh), (ch, sh)
@@ -248,10 +248,10 @@
             step_ref[j, 0] = now[0].astype(jnp.bfloat16)
             step_ref[j, 1] = now[1].astype(jnp.bfloat16)
             before, now = now, (twice * now[0] - before[0], twice * now[1] - before[1])
-        for a in range(groups):
+        for a, (mid_ref, at) in enumerate((ref, n) for ref in mid_refs for n in range(ref.shape[0])):
             c, s = turn_of(delays_ref[...] * (2 * (first_ref[0] + owners * GROUP * a) + GROUP - 1))
-            mid_ref[a, 0] = (c * (1.0 / math.sqrt(stations))).astype(jnp.bfloat16)
-            mid_ref[a, 1] = (s * (1.0 / math.sqrt(stations))).astype(jnp.bfloat16)
+            mid_ref[at, 0] = (c * (1.0 / math.sqrt(stations))).astype(jnp.bfloat16)
+            mid_ref[at, 1] = (s * (1.0 / math.sqrt(stations))).astype(jnp.bfloat16)
 
     return pl.pallas_call(
         kernel,
@@ -262,15 +262,15 @@
         ],
         out_specs=[
             pl.BlockSpec((pairs, 2, 2 * ROWS, beams), lambda i: (0, 0, i, 0)),
-            pl.BlockSpec((groups, 2, 2 * ROWS, beams), lambda i: (0, 0, i, 0)),
+            *[pl.BlockSpec((n, 2, 2 * ROWS, beams), lambda i: (0, 0, i, 0)) for n in counts],
         ],
         out_shape=[
             jax.ShapeDtypeStruct((pairs, 2, stations, beams), jnp.bfloat16),
-            jax.ShapeDtypeStruct((groups, 2, stations, beams), jnp.bfloat16),
+            *[jax.ShapeDtypeStruct((n, 2, stations, beams), jnp.bfloat16) for n in counts],
         ],
         compiler_params=pltpu.CompilerParams(vmem_limit_bytes=16 * MIB),
         cost_estimate=pl.CostEstimate(
-            flops=200 * stations * beams, bytes_accessed=4 * (pairs + groups) * stations * beams, transcendentals=0
+            flops=200 * stations * beams, bytes_accessed=4 * (pairs + sum(counts)) * stations * beams, transcendentals=0
         ),
         name="turns",
     )(first, delays)
@@ -342,7 +342,7 @@
         grid=(count, pairs),
         in_specs=[
             pl.BlockSpec((None, 2, stations, beams), lambda i, j: (j, 0, 0, 0)),
-            pl.BlockSpec((None, 2, stations, beams), lambda i, j: (i + start, 0, 0, 0)),
+            pl.BlockSpec((None, 2, stations, beams), lambda i, j: (i, 0, 0, 0)),
             *[
                 pl.BlockSpec((r.shape[0], GROUP, r.shape[2], lanes), lambda i, j, at=at: (0, i + start - at, 0, 0))
                 for r, at in received
@@ -476,12 +476,12 @@
     by_owner = delays.reshape(owners, share, delays.shape[1])
     delays = jnp.concatenate([by_owner[:, a:b].reshape(-1, delays.shape[1]) for a, b in zip(cuts, cuts[1:])])
     mine = (lax.axis_index("grp") * GROUP).astype(jnp.int32).reshape(1)
-    steps, mids = turns(mine, delays, owners, groups)
+    steps, *mids = turns(mine, delays, owners, early)
     out, start, n = None, 0, 0
     for call, many in enumerate(early):
         arrays = [(r, low) for r, low, high in received if low <= start and start + many <= high]
         apart = many if call else 1
-        given = beams_of(steps, mids, arrays, owners, start, many, apart)
+        given = beams_of(steps, mids[call], arrays, owners, start, many, apart)
         for power in given:
             owned = swapped(power, owners).reshape(power.shape)
             after = shift_along(owned, "tm", -1)

time: 206 us -> 204 us (level)
  local copies, waits for them, and re-layouts: 22.6 us -> 20.4 us
    unnamed x28 -> x26, local copies, waits for them, and re-layouts: 16.9 us -> 14.8 us
  transfers between devices with their start and end apart: 9 -> 9, of which waited for: 4 -> 4; matrix products, arithmetic and copies ran while one was open for 3% -> 3% of each run, Pallas kernels for 30% -> 31%
where the time goes in v6:
time: 204 us; the launch traced here: 203 us
  Pallas kernels  78.2 us (38%)
  blocking collectives  47.7 us (23%)
  starting transfers between devices  35.2 us (17%)
  local copies, waits for them, and re-layouts  20.4 us (10%)
  waiting for transfers between devices  20.4 us (10%)
    all_to_all x2, blocking collectives, swapped(): lax.all_to_all(x.reshape(owners, -1, LANES), 'grp', split_axis=0, concat_...  47.7 us
    pallas_call x2, Pallas kernels, channelize(): pl.pallas_call(functools.partial(channel_kernel, frames), grid=(stations...  33.8 us
    pallas_call x2, Pallas kernels, beams_of(): pl.pallas_call(functools.partial(beam_kernel, apart), grid=(count, pairs)...  24.1 us
    all_to_all x4, starting transfers between devices, swapped(): lax.all_to_all(x.reshape(owners, -1, LANES), 'grp', split_axis=0, concat_...  18.1 us
    ppermute x5, starting transfers between devices, shift_along(): return lax.ppermute(x, axis, pairs)  17.1 us
    unnamed x26, local copies, waits for them, and re-layouts  14.8 us
    ppermute x5, waiting for transfers between devices, shift_along(): return lax.ppermute(x, axis, pairs)  13.8 us
    pallas_call x1, Pallas kernels, turns(): pl.pallas_call(kernel, grid=(stations // (2 * ROWS),), in_specs=[pl.Block...  11.1 us
  transfers between devices with their start and end apart: 9, of which 4 were waited for; matrix products, arithmetic and copies ran while one was open for 3% of the time, Pallas kernels for 31%

profile of v6, /device:TPU:1, one launch (start us, length us, event | category | flops | bytes accessed | tf_op | source)
XLA Modules:
  0.0 203.3 jit_solution(2862601624664336448)
XLA Ops:
  0.0 1.0 slice.14
  1.0 4.5 %collective-permute-start = (bf16[2,8,12288]{2,1,0:T(8,128)(2,1)S(1)}, bf16[2,8,12288]{2,1,0:T(8,128)(2,1)S(1)}, u32[]{:S(2)}, u32[]{:S(2)}) collective-permute-start(bf16[2,8,12288]{2,1,0:T(8,128)(2,1)S(1)} %slice.14), channel_id=1, source_target_pairs={{0,1},{1,2},{2,3},{4,5},{5,6},{6,7},{8,9},{9,10},{10,11},{12,13},{... | collective-permute-start | bytes 1179656 | tf_op jit(solution)/shard_map/ppermute | solution.py:33
  5.5 4.7 %collective-permute-done.halo_ref = bf16[2,8,12288]{2,1,0:T(8,128)(2,1)S(1)} collective-permute-done((bf16[2,8,12288]{2,1,0:T(8,128)(2,1)S(1)}, bf16[2,8,12288]{2,1,0:T(8,128)(2,1)S(1)}, u32[]{:S(2)}, u32[]{:S(2)}) %collective-permute-start) | collective-permute-done | bytes 393248 | tf_op jit(solution)/shard_map/ppermute | solution.py:33
  10.2 1.0 copy-done
  11.3 0.8 copy-done.4
  12.1 0.8 copy-done.6
  12.9 12.6 %channelize.2 = bf16[8,4,4,4,8,128]{5,4,3,2,1,0:T(8,128)(2,1)} custom-call(bf16[2,24,262144]{2,1,0:T(8,128)(2,1)} %x_ref.3, bf16[2,8,12288]{2,1,0:T(8,128)(2,1)S(1)} %collective-permute-done.halo_ref, f32[4,4096]{1,0:T(4,128)S(1)} %copy-done.4, f32[4,2,8,128]{3,2,1,0:T(8,128)S(1)} %copy-done.6, f32[4,2,128,128]{3,2,1,0:T(8,128)S(1)} %copy-done), custom_call_target="tpu_custom_call" | custom-call | flops 2147483648 | bytes 8388608 | tf_op jit(solution)/shard_map/channelize/pallas_call | solution.py:183
  25.5 5.7 %all-to-all-start = ((bf16[8,512,128]{2,1,0:T(8,128)(2,1)}), bf16[8,512,128]{2,1,0:T(8,128)(2,1)S(1)}, u32[]{:S(2)}, u32[]{:S(2)}) async-start(bf16[8,512,128]{2,1,0:T(8,128)(2,1)} %bitcast.4), calls=%async_computation | async-start | bytes 2097152 | tf_op jit(solution)/shard_map/all_to_all | solution.py:448
  31.2 1.2 slice.15
  32.4 4.7 %collective-permute-start.1 = (bf16[2,16,12288]{2,1,0:T(8,128)(2,1)S(1)}, bf16[2,16,12288]{2,1,0:T(8,128)(2,1)S(1)}, u32[]{:S(2)}, u32[]{:S(2)}) collective-permute-start(bf16[2,16,12288]{2,1,0:T(8,128)(2,1)S(1)} %slice.15), channel_id=1, source_target_pairs={{0,1},{1,2},{2,3},{4,5},{5,6},{6,7},{8,9},{9,10},{10,11},{12,13},{... | collective-permute-start | bytes 2359304 | tf_op jit(solution)/shard_map/ppermute | solution.py:33
  37.0 8.9 %collective-permute-done.1.halo_ref = bf16[2,16,12288]{2,1,0:T(8,128)(2,1)S(1)} collective-permute-done((bf16[2,16,12288]{2,1,0:T(8,128)(2,1)S(1)}, bf16[2,16,12288]{2,1,0:T(8,128)(2,1)S(1)}, u32[]{:S(2)}, u32[]{:S(2)}) %collective-permute-start.1) | collective-permute-done | bytes 786464 | tf_op jit(solution)/shard_map/ppermute | solution.py:33
  45.9 0.0 copy-done.1
  46.0 0.0 copy-done.5
  46.0 0.0 copy-done.7
  46.0 21.2 %channelize.3 = (bf16[8,2,4,4,16,128]{5,4,3,2,1,0:T(8,128)(2,1)}, bf16[8,2,4,4,16,128]{5,4,3,2,1,0:T(8,128)(2,1)S(1)}) custom-call(bf16[2,24,262144]{2,1,0:T(8,128)(2,1)} %x_ref.3, bf16[2,16,12288]{2,1,0:T(8,128)(2,1)S(1)} %collective-permute-done.1.halo_ref, f32[4,4096]{1,0:T(4,128)S(1)} %copy-done.5, f32[4,2,8,128]{3,2,1,0:T(8,128)S(1)} %copy-done.7, ...), custom_call_target="tpu_custom_call" | custom-call | flops 4294967296 | bytes 16777216 | tf_op jit(solution)/shard_map/channelize/pallas_call | solution.py:183
  67.2 1.0 copy-done.2
  68.2 0.0 all-to-all-done
  68.2 22.9 %all_to_all.30 = bf16[8,512,128]{2,1,0:T(8,128)(2,1)S(1)} all-to-all(bf16[8,512,128]{2,1,0:T(8,128)(2,1)} %bitcast.30), channel_id=1, replica_groups=mesh['grp'=8,'tm'=4] {'grp'}, dimensions={0} | all-to-all | bytes 2097152 | tf_op jit(solution)/shard_map/all_to_all | solution.py:448
  91.1 3.6 %all-to-all-start.4 = ((bf16[8,512,128]{2,1,0:T(8,128)(2,1)}), bf16[8,512,128]{2,1,0:T(8,128)(2,1)S(1)}, u32[]{:S(2)}, u32[]{:S(2)}) async-start(bf16[8,512,128]{2,1,0:T(8,128)(2,1)} %bitcast.12), calls=%async_computation.4 | async-start | bytes 2097152 | tf_op jit(solution)/shard_map/all_to_all | solution.py:448
  94.7 2.1 %slice.17 = s32[8,16,1536]{2,1,0:T(8,128)} slice(s32[8,24,1536]{2,1,0:T(8,128)} %bitcast.34), slice={[0:8], [8:24], [0:1536]} | slice | bytes 1572864 | tf_op jit(solution)/shard_map/slice | solution.py:477
  96.8 1.0 slice_bitcast_fusion
  97.8 1.2 pad_add_fusion.delays_ref
  99.0 11.1 %turns.1 = (bf16[8,2,192,1536]{3,2,1,0:T(8,128)(2,1)S(1)}, bf16[2,2,192,1536]{3,2,1,0:T(8,128)(2,1)S(1)}, bf16[2,2,192,1536]{3,2,1,0:T(8,128)(2,1)S(1)}) custom-call(s32[1]{0:T(128)} %bitcast.first_ref, s32[192,1536]{1,0:T(8,128)S(1)} %pad_add_fusion.delays_ref), custom_call_target="tpu_custom_call" | custom-call | flops 58982400 | bytes 14155776 | tf_op jit(solution)/shard_map/turns/pallas_call | solution.py:256
  110.2 0.0 copy-start.10
  110.2 1.4 copy-done.10
  111.6 12.4 %beams.2 = (bf16[8,1,24,8,128]{4,3,2,1,0:T(8,128)(2,1)}, bf16[8,1,24,8,128]{4,3,2,1,0:T(8,128)(2,1)S(1)}) custom-call(bf16[8,2,192,1536]{3,2,1,0:T(8,128)(2,1)S(1)} %get-tuple-element.12.step_ref, bf16[2,2,192,1536]{3,2,1,0:T(8,128)(2,1)S(1)} %get-tuple-element.13.mid_ref, bf16[8,64,8,128]{3,2,1,0:T(8,128)(2,1)S(1)} %bitcast.26, ...), custom_call_target="tpu_custom_call" | custom-call | flops 9663676416 | bytes 1179648 | tf_op jit(solution)/shard_map/beams/pallas_call | solution.py:340
  124.0 0.7 copy-done.3
  124.8 3.7 %copy-done.8 = bf16[8,2,192,1536]{3,2,1,0:T(8,128)(2,1)} copy-done((bf16[8,2,192,1536]{3,2,1,0:T(8,128)(2,1)}, bf16[8,2,192,1536]{3,2,1,0:T(8,128)(2,1)S(1)}, u32[]{:S(2)}) %copy-start.8) | copy-done | bytes 9437208
  128.4 0.0 all-to-all-done.4
  128.4 5.4 %all-to-all-start.3 = ((bf16[8,192,128]{2,1,0:T(8,128)(2,1)}), bf16[8,192,128]{2,1,0:T(8,128)(2,1)S(1)}, u32[]{:S(2)}, u32[]{:S(2)}) async-start(bf16[8,192,128]{2,1,0:T(8,128)(2,1)} %bitcast.10), calls=%async_computation.3 | async-start | bytes 786432 | tf_op jit(solution)/shard_map/all_to_all | solution.py:448
  133.8 3.7 %copy-done.9 = bf16[8,2,192,1536]{3,2,1,0:T(8,128)(2,1)S(1)} copy-done((bf16[8,2,192,1536]{3,2,1,0:T(8,128)(2,1)S(1)}, bf16[8,2,192,1536]{3,2,1,0:T(8,128)(2,1)}, u32[]{:S(2)}) %copy-start.9) | copy-done | bytes 9437208
  137.5 1.7 copy-done.11
  139.1 11.6 %beams.3 = bf16[8,2,24,8,128]{4,3,2,1,0:T(8,128)(2,1)S(1)} custom-call(bf16[8,2,192,1536]{3,2,1,0:T(8,128)(2,1)S(1)} %copy-done.9, bf16[2,2,192,1536]{3,2,1,0:T(8,128)(2,1)S(1)} %copy-done.11, bf16[8,64,8,128]{3,2,1,0:T(8,128)(2,1)S(1)} %bitcast.27, bf16[8,32,16,128]{3,2,1,0:T(8,128)(2,1)S(1)} %bitcast.28), custom_call_target="tpu_custom_call" | custom-call | flops 9663676416 | bytes 1179648 | tf_op jit(solution)/shard_map/beams/pallas_call | solution.py:340
  150.8 0.0 copy-start.12
  150.8 0.0 all-to-all-done.3
  150.8 24.8 %all_to_all.31 = bf16[8,384,128]{2,1,0:T(8,128)(2,1)S(1)} all-to-all(bf16[8,384,128]{2,1,0:T(8,128)(2,1)S(1)} %bitcast.31), channel_id=1, replica_groups=mesh['grp'=8,'tm'=4] {'grp'}, dimensions={0} | all-to-all | bytes 1572864 | tf_op jit(solution)/shard_map/all_to_all | solution.py:448
  175.6 3.5 %all-to-all-start.2 = ((bf16[8,192,128]{2,1,0:T(8,128)(2,1)}), bf16[8,192,128]{2,1,0:T(8,128)(2,1)S(1)}, u32[]{:S(2)}, u32[]{:S(2)}) async-start(bf16[8,192,128]{2,1,0:T(8,128)(2,1)} %bitcast.32), calls=%async_computation.2 | async-start | bytes 786432 | tf_op jit(solution)/shard_map/all_to_all | solution.py:448
  179.1 2.6 %collective-permute-start.4 = (bf16[8,2,24,8,128]{4,3,2,1,0:T(8,128)(2,1)S(1)}, bf16[8,2,24,8,128]{4,3,2,1,0:T(8,128)(2,1)S(1)}, u32[]{:S(2)}, u32[]{:S(2)}) collective-permute-start(bf16[8,2,24,8,128]{4,3,2,1,0:T(8,128)(2,1)S(1)} %bitcast.20), channel_id=1, source_target_pairs={{1,0},{2,1},{3,2},{5,4},{6,5},{7,6},{9,8},{10,9},{11,10},{13,12},{... | collective-permute-start | bytes 2359304 | tf_op jit(solution)/shard_map/ppermute | solution.py:33
  181.7 1.9 collective-permute-start.3
  183.6 6.6 %all-to-all-done.2 = bf16[8,192,128]{2,1,0:T(8,128)(2,1)S(1)} async-done(((bf16[8,192,128]{2,1,0:T(8,128)(2,1)}), bf16[8,192,128]{2,1,0:T(8,128)(2,1)S(1)}, u32[]{:S(2)}, u32[]{:S(2)}) %all-to-all-start.2) | async-done | bytes 393248 | tf_op jit(solution)/shard_map/all_to_all | solution.py:448
  190.2 3.4 %collective-permute-start.2 = (bf16[8,1,24,8,128]{4,3,2,1,0:T(8,128)(2,1)S(1)}, bf16[8,1,24,8,128]{4,3,2,1,0:T(8,128)(2,1)S(1)}, u32[]{:S(2)}, u32[]{:S(2)}) collective-permute-start(bf16[8,1,24,8,128]{4,3,2,1,0:T(8,128)(2,1)S(1)} %bitcast.24), channel_id=1, source_target_pairs={{1,0},{2,1},{3,2},{5,4},{6,5},{7,6},{9,8},{10,9},{11,10},{13,12},{... | collective-permute-start | bytes 1179656 | tf_op jit(solution)/shard_map/ppermute | solution.py:33
  193.6 0.0 collective-permute-done.4.next_ref
  193.6 0.3 broadcast_in_dim.2.moves_ref
  194.0 4.2 %dedisperse.3.refs_0_ = f32[1536,512]{1,0:T(8,128)} custom-call(s32[4,512,128]{2,1,0:T(8,128)S(1)} %broadcast_in_dim.2.moves_ref, bf16[8,2,24,8,128]{4,3,2,1,0:T(8,128)(2,1)S(1)} %bitcast.21, bf16[8,2,24,8,128]{4,3,2,1,0:T(8,128)(2,1)S(1)} %collective-permute-done.4.next_ref), custom_call_target="tpu_custom_call" | custom-call | flops 6291456 | bytes 3932160 | tf_op jit(solution)/shard_map/dedisperse/pallas_call | solution.py:426
  198.2 0.0 collective-permute-done.3.next_ref
  198.2 2.5 %dedisperse.4.refs_0_ = f32[1536,512]{1,0:T(8,128)} custom-call(s32[4,512,128]{2,1,0:T(8,128)S(1)} %broadcast_in_dim.2.moves_ref, bf16[8,1,24,8,128]{4,3,2,1,0:T(8,128)(2,1)S(1)} %bitcast.23, bf16[8,1,24,8,128]{4,3,2,1,0:T(8,128)(2,1)S(1)} %collective-permute-done.3.next_ref, f32[1536,512]{1,0:T(8,128)} %dedisperse.3.refs_0_), custom_call_target="tpu_custom_call", output_to_operand_aliasing={{}: (3, {})} | custom-call | flops 3145728 | bytes 1966080 | tf_op jit(solution)/shard_map/dedisperse/pallas_call | solution.py:426
  200.7 0.1 collective-permute-done.2.next_ref
  200.8 2.5 %dedisperse.5 = f32[1536,512]{1,0:T(8,128)} custom-call(s32[4,512,128]{2,1,0:T(8,128)S(1)} %broadcast_in_dim.2.moves_ref, bf16[8,1,24,8,128]{4,3,2,1,0:T(8,128)(2,1)S(1)} %bitcast.25, bf16[8,1,24,8,128]{4,3,2,1,0:T(8,128)(2,1)S(1)} %collective-permute-done.2.next_ref, f32[1536,512]{1,0:T(8,128)} %dedisperse.4.refs_0_), custom_call_target="tpu_custom_call", output_to_operand_aliasing={{}: (3, {})} | custom-call | flops 3145728 | bytes 1966080 | tf_op jit(solution)/shard_map/dedisperse/pallas_call | solution.py:426
  (12 shorter events, 0.0 us)
Async XLA Ops:
  1.0 9.2 %collective-permute-start = (bf16[2,8,12288]{2,1,0:T(8,128)(2,1)S(1)}, bf16[2,8,12288]{2,1,0:T(8,128)(2,1)S(1)}, u32[]{:S(2)}, u32[]{:S(2)}) collective-permute-start(bf16[2,8,12288]{2,1,0:T(8,128)(2,1)S(1)} %slice.14), channel_id=1, source_target_pairs={{0,1},{1,2},{2,3},{4,5},{5,6},{6,7},{8,9},{9,10},{10,11},{12,13},{... | collective-permute-start | bytes 1179656 | tf_op jit(solution)/shard_map/ppermute | solution.py:33
  10.2 1.0 copy-start
  11.3 0.8 copy-start.4
  12.1 0.8 copy-start.6
  25.5 20.5 %copy-start.1 = (f32[4,2,128,128]{3,2,1,0:T(8,128)S(1)}, f32[4,2,128,128]{3,2,1,0:T(8,128)}, u32[]{:S(2)}) copy-start(f32[4,2,128,128]{3,2,1,0:T(8,128)} %constant.13.clone.coarse_ref) | copy-start | bytes 1572868
  25.5 20.5 %copy-start.5 = (f32[4,4096]{1,0:T(4,128)S(1)}, f32[4,4096]{1,0:T(4,128)}, u32[]{:S(2)}) copy-start(f32[4,4096]{1,0:T(4,128)} %taps_ref.3) | copy-start | bytes 196612
  25.5 20.5 %copy-start.7 = (f32[4,2,8,128]{3,2,1,0:T(8,128)S(1)}, f32[4,2,8,128]{3,2,1,0:T(8,128)}, u32[]{:S(2)}) copy-start(f32[4,2,8,128]{3,2,1,0:T(8,128)} %constant.12.clone.fine_ref) | copy-start | bytes 98308
  25.5 42.7 %all-to-all-start = ((bf16[8,512,128]{2,1,0:T(8,128)(2,1)}), bf16[8,512,128]{2,1,0:T(8,128)(2,1)S(1)}, u32[]{:S(2)}, u32[]{:S(2)}) async-start(bf16[8,512,128]{2,1,0:T(8,128)(2,1)} %bitcast.4), calls=%async_computation | async-start | bytes 2097152 | tf_op jit(solution)/shard_map/all_to_all | solution.py:448
  32.4 13.6 %collective-permute-start.1 = (bf16[2,16,12288]{2,1,0:T(8,128)(2,1)S(1)}, bf16[2,16,12288]{2,1,0:T(8,128)(2,1)S(1)}, u32[]{:S(2)}, u32[]{:S(2)}) collective-permute-start(bf16[2,16,12288]{2,1,0:T(8,128)(2,1)S(1)} %slice.15), channel_id=1, source_target_pairs={{0,1},{1,2},{2,3},{4,5},{5,6},{6,7},{8,9},{9,10},{10,11},{12,13},{... | collective-permute-start | bytes 2359304 | tf_op jit(solution)/shard_map/ppermute | solution.py:33
  67.2 1.0 copy-start.2
  91.1 37.3 %all-to-all-start.4 = ((bf16[8,512,128]{2,1,0:T(8,128)(2,1)}), bf16[8,512,128]{2,1,0:T(8,128)(2,1)S(1)}, u32[]{:S(2)}, u32[]{:S(2)}) async-start(bf16[8,512,128]{2,1,0:T(8,128)(2,1)} %bitcast.12), calls=%async_computation.4 | async-start | bytes 2097152 | tf_op jit(solution)/shard_map/all_to_all | solution.py:448
  110.2 1.4 copy-start.10
  124.0 0.7 copy-start.3
  124.8 3.7 %copy-start.8 = (bf16[8,2,192,1536]{3,2,1,0:T(8,128)(2,1)}, bf16[8,2,192,1536]{3,2,1,0:T(8,128)(2,1)S(1)}, u32[]{:S(2)}) copy-start(bf16[8,2,192,1536]{3,2,1,0:T(8,128)(2,1)S(1)} %get-tuple-element.12.step_ref) | copy-start | bytes 28311556
  128.4 22.4 %all-to-all-start.3 = ((bf16[8,192,128]{2,1,0:T(8,128)(2,1)}), bf16[8,192,128]{2,1,0:T(8,128)(2,1)S(1)}, u32[]{:S(2)}, u32[]{:S(2)}) async-start(bf16[8,192,128]{2,1,0:T(8,128)(2,1)} %bitcast.10), calls=%async_computation.3 | async-start | bytes 786432 | tf_op jit(solution)/shard_map/all_to_all | solution.py:448
  133.8 3.7 %copy-start.9 = (bf16[8,2,192,1536]{3,2,1,0:T(8,128)(2,1)S(1)}, bf16[8,2,192,1536]{3,2,1,0:T(8,128)(2,1)}, u32[]{:S(2)}) copy-start(bf16[8,2,192,1536]{3,2,1,0:T(8,128)(2,1)} %copy-done.8) | copy-start | bytes 28311556
  137.5 1.7 copy-start.11
  150.8 42.8 %copy-start.12 = (s32[4,512]{1,0:T(4,128)S(1)}, s32[4,512]{1,0:T(4,128)}, u32[]{:S(2)}) copy-start(s32[4,512]{1,0:T(4,128)} %param.11) | copy-start | bytes 24580
  175.6 14.6 %all-to-all-start.2 = ((bf16[8,192,128]{2,1,0:T(8,128)(2,1)}), bf16[8,192,128]{2,1,0:T(8,128)(2,1)S(1)}, u32[]{:S(2)}, u32[]{:S(2)}) async-start(bf16[8,192,128]{2,1,0:T(8,128)(2,1)} %bitcast.32), calls=%async_computation.2 | async-start | bytes 786432 | tf_op jit(solution)/shard_map/all_to_all | solution.py:448
  179.1 14.5 %collective-permute-start.4 = (bf16[8,2,24,8,128]{4,3,2,1,0:T(8,128)(2,1)S(1)}, bf16[8,2,24,8,128]{4,3,2,1,0:T(8,128)(2,1)S(1)}, u32[]{:S(2)}, u32[]{:S(2)}) collective-permute-start(bf16[8,2,24,8,128]{4,3,2,1,0:T(8,128)(2,1)S(1)} %bitcast.20), channel_id=1, source_target_pairs={{1,0},{2,1},{3,2},{5,4},{6,5},{7,6},{9,8},{10,9},{11,10},{13,12},{... | collective-permute-start | bytes 2359304 | tf_op jit(solution)/shard_map/ppermute | solution.py:33
  181.7 16.5 %collective-permute-start.3 = (bf16[8,1,24,8,128]{4,3,2,1,0:T(8,128)(2,1)S(1)}, bf16[8,1,24,8,128]{4,3,2,1,0:T(8,128)(2,1)S(1)}, u32[]{:S(2)}, u32[]{:S(2)}) collective-permute-start(bf16[8,1,24,8,128]{4,3,2,1,0:T(8,128)(2,1)S(1)} %bitcast.22), channel_id=1, source_target_pairs={{1,0},{2,1},{3,2},{5,4},{6,5},{7,6},{9,8},{10,9},{11,10},{13,12},{... | collective-permute-start | bytes 1179656 | tf_op jit(solution)/shard_map/ppermute | solution.py:33
  190.2 10.6 %collective-permute-start.2 = (bf16[8,1,24,8,128]{4,3,2,1,0:T(8,128)(2,1)S(1)}, bf16[8,1,24,8,128]{4,3,2,1,0:T(8,128)(2,1)S(1)}, u32[]{:S(2)}, u32[]{:S(2)}) collective-permute-start(bf16[8,1,24,8,128]{4,3,2,1,0:T(8,128)(2,1)S(1)} %bitcast.24), channel_id=1, source_target_pairs={{1,0},{2,1},{3,2},{5,4},{6,5},{7,6},{9,8},{10,9},{11,10},{13,12},{... | collective-permute-start | bytes 1179656 | tf_op jit(solution)/shard_map/ppermute | solution.py:33
